TPU v7x, 32 devices: a whole 2x2x4 slice. The times are simulated.
32 devices in a mesh: layer: 2 (over x), row: 4 (over z), col: 4 (over y, core).
Axes of the slice: x: 2, y: 2, z: 4, core: 2. Of those that a mesh axis runs over, the one named last changes fastest.
Arguments:
- covariance: float32 [16384, 8192], P(('layer', 'row'), 'col'), parts along dimension 0, may hold values from -2 to 20, as said below
- weight: bfloat16 [16384, 2, 1024], P(('layer', 'col', 'row')), parts along dimension 0, may hold values from -6 to 6
- factor_a: bfloat16 [16384, 2, 256], P(('layer', 'col', 'row')), parts along dimension 0, may hold values from -1.5 to 1.5
- factor_b: bfloat16 [4, 256, 1024], P('layer', ('row', 'col')), parts along dimension 0, may hold values from -1.5 to 1.5
Outputs:
- new_a: float32 [16384, 2, 256], P(('layer', 'col', 'row')), parts along dimension 0
- new_b: float32 [4, 256, 1024], P('layer', ('row', 'col')), parts along dimension 0
There are 2 independent parts, one for each index of `layer`. A program takes and returns all parts, laid end to end along the dimension named above; each array names one. Nothing has to cross between parts.
Inputs may be any that keep to these rules, and one draw needn't show every extreme that they name: covariance is symmetric and positive definite.
All inputs are finite; a program needn't handle non-finite values.
Results may differ from a plain program's by a relative error of at most 0.0012.
Values may be sent and summed in bfloat16 or wider, within the bound.
No kernel may reach another device: no remote copies, remote signals or barrier semaphores. Data moves between devices by JAX's collectives and lax.ppermute only.
A program may use at most 64 MiB of HBM per device.

v0:
```python
import jax
import jax.numpy as jnp
from jax import lax
from jax.sharding import PartitionSpec as P

D = 8192
O = 1024
R = 256


def reorder_slots(spread):
    side = lax.axis_size("row")
    total = side * side
    return spread.reshape(side, side, -1).transpose(1, 0, 2).reshape(total, -1)


def transpose_full(values):
    side = lax.axis_size("row")
    flat = values.reshape(side * side, -1)
    spread = lax.all_to_all(flat, ("row", "col"), split_axis=0, concat_axis=0, tiled=True)
    landed = lax.all_to_all(
        reorder_slots(spread), ("row", "col"), split_axis=0, concat_axis=0, tiled=True
    )
    return landed.reshape(values.shape)


def per_device(covariance, weight, factor_a, factor_b):
    highest = lax.Precision.HIGHEST
    row_count = weight.shape[0]
    full_b = lax.all_gather(factor_b, ("row", "col"), axis=1, tiled=True)
    right_f = full_b.astype(jnp.float32)
    diff_one = (
        weight.astype(jnp.float32)
        - jnp.einsum("nkr,kro->nko", factor_a, full_b, preferred_element_type=jnp.float32)
    ).astype(jnp.bfloat16)
    panels = lax.all_gather(
        jnp.einsum("nko,kro->nkr", diff_one, full_b, preferred_element_type=jnp.float32),
        "row",
        axis=0,
        tiled=True,
    )
    panel_flat = panels.reshape(panels.shape[0], -1)
    cov_rows = covariance
    grad_one = lax.psum_scatter(
        jnp.dot(cov_rows, panel_flat, precision=highest, preferred_element_type=jnp.float32),
        "col",
        scatter_dimension=0,
        tiled=True,
    )
    grad_one = transpose_full(grad_one)
    new_a = factor_a.astype(jnp.float32) + 4.0 / O * grad_one.reshape(row_count, 2, R)
    diff_two = (
        weight.astype(jnp.float32) - jnp.einsum("nkr,kro->nko", new_a, right_f, precision=highest)
    ).astype(jnp.bfloat16)
    a_panel = lax.all_gather(new_a.reshape(row_count, 2 * R), "row", axis=0, tiled=True)
    cov_rows = covariance
    field = lax.psum_scatter(
        jnp.dot(cov_rows, a_panel, precision=highest, preferred_element_type=jnp.float32),
        "col",
        scatter_dimension=0,
        tiled=True,
    )
    field = transpose_full(field)
    partial_value = jnp.einsum(
        "nkr,nko->kro",
        field.reshape(row_count, 2, R),
        diff_two.astype(jnp.float32),
        precision=highest,
    )
    summed = lax.psum(partial_value, ("row", "col"))
    share_rows = factor_b.shape[1]
    linear_id = lax.axis_index("row") * lax.axis_size("col") + lax.axis_index("col")
    own_share = lax.dynamic_slice_in_dim(summed, linear_id * share_rows, share_rows, 1)
    new_b = factor_b.astype(jnp.float32) + 8.0 / D * own_share
    return (new_a, new_b)


def solution(mesh):
    in_specs = (
        P(("layer", "row"), "col"),
        P(("layer", "col", "row"), None, None),
        P(("layer", "col", "row"), None, None),
        P("layer", ("row", "col"), None),
    )
    out_specs = (P(("layer", "col", "row"), None, None), P("layer", ("row", "col"), None))
    return jax.shard_map(
        per_device, mesh=mesh, in_specs=in_specs, out_specs=out_specs, check_vma=False
    )
```

profile of v0, /device:TPU:0, one launch (start us, length us, event | category | flops | bytes accessed | tf_op | source)
XLA Modules:
  0.0 675.6 jit_solution(4953905984134823521)
XLA Ops:
  8.0 4.7 copy.27
  12.7 38.1 %all-gather.4.cloned.1.call-done = bf16[2,256,1024]{2,1,0:T(8,128)(2,1)} async-done(((bf16[2,16,1024]{2,1,0:T(8,128)(2,1)}), bf16[2,256,1024]{2,1,0:T(8,128)(2,1)}) %all-gather.4.cloned.1.call-update) | async-done | bytes 1048592 | tf_op jit(solution)/shard_map/all_gather | solution.py:30
  50.8 4.3 fusion.3
  55.2 79.8 %all-gather.6.cloned.1.call-done = f32[2048,2,256]{2,0,1:T(8,128)} async-done(((f32[512,2,256]{2,0,1:T(8,128)}), f32[2048,2,256]{2,0,1:T(8,128)}) %all-gather.6.cloned.1.call-update) | async-done | bytes 4194320 | tf_op jit(solution)/shard_map/all_gather | solution.py:36
  135.0 5.4 copy.30
  140.4 32.4 %convolution_bitcast_fusion.1 = f32[2048,512]{0,1:T(8,128)} fusion(f32[2048,512]{0,1:T(8,128)} %bitcast.35, f32[2048,2048]{1,0:T(8,128)} %param.4), kind=kOutput, calls=%fused_computation.5 | convolution fusion | flops 25769803776 | bytes 25165824 | tf_op jit(solution)/shard_map/dot_general | solution.py:45
  172.8 43.0 %reduce-scatter.3.cloned.1.call-done = f32[512,512]{0,1:T(8,128)} async-done(((f32[2048,512]{0,1:T(8,128)}), f32[512,512]{0,1:T(8,128)}) %reduce-scatter.3.cloned.1.call-update) | async-done | bytes 1048592 | tf_op jit(solution)/shard_map/reduce_scatter | solution.py:44
  217.4 2.2 all_to_all.32
  219.6 29.6 %all_to_all.40 = f32[16,1,16384]{2,1,0:T(1,128)S(1)} all-to-all(f32[16,1,16384]{2,1,0:T(1,128)} %all_to_all.32), channel_id=1, replica_groups=mesh['layer'=2,'row'=4,'col'=4] {'row','col'}, dimensions={0} | all-to-all | bytes 2097152 | tf_op jit(solution)/shard_map/all_to_all | solution.py:20
  249.2 3.7 reduce
  254.5 1.6 copy.33
  256.2 2.6 all_to_all.33
  258.8 29.5 %all_to_all.41 = f32[16,1,16384]{2,1,0:T(1,128)S(1)} all-to-all(f32[16,1,16384]{2,1,0:T(1,128)S(1)} %all_to_all.33), channel_id=1, replica_groups=mesh['layer'=2,'row'=4,'col'=4] {'row','col'}, dimensions={0} | all-to-all | bytes 2097152 | tf_op jit(solution)/shard_map/all_to_all | solution.py:21
  288.3 3.0 multiply_reduce_fusion
  291.3 1.9 mul.23
  295.8 81.2 %all-gather.8.cloned.1.call-done = f32[2048,512]{1,0:T(8,128)} async-done(((f32[512,512]{1,0:T(8,128)}), f32[2048,512]{1,0:T(8,128)}) %all-gather.8.cloned.1.call-update) | async-done | bytes 4194320 | tf_op jit(solution)/shard_map/all_gather | solution.py:55
  377.0 57.8 %convolution_bitcast_fusion = f32[2048,512]{0,1:T(8,128)} fusion(f32[2048,512]{1,0:T(8,128)} %all-gather.8.cloned.1.call-done, f32[2048,2048]{1,0:T(8,128)} %param.4), kind=kOutput, calls=%fused_computation.4 | convolution fusion | flops 25769803776 | bytes 25165824 | tf_op jit(solution)/shard_map/dot_general | solution.py:58
  434.8 43.1 %reduce-scatter.5.cloned.1.call-done = f32[512,512]{0,1:T(8,128)} async-done(((f32[2048,512]{0,1:T(8,128)}), f32[512,512]{0,1:T(8,128)}) %reduce-scatter.5.cloned.1.call-update) | async-done | bytes 1048592 | tf_op jit(solution)/shard_map/reduce_scatter | solution.py:57
  477.9 2.6 copy.35
  480.5 3.4 all_to_all.34
  483.9 29.5 %all_to_all.42 = f32[16,1,16384]{2,1,0:T(1,128)} all-to-all(f32[16,1,16384]{2,1,0:T(1,128)} %all_to_all.34), channel_id=1, replica_groups=mesh['layer'=2,'row'=4,'col'=4] {'row','col'}, dimensions={0} | all-to-all | bytes 2097152 | tf_op jit(solution)/shard_map/all_to_all | solution.py:20
  513.4 4.7 reduce.2
  518.1 2.5 reshape.41
  520.7 2.9 copy.57
  523.6 3.3 all_to_all.35
  526.9 5.1 all-to-all-start.3
  532.2 4.5 fusion.1
  536.8 18.1 %all-to-all-done.3 = f32[16,1,16384]{2,1,0:T(1,128)} async-done(((f32[16,1,16384]{2,1,0:T(1,128)}), f32[16,1,16384]{2,1,0:T(1,128)}, u32[]{:S(2)}, u32[]{:S(2)}) %all-to-all-start.3) | async-done | bytes 1048608 | tf_op jit(solution)/shard_map/all_to_all | solution.py:21
  554.9 4.7 reduce.3
  559.7 2.1 reshape_reshape.4
  561.8 4.8 fusion.4
  566.6 100.3 %all-reduce.2.cloned.1.call-done = f32[2,256,1024]{2,1,0:T(8,128)} async-done(((f32[2,256,1024]{2,1,0:T(8,128)}), f32[2,256,1024]{2,1,0:T(8,128)}) %all-reduce.2.cloned.1.call-update) | async-done | bytes 2097168 | tf_op jit(solution)/shard_map/psum | solution.py:70
  (25 shorter events, 8.5 us)
Async XLA Ops:
  7.2 43.6 %copy-start.2 = (bf16[512,2,256]{2,1,0:T(2,128)(2,1)S(1)}, bf16[512,2,256]{2,1,0:T(2,128)(2,1)}, u32[]{:S(2)}) copy-start(bf16[512,2,256]{2,1,0:T(2,128)(2,1)} %param.6) | copy-start | bytes 1572868
  7.2 43.6 %all-gather.4.cloned.1.call-start = ((), (), s32[]{:S(2)}) async-start(), calls=%async_computation.6 | async-start | bytes 1114112 | tf_op jit(solution)/shard_map/all_gather | solution.py:30
  7.9 127.1 %all-gather.6.cloned.1.call-start = ((), (), s32[]{:S(2)}) async-start(), calls=%async_computation.7 | async-start | bytes 5242880 | tf_op jit(solution)/shard_map/all_gather | solution.py:36
  55.2 160.7 %reduce-scatter.3.cloned.1.call-start = ((), (), s32[]{:S(2)}) async-start(), calls=%async_computation.8 | async-start | bytes 5242880 | tf_op jit(solution)/shard_map/reduce_scatter | solution.py:44
  172.8 204.2 %all-gather.8.cloned.1.call-start = ((), (), s32[]{:S(2)}) async-start(), calls=%async_computation.9 | async-start | bytes 5242880 | tf_op jit(solution)/shard_map/all_gather | solution.py:55
  294.6 237.6 %copy-start = (f32[128,8,256]{2,1,0:T(8,128)}, f32[128,8,256]{2,1,0:T(8,128)S(1)}, u32[]{:S(2)}) copy-start(f32[128,8,256]{2,1,0:T(8,128)S(1)} %convert_add_fusion) | copy-start | bytes 3145732
  295.8 182.1 %reduce-scatter.5.cloned.1.call-start = ((), (), s32[]{:S(2)}) async-start(), calls=%async_computation.10 | async-start | bytes 5242880 | tf_op jit(solution)/shard_map/reduce_scatter | solution.py:57
  526.9 28.0 %all-to-all-start.3 = ((f32[16,1,16384]{2,1,0:T(1,128)}), f32[16,1,16384]{2,1,0:T(1,128)}, u32[]{:S(2)}, u32[]{:S(2)}) async-start(f32[16,1,16384]{2,1,0:T(1,128)} %all_to_all.35), calls=%async_computation.5 | async-start | bytes 2097152 | tf_op jit(solution)/shard_map/all_to_all | solution.py:21
  532.0 134.9 %all-reduce.2.cloned.1.call-start = ((), (), s32[]{:S(2)}) async-start(), calls=%async_computation.11 | async-start | bytes 4194304 | tf_op jit(solution)/shard_map/psum | solution.py:70
  536.8 25.0 %copy-start.1 = (bf16[512,2,1024]{0,2,1:T(8,128)(2,1)S(1)}, bf16[512,2,1024]{0,2,1:T(8,128)(2,1)}, u32[]{:S(2)}) copy-start(bf16[512,2,1024]{0,2,1:T(8,128)(2,1)} %fusion.1) | copy-start | bytes 6291460
  561.8 105.1 %copy-start.3 = (bf16[2,16,1024]{2,1,0:T(8,128)(2,1)S(1)}, bf16[2,16,1024]{2,1,0:T(8,128)(2,1)}, u32[]{:S(2)}) copy-start(bf16[2,16,1024]{2,1,0:T(8,128)(2,1)} %param.7) | copy-start | bytes 196612
Sparse Core Ops, SparseCore 0:
  10.2 40.5 all-gather.3
  55.3 79.7 all-gather.5
  172.9 42.9 reduce-scatter.2
  295.9 81.0 all-gather.7
  435.0 42.9 reduce-scatter.4
  566.7 100.1 all-reduce.1
where the time goes:
time: 683 us; the launch traced here: 676 us
  waiting for transfers between devices  404 us (59%)
  matrix products  104 us (15%)
  blocking collectives  88.6 us (13%)
  local copies, waits for them, and re-layouts  39.6 us (6%)
  other arithmetic  19.2 us (3%)
  between operations  14.4 us (2%)
    psum x1, waiting for transfers between devices, per_device(): summed = lax.psum(partial_value, ('row', 'col'))  100 us
    all_gather x1, waiting for transfers between devices, per_device(): lax.all_gather(new_a.reshape(row_count, 2 * R), 'row', axis=0, tiled=True)  81.2 us
    all_gather x1, waiting for transfers between devices, per_device(): lax.all_gather(jnp.einsum('nko,kro->nkr', diff_one, full_b, preferred_ele...  79.8 us
    all_to_all x2, blocking collectives, transpose_full(): lax.all_to_all(flat, ('row', 'col'), split_axis=0, concat_axis=0, tiled=T...  59.1 us
    dot_general x1, matrix products, per_device(): jnp.dot(cov_rows, a_panel, precision=highest, preferred_element_type=jnp....  57.8 us
    reduce_scatter x1, waiting for transfers between devices, per_device(): lax.psum_scatter(jnp.dot(cov_rows, a_panel, precision=highest, preferred_...  43.1 us
    reduce_scatter x1, waiting for transfers between devices, per_device(): lax.psum_scatter(jnp.dot(cov_rows, panel_flat, precision=highest, preferr...  43 us
    all_gather x1, waiting for transfers between devices, per_device(): full_b = lax.all_gather(factor_b, ('row', 'col'), axis=1, tiled=True)  38.1 us
  transfers between devices with their start and end apart: 7, of which 7 were waited for; matrix products, arithmetic and copies ran while one was open for 1% of the time, Pallas kernels for 0%

commit v1 on v0

v1 whole, which is shorter than its diff:
```python
import jax
import jax.numpy as jnp
from jax import lax
from jax.experimental import pallas as pl
from jax.experimental.pallas import tpu as pltpu
from jax.sharding import PartitionSpec as P


CORES = 2
F32, BF16 = jnp.float32, jnp.bfloat16
VMEM_LIMIT = 12 * 2**20

SCALE_P = 2.0**-2
SCALE_G = 2.0**-7
SCALE_A = 2.0**-4
SCALE_F = 2.0**-12
SCALE_V = 2.0**-16


def encode(x, scale):
    u = x * scale
    return (u * jnp.abs(u) * (u * u)).astype(BF16)


def decode(code, scale):
    v = code.astype(F32)
    root = lax.rsqrt(lax.rsqrt(jnp.abs(v))) * (1.0 / scale)
    return jnp.where(v < 0, -root, root)


def halves(x):
    high = x.astype(BF16)
    return high, (x - high.astype(F32)).astype(BF16)


def mm(a, b):
    return jnp.dot(a, b, preferred_element_type=F32)


class Queue:
    def __init__(self, meta):
        self.meta = meta

    def call(self, body, grid, ins, outs, shapes, args, scratch=(), alias=None, flops=0, limit=VMEM_LIMIT):
        moved = sum(a.size * a.dtype.itemsize for a in args)
        moved += sum(s.size * s.dtype.itemsize for s in shapes)
        spec = pltpu.PrefetchScalarGridSpec(
            num_scalar_prefetch=1,
            grid=grid,
            in_specs=ins,
            out_specs=outs,
            scratch_shapes=list(scratch),
        )
        got = pl.pallas_call(
            body,
            out_shape=shapes,
            grid_spec=spec,
            input_output_aliases=alias or {},
            cost_estimate=pl.CostEstimate(flops=flops, bytes_accessed=moved, transcendentals=0),
            compiler_params=pltpu.CompilerParams(
                dimension_semantics=("arbitrary",) * len(grid), vmem_limit_bytes=limit
            ),
        )(self.meta, *args)
        self.meta, *got = lax.optimization_barrier((self.meta, *got))
        return got[0] if len(got) == 1 else got


def shape(dims, dtype):
    return jax.ShapeDtypeStruct(dims, dtype)


def split_cov(queue, cov):
    rows, cols = cov.shape
    tile = min(rows, 256)

    def body(m, c, hi, lo):
        hi[...], lo[...] = halves(c[...])

    spec = pl.BlockSpec((tile, cols), lambda i, m: (i, 0))
    return queue.call(
        body, (rows // tile,), [spec], [spec, spec], [shape(cov.shape, BF16)] * 2, [cov],
        limit=3 * VMEM_LIMIT,
    )


def place_b(queue, own, other, from_row, from_y, core_at):
    ys, side, projections, share, features = own.shape
    rank = ys * side * CORES * share

    def body(m, own, other, out):
        s = pl.program_id(0)
        for t in range(ys):
            place = (m[from_row + s] * ys + m[from_y + t]) * CORES
            for ref, core in ((own, m[core_at]), (other, 1 - m[core_at])):
                at = pl.ds(pl.multiple_of((place + core) * share, share), share)
                for k in range(projections):
                    out[k, at, :] = ref[t, 0, k]

    spec = pl.BlockSpec((ys, 1, projections, share, features), lambda s, m: (0, s, 0, 0, 0))
    return queue.call(
        body,
        (side,),
        [spec, spec],
        [pl.BlockSpec((projections, rank, features), lambda s, m: (0, 0, 0))],
        [shape((projections, rank, features), BF16)],
        [own, other],
    )


def project(queue, w, a, b, k):
    rank, features = b.shape[1:]
    n = w.shape[0]
    tile = min(n, 256)

    def body(m, w, a, b, code):
        diff = (w[...].astype(F32) - mm(a[...], b[0])).astype(BF16)
        proj = lax.dot_general(diff, b[0], (((1,), (1,)), ((), ())), preferred_element_type=F32)
        code[...] = encode(proj, SCALE_P)

    return queue.call(
        body,
        (n // tile,),
        [
            pl.BlockSpec((tile, features), lambda i, m: (i, k)),
            pl.BlockSpec((tile, rank), lambda i, m: (i, k)),
            pl.BlockSpec((1, rank, features), lambda i, m: (k, 0, 0)),
        ],
        [pl.BlockSpec((tile, rank), lambda i, m: (i, 0))],
        [shape((n, rank), BF16)],
        [w, a, b],
        flops=4 * n * rank * features,
    )


def product_one(queue, cov, blocks, acc, row_of, count, add=None, coded=False):
    hi, lo = cov
    n, width = blocks[0][0].shape
    whole = count * n == hi.shape[0]
    terms = len(blocks)
    tall = n
    if whole and count % 2 == 0:
        tall, count = 2 * n, count // 2

    def body(m, *refs):
        refs = list(refs)
        his, los, codes = refs[:terms], refs[terms : 2 * terms], refs[2 * terms : 3 * terms]
        refs = refs[3 * terms :]
        acc_ref = refs.pop(0) if acc is not None else None
        add_ref = refs.pop(0) if add is not None else None
        out, p_hi, p_lo = refs

        @pl.when(pl.program_id(0) == 0)
        def _():
            for t in range(terms):
                p_hi[t], p_lo[t] = halves(decode(codes[t][...], SCALE_P))

        got = None
        for t in range(terms):
            c = his[t][...]
            part = mm(c, p_hi[t]) + mm(c, p_lo[t]) + mm(los[t][...], p_hi[t])
            got = part if got is None else got + part
        if acc is not None:
            got = got + acc_ref[...]
        if add is not None:
            got = got + add_ref[...]
        out[...] = encode(got, SCALE_G) if coded else got

    specs = [
        pl.BlockSpec((tall, n), lambda i, m, at=at: (row_of(i, m), m[at])) for _, at in blocks
    ]
    ins = specs + specs + [pl.BlockSpec((n, width), lambda i, m: (0, 0))] * terms
    args = [hi] * terms + [lo] * terms + [code for code, _ in blocks]
    alias = None
    if acc is not None:
        if whole:
            alias = {1 + len(args): 0}
        ins.append(pl.BlockSpec((tall, width), lambda i, m: (row_of(i, m), 0)))
        args.append(acc)
    if add is not None:
        ins.append(pl.BlockSpec((tall, width), lambda i, m: (i, 0)))
        args.append(add)
    return queue.call(
        body,
        (count,),
        ins,
        [pl.BlockSpec((tall, width), lambda i, m: (i, 0))],
        [shape((count * tall, width), BF16 if coded else F32)],
        args,
        scratch=[pltpu.VMEM((terms, n, width), BF16)] * 2,
        alias=alias,
        flops=6 * terms * count * tall * n * width,
    )


def finish_grad(queue, part, codes, mirrored_a, k, step):
    n, width = part.shape
    tile = min(n, 128)
    count = len(codes)

    def body(m, part, a, *rest):
        grad = part[...]
        for ref in rest[:count]:
            grad = grad + decode(ref[...], SCALE_G)
        grad_code, a_code = rest[count:]
        grad_code[...] = encode(grad, SCALE_G)
        a_new = a[...].astype(F32) + step * grad
        a_code[...] = encode(a_new.T, SCALE_A)

    spec = pl.BlockSpec((tile, width), lambda i, m: (i, 0))
    return queue.call(
        body,
        (n // tile,),
        [spec, pl.BlockSpec((tile, width), lambda i, m: (i, k))] + [spec] * count,
        [spec, pl.BlockSpec((width, tile), lambda i, m: (0, i))],
        [shape((n, width), BF16), shape((width, n), BF16)],
        [part, mirrored_a, *codes],
    )


def product_two(queue, cov, blocks, acc, col_of, count, coded=False):
    hi, lo = cov
    width, n = blocks[0][0].shape
    whole = count * n == hi.shape[1]
    terms = len(blocks)

    def body(m, *refs):
        refs = list(refs)
        his, los, codes = refs[:terms], refs[terms : 2 * terms], refs[2 * terms : 3 * terms]
        refs = refs[3 * terms :]
        acc_ref = refs.pop(0) if acc is not None else None
        out, parts = refs

        @pl.when(pl.program_id(0) == 0)
        def _():
            for t in range(terms):
                parts[t, :width], parts[t, width:] = halves(decode(codes[t][...], SCALE_A))

        got = None
        for t in range(terms):
            c = his[t][...]
            both = mm(parts[t], c)
            part = both[:width] + both[width:] + mm(parts[t, :width], los[t][...])
            got = part if got is None else got + part
        if acc is not None:
            got = got + acc_ref[...]
        out[...] = encode(got, SCALE_F) if coded else got

    specs = [
        pl.BlockSpec((n, n), lambda i, m, row=row: (row(m), col_of(i, m))) for _, row in blocks
    ]
    ins = specs + specs + [pl.BlockSpec((width, n), lambda i, m: (0, 0))] * terms
    args = [hi] * terms + [lo] * terms + [code for code, _ in blocks]
    alias = None
    if acc is not None:
        if whole:
            alias = {1 + len(args): 0}
        ins.append(pl.BlockSpec((width, n), lambda i, m: (0, col_of(i, m))))
        args.append(acc)
    return queue.call(
        body,
        (count,),
        ins,
        [pl.BlockSpec((width, n), lambda i, m: (0, i))],
        [shape((width, count * n), BF16 if coded else F32)],
        args,
        scratch=[pltpu.VMEM((terms, 2 * width, n), BF16)],
        alias=alias,
        flops=6 * terms * count * n * n * width,
    )


def second_diff(queue, grad_code, w, a, b, k, step):
    n, rank = grad_code.shape
    features = b.shape[2]
    tile = min(n, 256)

    def body(m, grad_code, w, a, b, new_a, diff):
        a_new = a[...].astype(F32) + step * decode(grad_code[...], SCALE_G)
        new_a[...] = a_new
        high, low = halves(a_new)
        value = mm(high, b[0]) + mm(low, b[0])
        diff[...] = (w[...].astype(F32) - value).astype(BF16)

    narrow = pl.BlockSpec((tile, rank), lambda i, m: (i, 0))
    return queue.call(
        body,
        (n // tile,),
        [
            narrow,
            pl.BlockSpec((tile, features), lambda i, m: (i, k)),
            pl.BlockSpec((tile, rank), lambda i, m: (i, k)),
            pl.BlockSpec((1, rank, features), lambda i, m: (k, 0, 0)),
        ],
        [narrow, pl.BlockSpec((tile, features), lambda i, m: (i, 0))],
        [shape((n, rank), F32), shape((n, features), BF16)],
        [grad_code, w, a, b],
        flops=4 * n * rank * features,
    )


def second_grad(queue, own, codes, diff):
    rank, n = own.shape
    features = diff.shape[1]
    count = len(codes)
    tile = min(features, 512)

    def body(m, own, diff, *rest):
        out, f_hi, f_lo = rest[count:]

        @pl.when(pl.program_id(0) == 0)
        def _():
            field = own[...]
            for ref in rest[:count]:
                field = field + decode(ref[...], SCALE_F)
            f_hi[...], f_lo[...] = halves(field)

        out[...] = mm(f_hi[...], diff[...]) + mm(f_lo[...], diff[...])

    spec = pl.BlockSpec((rank, n), lambda i, m: (0, 0))
    return queue.call(
        body,
        (features // tile,),
        [spec, pl.BlockSpec((n, tile), lambda i, m: (0, i))] + [spec] * count,
        [pl.BlockSpec((rank, tile), lambda i, m: (0, i))],
        [shape((rank, features), F32)],
        [own, diff, *codes],
        scratch=[pltpu.VMEM((rank, n), BF16)] * 2,
        flops=4 * n * rank * features,
    )


def per_device(covariance, weight, factor_a, factor_b):
    side = lax.axis_size("row")
    ys = lax.axis_size("col") // CORES
    row = lax.axis_index("row")
    col = lax.axis_index("col")
    y, core = col // CORES, col % CORES
    n, projections, features = weight.shape
    rank = factor_a.shape[2]
    width = projections * rank
    share = factor_b.shape[1]
    step_a = 4.0 / features
    step_b = 8.0 / (n * side * side)

    def swap_core(x):
        return lax.ppermute(x, "col", [(i, i ^ 1) for i in range(ys * CORES)])

    def shift_y(x, s):
        pairs = [(i, (i // CORES + s) % ys * CORES + i % CORES) for i in range(ys * CORES)]
        return lax.ppermute(x, "col", pairs)

    def shift_row(x, s):
        return lax.ppermute(x, "row", [(i, (i + s) % side) for i in range(side)])

    def mirror(x):
        pairs = [(i * side + j, j * side + i) for i in range(side) for j in range(side)]
        return lax.ppermute(x, ("row", "col"), pairs)

    def pick(x, i, axis=0):
        return lax.dynamic_index_in_dim(x, i, axis, keepdims=False)

    hops, lanes = jnp.arange(side), jnp.arange(ys)
    meta = jnp.concatenate(
        [(row - hops) % side, (row + hops) % side, (y - lanes) % ys, (y + lanes) % ys, core[None]]
    ).astype(jnp.int32)
    from_row, to_row = 0, side
    from_y, to_y = 2 * side, 2 * side + ys
    core_at = 2 * side + 2 * ys
    here = [core, 1 - core, y, row]
    here += [(y + t) % ys for t in range(1, ys)] + [(row + t) % side for t in range(1, side)]
    here = [i.astype(jnp.uint32) for i in here]
    a = factor_a.reshape(n, width)
    w = weight.reshape(n, projections * features)
    meta, a, w, *here = lax.optimization_barrier((meta, a, w, *here))
    own_core, other_core, own_y, own_row = here[:4]
    next_y, next_row = here[3 : 3 + ys], here[2 + ys :]
    queue = Queue(meta)

    z = jnp.stack([factor_b] + [shift_row(factor_b, s) for s in range(1, side)])
    mirrored_a = mirror(factor_a)
    zy = jnp.stack([z] + [shift_y(z, s) for s in range(1, ys)])
    cov = split_cov(queue, covariance)
    cov = [pltpu.with_memory_space_constraint(x, pltpu.VMEM) for x in cov]
    zyc = swap_core(zy)
    if share % 16 == 0:
        b = place_b(queue, zy, zyc, from_row, from_y, core_at)
    else:
        both = jnp.where(core == 0, jnp.stack([zy, zyc]), jnp.stack([zyc, zy]))
        both = jnp.take(both, (y - lanes) % ys, axis=1)
        both = jnp.take(both, (row - hops) % side, axis=2)
        b = both.transpose(3, 2, 1, 0, 4, 5).reshape(projections, rank, features)

    ks = range(projections)
    panels = []
    for k in ks:
        code = project(queue, w, a, b, k)
        panels.append([code] + [shift_row(code, s) for s in range(1, side)])
    mirrored_a = mirrored_a.reshape(n, width)
    late = 2

    def early_one(k, acc, s):
        return product_one(queue, cov, [(panels[k][s], from_row + s)], acc, lambda i, m: i, side)

    def pieces_one(k, acc):
        blocks = [(panels[k][s], from_row + s) for s in range(side - late, side)]

        def piece(row_of, count, add=None, coded=False):
            return product_one(queue, cov, blocks, acc, row_of, count, add, coded)

        far_other = piece(lambda i, m: m[to_y + 1 + i] * CORES + 1 - m[core_at], ys - 1)
        far_add = swap_core(far_other)
        near_other = piece(lambda i, m: m[to_y] * CORES + 1 - m[core_at], 1)
        near_add = swap_core(near_other)
        far_code = piece(
            lambda i, m: m[to_y + 1 + i] * CORES + m[core_at], ys - 1, add=far_add, coded=True
        )
        far = [shift_y(far_code[(s - 1) * n : s * n], s) for s in range(1, ys)]
        near = piece(lambda i, m: m[to_y] * CORES + m[core_at], 1, add=near_add)
        return near, far

    def start_two(k, near, far):
        grad_code, a_code = finish_grad(queue, near, far, mirrored_a, k, step_a)
        codes = [a_code] + [shift_y(a_code, s) for s in range(1, ys)]
        others = [swap_core(x) for x in codes]
        back = mirror(grad_code)
        blocks = []
        for s in range(ys):
            blocks.append((codes[s], lambda m, s=s: m[from_y + s] * CORES + m[core_at]))
            blocks.append((others[s], lambda m, s=s: m[from_y + s] * CORES + 1 - m[core_at]))
        acc = None
        for block in blocks[:-late]:
            acc = product_two(queue, cov, [block], acc, lambda i, m: i, side)
        return acc, blocks[-late:], back

    def pieces_two(acc, blocks):
        landed = []
        for hop in range(1, side):
            piece = product_two(
                queue, cov, blocks, acc, lambda i, m, hop=hop: m[to_row + hop], 1, coded=True
            )
            landed.append(shift_row(piece, hop))
        kept = product_two(queue, cov, blocks, acc, lambda i, m: m[to_row], 1)
        return kept, landed

    def finish_b(k, value):
        value = value.reshape(side, ys, CORES, share, features)
        value = pick(value, own_core, 2) + swap_core(pick(value, other_core, 2))
        mine = pick(value, own_y, 1)
        for s in range(1, ys):
            away = encode(pick(value, next_y[s], 1), SCALE_V)
            mine = mine + decode(shift_y(away, s), SCALE_V)
        total = pick(mine, own_row, 0)
        for s in range(1, side):
            away = encode(pick(mine, next_row[s], 0), SCALE_V)
            total = total + decode(shift_row(away, s), SCALE_V)
        return factor_b[k].astype(F32) + step_b * total

    accs = [None] * projections
    for k in ks:
        accs[k] = early_one(k, None, 0)
    sums, seconds, fields, diffs, new_a, new_b = ({} for _ in range(6))
    for k in range(projections + 1):
        if k < projections:
            for s in range(1, side - late):
                accs[k] = early_one(k, accs[k], s)
            sums[k] = pieces_one(k, accs[k])
        if k > 0:
            fields[k - 1] = pieces_two(*seconds[k - 1][:2])
        if k > 1:
            value = second_grad(queue, fields[k - 2][0], fields[k - 2][1], diffs[k - 2])
            new_b[k - 2] = finish_b(k - 2, value)
        if k > 0:
            new_a[k - 1], diffs[k - 1] = second_diff(
                queue, seconds[k - 1][2], w, a, b, k - 1, step_a
            )
        if k < projections:
            seconds[k] = start_two(k, *sums[k])
    last = projections - 1
    value = second_grad(queue, fields[last][0], fields[last][1], diffs[last])
    new_b[last] = finish_b(last, value)
    return jnp.stack([new_a[k] for k in ks], 1), jnp.stack([new_b[k] for k in ks], 0)


def solution(mesh):
    in_specs = (
        P(("layer", "row"), "col"),
        P(("layer", "col", "row"), None, None),
        P(("layer", "col", "row"), None, None),
        P("layer", ("row", "col"), None),
    )
    out_specs = (P(("layer", "col", "row"), None, None), P("layer", ("row", "col"), None))

    return jax.shard_map(
        per_device, mesh=mesh, in_specs=in_specs, out_specs=out_specs, check_vma=False
    )
```

time: 683 us -> 240 us (0.35); the launches traced: 676 us -> 239 us
  waiting for transfers between devices: 404 us -> 77.1 us
  matrix products: 104 us -> 0 us
  blocking collectives: 88.6 us -> 0 us
  Pallas kernels: 0 us -> 80.3 us
  starting transfers between devices: 5.53 us -> 73.7 us
  local copies, waits for them, and re-layouts: 39.6 us -> 4.59 us
  other arithmetic: 19.2 us -> 2.35 us
  between operations: 14.4 us -> 1.41 us
    all_gather x3 -> x0, waiting for transfers between devices: 199 us -> none  [the longest x1 81.2 us: per_device(): lax.all_gather(new_a.reshape(row_count, 2 * R), 'row', axis=0, tiled=True)]
    dot_general x5 -> x0, matrix products: 104 us -> none  [the longest x1 57.8 us: per_device(): jnp.dot(cov_rows, a_panel, precision=highest, preferred_element_type=jnp....]
    psum x1 -> x0, waiting for transfers between devices: 100 us -> none  [per_device(): summed = lax.psum(partial_value, ('row', 'col'))]
    all_to_all x3 -> x0, blocking collectives: 88.6 us -> none  [the longest x2 59.1 us: transpose_full(): lax.all_to_all(flat, ('row', 'col'), split_axis=0, concat_axis=0, tiled=T...]
    reduce_scatter x2 -> x0, waiting for transfers between devices: 86.1 us -> none  [the longest x1 43.1 us: per_device(): lax.psum_scatter(jnp.dot(cov_rows, a_panel, precision=highest, preferred_...]
    pallas_call x0 -> x34, Pallas kernels: none -> 80.3 us  [call(): pl.pallas_call(body, out_shape=shapes, grid_spec=spec, input_output_alias...]
    ppermute x0 -> x42, waiting for transfers between devices: none -> 77.1 us  [the longest x21 49.1 us: shift_row(): return lax.ppermute(x, 'row', [(i, (i + s) % side) for i in range(side)])]
    ppermute x0 -> x42, starting transfers between devices: none -> 73.7 us  [the longest x21 41.3 us: shift_row(): return lax.ppermute(x, 'row', [(i, (i + s) % side) for i in range(side)])]
  transfers between devices with their start and end apart: 7 -> 42, of which waited for: 7 -> 14; matrix products, arithmetic and copies ran while one was open for 1% -> 2% of each run, Pallas kernels for 0% -> 29%
where the time goes in v1:
time: 240 us; the launch traced here: 239 us
  Pallas kernels  80.3 us (33%)
  waiting for transfers between devices  77.1 us (32%)
  starting transfers between devices  73.7 us (31%)
  local copies, waits for them, and re-layouts  4.59 us (2%)
    pallas_call x34, Pallas kernels, call(): pl.pallas_call(body, out_shape=shapes, grid_spec=spec, input_output_alias...  80.3 us
    ppermute x21, waiting for transfers between devices, shift_row(): return lax.ppermute(x, 'row', [(i, (i + s) % side) for i in range(side)])  49.1 us
    ppermute x21, starting transfers between devices, shift_row(): return lax.ppermute(x, 'row', [(i, (i + s) % side) for i in range(side)])  41.3 us
    ppermute x7, waiting for transfers between devices, shift_y(): return lax.ppermute(x, 'col', pairs)  27.9 us
    ppermute x7, starting transfers between devices, shift_y(): return lax.ppermute(x, 'col', pairs)  21.8 us
    ppermute x11, starting transfers between devices, swap_core(): return lax.ppermute(x, 'col', [(i, i ^ 1) for i in range(ys * CORES)])  8.61 us
  transfers between devices with their start and end apart: 42, of which 14 were waited for; matrix products, arithmetic and copies ran while one was open for 2% of the time, Pallas kernels for 29%

profile of v1, /device:TPU:0, one launch (start us, length us, event | category | flops | bytes accessed | tf_op | source)
XLA Modules:
  0.0 239.5 jit_solution(10315554796550353031)
XLA Ops:
  0.6 3.1 %collective-permute-start = (bf16[2,16,1024]{2,1,0:T(8,128)(2,1)}, bf16[2,16,1024]{2,1,0:T(8,128)(2,1)S(1)}, u32[]{:S(2)}, u32[]{:S(2)}) collective-permute-start(bf16[2,16,1024]{2,1,0:T(8,128)(2,1)} %param.7), channel_id=1, source_target_pairs={{0,4},{4,8},{8,12},{12,0},{1,5},{5,9},{9,13},{13,1},{2,6},{6,10},{... | collective-permute-start | bytes 196616 | tf_op jit(solution)/shard_map/ppermute | solution.py:353
  3.7 2.6 %collective-permute-start.1 = (bf16[2,16,1024]{2,1,0:T(8,128)(2,1)}, bf16[2,16,1024]{2,1,0:T(8,128)(2,1)S(1)}, u32[]{:S(2)}, u32[]{:S(2)}) collective-permute-start(bf16[2,16,1024]{2,1,0:T(8,128)(2,1)} %param.7), channel_id=1, source_target_pairs={{0,8},{4,12},{8,0},{12,4},{1,9},{5,13},{9,1},{13,5},{2,10},{6,14},... | collective-permute-start | bytes 196616 | tf_op jit(solution)/shard_map/ppermute | solution.py:353
  8.4 2.6 %collective-permute-done.1 = bf16[2,16,1024]{2,1,0:T(8,128)(2,1)S(1)} collective-permute-done((bf16[2,16,1024]{2,1,0:T(8,128)(2,1)}, bf16[2,16,1024]{2,1,0:T(8,128)(2,1)S(1)}, u32[]{:S(2)}, u32[]{:S(2)}) %collective-permute-start.1) | collective-permute-done | bytes 65568 | tf_op jit(solution)/shard_map/ppermute | solution.py:353
  13.7 6.3 %collective-permute-done.3 = bf16[4,2,16,1024]{3,2,1,0:T(8,128)(2,1)S(1)} collective-permute-done((bf16[4,2,16,1024]{3,2,1,0:T(8,128)(2,1)S(1)}, bf16[4,2,16,1024]{3,2,1,0:T(8,128)(2,1)S(1)}, u32[]{:S(2)}, u32[]{:S(2)}) %collective-permute-start.3) | collective-permute-done | bytes 262176 | tf_op jit(solution)/shard_map/ppermute | solution.py:350
  22.7 9.2 %shard_map.59 = (bf16[2048,2048]{1,0:T(8,128)(2,1)S(1)}, bf16[2048,2048]{1,0:T(8,128)(2,1)S(1)}) custom-call(s32[13]{0:T(128)S(1)} %concatenate.3.m, f32[2048,2048]{1,0:T(8,128)} %c.1), custom_call_target="tpu_custom_call" | custom-call | bytes 33554432 | tf_op jit(solution)/shard_map/pallas_call | solution.py:54
  31.9 2.5 %shard_map.60.b = bf16[2,256,1024]{2,1,0:T(8,128)(2,1)S(1)} custom-call(s32[13]{0:T(128)S(1)} %concatenate.3.m, bf16[2,4,2,16,1024]{4,3,2,1,0:T(8,128)(2,1)S(1)} %pad_maximum_fusion.1.own, bf16[2,4,2,16,1024]{4,3,2,1,0:T(8,128)(2,1)} %collective-permute-done.4.other), custom_call_target="tpu_custom_call" | custom-call | bytes 2097152 | tf_op jit(solution)/shard_map/pallas_call | solution.py:54
  42.5 3.1 %shard_map.63.refs_3_ = f32[2048,256]{1,0:T(8,128)S(1)} custom-call(s32[13]{0:T(128)S(1)} %concatenate.3.m, bf16[2048,2048]{1,0:T(8,128)(2,1)S(1)} %get-tuple-element.105.refs_0_.refs_1_, bf16[2048,2048]{1,0:T(8,128)(2,1)S(1)} %get-tuple-element.106.refs_1_.refs_2_.refs_3_, bf16[512,256]{1,0:T(8,128)(2,1)S(1)} %shard_map.61.refs_2_), custom_call_target="tpu_custom_call" | custom-call | flops 1610612736 | bytes 19136512 | tf_op jit(solution)/shard_map/pallas_call | solution.py:54
  45.6 3.1 %shard_map.64.refs_3_ = f32[2048,256]{1,0:T(8,128)S(1)} custom-call(s32[13]{0:T(128)S(1)} %concatenate.3.m, bf16[2048,2048]{1,0:T(8,128)(2,1)S(1)} %get-tuple-element.105.refs_0_.refs_1_, bf16[2048,2048]{1,0:T(8,128)(2,1)S(1)} %get-tuple-element.106.refs_1_.refs_2_.refs_3_, bf16[512,256]{1,0:T(8,128)(2,1)S(1)} %shard_map.62.refs_2_), custom_call_target="tpu_custom_call" | custom-call | flops 1610612736 | bytes 19136512 | tf_op jit(solution)/shard_map/pallas_call | solution.py:54
  48.8 3.3 %shard_map.65.refs_6_ = f32[2048,256]{1,0:T(8,128)S(1)} custom-call(s32[13]{0:T(128)S(1)} %concatenate.3.m, bf16[2048,2048]{1,0:T(8,128)(2,1)S(1)} %get-tuple-element.105.refs_0_.refs_1_, bf16[2048,2048]{1,0:T(8,128)(2,1)S(1)} %get-tuple-element.106.refs_1_.refs_2_.refs_3_, ...), custom_call_target="tpu_custom_call", output_to_operand_aliasing={{}: (4, {})} | custom-call | flops 1610612736 | bytes 21233664 | tf_op jit(solution)/shard_map/pallas_call | solution.py:54
  52.1 6.0 %collective-permute-done.6.refs_4_ = bf16[512,256]{1,0:T(8,128)(2,1)S(1)} collective-permute-done((bf16[512,256]{1,0:T(8,128)(2,1)S(1)}, bf16[512,256]{1,0:T(8,128)(2,1)S(1)}, u32[]{:S(2)}, u32[]{:S(2)}) %collective-permute-start.6) | collective-permute-done | bytes 262176 | tf_op jit(solution)/shard_map/ppermute | solution.py:353
  62.5 7.5 %collective-permute-start.9 = (f32[512,256]{1,0:T(8,128)S(1)}, f32[512,256]{1,0:T(8,128)S(1)}, u32[]{:S(2)}, u32[]{:S(2)}) collective-permute-start(f32[512,256]{1,0:T(8,128)S(1)} %shard_map.67), channel_id=1, source_target_pairs={{0,1},{1,0},{2,3},{3,2},{4,5},{5,4},{6,7},{7,6},{8,9},{9,8},{10,11... | collective-permute-start | bytes 1572872 | tf_op jit(solution)/shard_map/ppermute | solution.py:346
  75.5 7.2 %collective-permute-done.11.rest_0_ = bf16[512,256]{1,0:T(8,128)(2,1)S(1)} collective-permute-done((bf16[512,256]{1,0:T(8,128)(2,1)S(1)}, bf16[512,256]{1,0:T(8,128)(2,1)S(1)}, u32[]{:S(2)}, u32[]{:S(2)}) %collective-permute-start.11) | collective-permute-done | bytes 262176 | tf_op jit(solution)/shard_map/ppermute | solution.py:350
  84.2 4.7 %collective-permute-start.13 = (bf16[512,256]{1,0:T(8,128)(2,1)S(1)}, bf16[512,256]{1,0:T(8,128)(2,1)S(1)}, u32[]{:S(2)}, u32[]{:S(2)}) collective-permute-start(bf16[512,256]{1,0:T(8,128)(2,1)S(1)} %shard_map.62.refs_2_), channel_id=1, source_target_pairs={{0,4},{4,8},{8,12},{12,0},{1,5},{5,9},{9,13},{13,1},{2,6},{6,10},{... | collective-permute-start | bytes 786440 | tf_op jit(solution)/shard_map/ppermute | solution.py:353
  88.9 9.8 %collective-permute-start.14 = (bf16[512,256]{1,0:T(8,128)(2,1)S(1)}, bf16[512,256]{1,0:T(8,128)(2,1)S(1)}, u32[]{:S(2)}, u32[]{:S(2)}) collective-permute-start(bf16[512,256]{1,0:T(8,128)(2,1)S(1)} %shard_map.62.refs_2_), channel_id=1, source_target_pairs={{0,8},{4,12},{8,0},{12,4},{1,9},{5,13},{9,1},{13,5},{2,10},{6,14},... | collective-permute-start | bytes 786440 | tf_op jit(solution)/shard_map/ppermute | solution.py:353
  99.4 3.6 %shard_map.71.refs_3_ = f32[256,2048]{1,0:T(8,128)S(1)} custom-call(s32[13]{0:T(128)S(1)} %concatenate.3.m, bf16[2048,2048]{1,0:T(8,128)(2,1)S(1)} %get-tuple-element.105.refs_0_.refs_1_, bf16[2048,2048]{1,0:T(8,128)(2,1)S(1)} %get-tuple-element.106.refs_1_.refs_2_.refs_3_, bf16[256,512]{1,0:T(8,128)(2,1)S(1)} %get-tuple-element.125.refs_2_), custom_call_target="tpu_custom_call" | custom-call | flops 1610612736 | bytes 19136512 | tf_op jit(solution)/shard_map/pallas_call | solution.py:54
  103.1 3.8 %shard_map.72.refs_6_ = f32[256,2048]{1,0:T(8,128)S(1)} custom-call(s32[13]{0:T(128)S(1)} %concatenate.3.m, bf16[2048,2048]{1,0:T(8,128)(2,1)S(1)} %get-tuple-element.105.refs_0_.refs_1_, bf16[2048,2048]{1,0:T(8,128)(2,1)S(1)} %get-tuple-element.106.refs_1_.refs_2_.refs_3_, ...), custom_call_target="tpu_custom_call", output_to_operand_aliasing={{}: (4, {})} | custom-call | flops 1610612736 | bytes 21233664 | tf_op jit(solution)/shard_map/pallas_call | solution.py:54
  106.8 3.3 %shard_map.73.refs_6_ = f32[2048,256]{1,0:T(8,128)S(1)} custom-call(s32[13]{0:T(128)S(1)} %concatenate.3.m, bf16[2048,2048]{1,0:T(8,128)(2,1)S(1)} %get-tuple-element.105.refs_0_.refs_1_, bf16[2048,2048]{1,0:T(8,128)(2,1)S(1)} %get-tuple-element.106.refs_1_.refs_2_.refs_3_, ...), custom_call_target="tpu_custom_call", output_to_operand_aliasing={{}: (4, {})} | custom-call | flops 1610612736 | bytes 21233664 | tf_op jit(solution)/shard_map/pallas_call | solution.py:54
  110.1 5.9 %collective-permute-done.14.refs_4_ = bf16[512,256]{1,0:T(8,128)(2,1)S(1)} collective-permute-done((bf16[512,256]{1,0:T(8,128)(2,1)S(1)}, bf16[512,256]{1,0:T(8,128)(2,1)S(1)}, u32[]{:S(2)}, u32[]{:S(2)}) %collective-permute-start.14) | collective-permute-done | bytes 262176 | tf_op jit(solution)/shard_map/ppermute | solution.py:353
  120.7 7.9 %collective-permute-done.18.refs_4_ = bf16[256,512]{1,0:T(8,128)(2,1)S(1)} collective-permute-done((bf16[256,512]{1,0:T(8,128)(2,1)S(1)}, bf16[256,512]{1,0:T(8,128)(2,1)S(1)}, u32[]{:S(2)}, u32[]{:S(2)}) %collective-permute-start.18) | collective-permute-done | bytes 262176 | tf_op jit(solution)/shard_map/ppermute | solution.py:350
  134.6 7.8 %collective-permute-start.21 = (bf16[512,256]{1,0:T(8,128)(2,1)S(1)}, bf16[512,256]{1,0:T(8,128)(2,1)S(1)}, u32[]{:S(2)}, u32[]{:S(2)}) collective-permute-start(bf16[512,256]{1,0:T(8,128)(2,1)S(1)} %shard_map.76), channel_id=1, source_target_pairs={{0,2},{1,3},{2,0},{3,1},{4,6},{5,7},{6,4},{7,5},{8,10},{9,11},{10,... | collective-permute-start | bytes 786440 | tf_op jit(solution)/shard_map/ppermute | solution.py:350
  151.3 2.5 %collective-permute-start.23 = (bf16[256,512]{1,0:T(8,128)(2,1)S(1)}, bf16[256,512]{1,0:T(8,128)(2,1)S(1)}, u32[]{:S(2)}, u32[]{:S(2)}) collective-permute-start(bf16[256,512]{1,0:T(8,128)(2,1)S(1)} %get-tuple-element.153.refs_2_), channel_id=1, source_target_pairs={{0,2},{1,3},{2,0},{3,1},{4,6},{5,7},{6,4},{7,5},{8,10},{9,11},{10,... | collective-permute-start | bytes 786440 | tf_op jit(solution)/shard_map/ppermute | solution.py:350
  153.8 3.0 %collective-permute-start.27 = (bf16[256,512]{1,0:T(8,128)(2,1)S(1)}, bf16[256,512]{1,0:T(8,128)(2,1)S(1)}, u32[]{:S(2)}, u32[]{:S(2)}) collective-permute-start(bf16[256,512]{1,0:T(8,128)(2,1)S(1)} %shard_map.80), channel_id=1, source_target_pairs={{0,12},{4,0},{8,4},{12,8},{1,13},{5,1},{9,5},{13,9},{2,14},{6,2},{... | collective-permute-start | bytes 786440 | tf_op jit(solution)/shard_map/ppermute | solution.py:353
  157.4 3.0 %collective-permute-done.23.refs_4_ = bf16[256,512]{1,0:T(8,128)(2,1)S(1)} collective-permute-done((bf16[256,512]{1,0:T(8,128)(2,1)S(1)}, bf16[256,512]{1,0:T(8,128)(2,1)S(1)}, u32[]{:S(2)}, u32[]{:S(2)}) %collective-permute-start.23) | collective-permute-done | bytes 262176 | tf_op jit(solution)/shard_map/ppermute | solution.py:350
  160.4 3.6 %shard_map.84.refs_3_ = f32[256,2048]{1,0:T(8,128)S(1)} custom-call(s32[13]{0:T(128)S(1)} %concatenate.3.m, bf16[2048,2048]{1,0:T(8,128)(2,1)S(1)} %get-tuple-element.105.refs_0_.refs_1_, bf16[2048,2048]{1,0:T(8,128)(2,1)S(1)} %get-tuple-element.106.refs_1_.refs_2_.refs_3_, bf16[256,512]{1,0:T(8,128)(2,1)S(1)} %get-tuple-element.153.refs_2_), custom_call_target="tpu_custom_call" | custom-call | flops 1610612736 | bytes 19136512 | tf_op jit(solution)/shard_map/pallas_call | solution.py:54
  164.7 3.8 %shard_map.85.refs_6_ = f32[256,2048]{1,0:T(8,128)S(1)} custom-call(s32[13]{0:T(128)S(1)} %concatenate.3.m, bf16[2048,2048]{1,0:T(8,128)(2,1)S(1)} %get-tuple-element.105.refs_0_.refs_1_, bf16[2048,2048]{1,0:T(8,128)(2,1)S(1)} %get-tuple-element.106.refs_1_.refs_2_.refs_3_, ...), custom_call_target="tpu_custom_call", output_to_operand_aliasing={{}: (4, {})} | custom-call | flops 1610612736 | bytes 21233664 | tf_op jit(solution)/shard_map/pallas_call | solution.py:54
  174.9 12.2 %collective-permute-done.26.rest_1_ = bf16[256,512]{1,0:T(8,128)(2,1)S(1)} collective-permute-done((bf16[256,512]{1,0:T(8,128)(2,1)S(1)}, bf16[256,512]{1,0:T(8,128)(2,1)S(1)}, u32[]{:S(2)}, u32[]{:S(2)}) %collective-permute-start.26) | collective-permute-done | bytes 262176 | tf_op jit(solution)/shard_map/ppermute | solution.py:353
  193.2 4.2 %collective-permute-done.36.rest_2_ = bf16[256,512]{1,0:T(8,128)(2,1)S(1)} collective-permute-done((bf16[256,512]{1,0:T(8,128)(2,1)S(1)}, bf16[256,512]{1,0:T(8,128)(2,1)S(1)}, u32[]{:S(2)}, u32[]{:S(2)}) %collective-permute-start.36) | collective-permute-done | bytes 262176 | tf_op jit(solution)/shard_map/ppermute | solution.py:353
  197.5 17.2 %collective-permute-done.35.rest_1_ = bf16[256,512]{1,0:T(8,128)(2,1)S(1)} collective-permute-done((bf16[256,512]{1,0:T(8,128)(2,1)S(1)}, bf16[256,512]{1,0:T(8,128)(2,1)S(1)}, u32[]{:S(2)}, u32[]{:S(2)}) %collective-permute-start.35) | collective-permute-done | bytes 262176 | tf_op jit(solution)/shard_map/ppermute | solution.py:353
  217.2 6.0 %collective-permute-start.30 = (bf16[4,16,1024]{2,1,0:T(8,128)(2,1)S(1)}, bf16[4,16,1024]{2,1,0:T(8,128)(2,1)S(1)}, u32[]{:S(2)}, u32[]{:S(2)}) collective-permute-start(bf16[4,16,1024]{2,1,0:T(8,128)(2,1)S(1)} %fusion.7), channel_id=1, source_target_pairs={{0,2},{1,3},{2,0},{3,1},{4,6},{5,7},{6,4},{7,5},{8,10},{9,11},{10,... | collective-permute-start | bytes 393224 | tf_op jit(solution)/shard_map/ppermute | solution.py:350
  225.1 2.5 %collective-permute-done.30 = bf16[4,16,1024]{2,1,0:T(8,128)(2,1)S(1)} collective-permute-done((bf16[4,16,1024]{2,1,0:T(8,128)(2,1)S(1)}, bf16[4,16,1024]{2,1,0:T(8,128)(2,1)S(1)}, u32[]{:S(2)}, u32[]{:S(2)}) %collective-permute-start.30) | collective-permute-done | bytes 131104 | tf_op jit(solution)/shard_map/ppermute | solution.py:350
  227.8 3.7 %collective-permute-start.33 = (bf16[16,1024]{1,0:T(8,128)(2,1)S(1)}, bf16[16,1024]{1,0:T(8,128)(2,1)S(1)}, u32[]{:S(2)}, u32[]{:S(2)}) collective-permute-start(bf16[16,1024]{1,0:T(8,128)(2,1)S(1)} %get-tuple-element.194), channel_id=1, source_target_pairs={{0,12},{4,0},{8,4},{12,8},{1,13},{5,1},{9,5},{13,9},{2,14},{6,2},{... | collective-permute-start | bytes 98312 | tf_op jit(solution)/shard_map/ppermute | solution.py:353
  233.9 2.8 %collective-permute-start.41 = (bf16[16,1024]{1,0:T(8,128)(2,1)S(1)}, bf16[16,1024]{1,0:T(8,128)(2,1)S(1)}, u32[]{:S(2)}, u32[]{:S(2)}) collective-permute-start(bf16[16,1024]{1,0:T(8,128)(2,1)S(1)} %get-tuple-element.197), channel_id=1, source_target_pairs={{0,12},{4,0},{8,4},{12,8},{1,13},{5,1},{9,5},{13,9},{2,14},{6,2},{... | collective-permute-start | bytes 98312 | tf_op jit(solution)/shard_map/ppermute | solution.py:353
  (120 shorter events, 70.3 us)
Async XLA Ops:
  20.1 11.8 %collective-permute-start.4 = (bf16[2,4,2,16,1024]{4,3,2,1,0:T(8,128)(2,1)S(1)}, bf16[2,4,2,16,1024]{4,3,2,1,0:T(8,128)(2,1)}, u32[]{:S(2)}, u32[]{:S(2)}) collective-permute-start(bf16[2,4,2,16,1024]{4,3,2,1,0:T(8,128)(2,1)S(1)} %pad_maximum_fusion.1.own), channel_id=1, source_target_pairs={{0,1},{1,0},{2,3},{3,2},{4,5},{5,4},{6,7},{7,6},{8,9},{9,8},{10,11... | collective-permute-start | bytes 1572872 | tf_op jit(solution)/shard_map/ppermute | solution.py:346
  36.3 12.5 %collective-permute-start.5 = (bf16[512,256]{1,0:T(8,128)(2,1)S(1)}, bf16[512,256]{1,0:T(8,128)(2,1)S(1)}, u32[]{:S(2)}, u32[]{:S(2)}) collective-permute-start(bf16[512,256]{1,0:T(8,128)(2,1)S(1)} %shard_map.61.refs_2_), channel_id=1, source_target_pairs={{0,4},{4,8},{8,12},{12,0},{1,5},{5,9},{9,13},{13,1},{2,6},{6,10},{... | collective-permute-start | bytes 786440 | tf_op jit(solution)/shard_map/ppermute | solution.py:353
  38.3 19.8 %collective-permute-start.6 = (bf16[512,256]{1,0:T(8,128)(2,1)S(1)}, bf16[512,256]{1,0:T(8,128)(2,1)S(1)}, u32[]{:S(2)}, u32[]{:S(2)}) collective-permute-start(bf16[512,256]{1,0:T(8,128)(2,1)S(1)} %shard_map.61.refs_2_), channel_id=1, source_target_pairs={{0,8},{4,12},{8,0},{12,4},{1,9},{5,13},{9,1},{13,5},{2,10},{6,14},... | collective-permute-start | bytes 786440 | tf_op jit(solution)/shard_map/ppermute | solution.py:353
  38.5 19.6 %collective-permute-start.7 = (bf16[512,256]{1,0:T(8,128)(2,1)S(1)}, bf16[512,256]{1,0:T(8,128)(2,1)S(1)}, u32[]{:S(2)}, u32[]{:S(2)}) collective-permute-start(bf16[512,256]{1,0:T(8,128)(2,1)S(1)} %shard_map.61.refs_2_), channel_id=1, source_target_pairs={{0,12},{4,0},{8,4},{12,8},{1,13},{5,1},{9,5},{13,9},{2,14},{6,2},{... | collective-permute-start | bytes 786440 | tf_op jit(solution)/shard_map/ppermute | solution.py:353
  59.9 10.1 %collective-permute-start.8 = (f32[512,256]{1,0:T(8,128)S(1)}, f32[512,256]{1,0:T(8,128)S(1)}, u32[]{:S(2)}, u32[]{:S(2)}) collective-permute-start(f32[512,256]{1,0:T(8,128)S(1)} %shard_map.66), channel_id=1, source_target_pairs={{0,1},{1,0},{2,3},{3,2},{4,5},{5,4},{6,7},{7,6},{8,9},{9,8},{10,11... | collective-permute-start | bytes 1572872 | tf_op jit(solution)/shard_map/ppermute | solution.py:346
  60.0 13.6 %collective-permute-start.10 = (bf16[512,2,256]{2,1,0:T(2,128)(2,1)S(1)}, bf16[512,2,256]{2,1,0:T(2,128)(2,1)S(1)}, u32[]{:S(2)}, u32[]{:S(2)}) collective-permute-start(bf16[512,2,256]{2,1,0:T(2,128)(2,1)S(1)} %copy-done.3), channel_id=1, source_target_pairs={{0,0},{1,4},{2,8},{3,12},{4,1},{5,5},{6,9},{7,13},{8,2},{9,6},{10,... | collective-permute-start | bytes 1572872 | tf_op jit(solution)/shard_map/ppermute | solution.py:357
  62.5 11.1 %collective-permute-start.9 = (f32[512,256]{1,0:T(8,128)S(1)}, f32[512,256]{1,0:T(8,128)S(1)}, u32[]{:S(2)}, u32[]{:S(2)}) collective-permute-start(f32[512,256]{1,0:T(8,128)S(1)} %shard_map.67), channel_id=1, source_target_pairs={{0,1},{1,0},{2,3},{3,2},{4,5},{5,4},{6,7},{7,6},{8,9},{9,8},{10,11... | collective-permute-start | bytes 1572872 | tf_op jit(solution)/shard_map/ppermute | solution.py:346
  71.9 10.8 %collective-permute-start.11 = (bf16[512,256]{1,0:T(8,128)(2,1)S(1)}, bf16[512,256]{1,0:T(8,128)(2,1)S(1)}, u32[]{:S(2)}, u32[]{:S(2)}) collective-permute-start(bf16[512,256]{1,0:T(8,128)(2,1)S(1)} %shard_map.68), channel_id=1, source_target_pairs={{0,2},{1,3},{2,0},{3,1},{4,6},{5,7},{6,4},{7,5},{8,10},{9,11},{10,... | collective-permute-start | bytes 786440 | tf_op jit(solution)/shard_map/ppermute | solution.py:350
  84.0 19.0 %collective-permute-start.12 = (bf16[256,512]{1,0:T(8,128)(2,1)S(1)}, bf16[256,512]{1,0:T(8,128)(2,1)S(1)}, u32[]{:S(2)}, u32[]{:S(2)}) collective-permute-start(bf16[256,512]{1,0:T(8,128)(2,1)S(1)} %get-tuple-element.125.refs_2_), channel_id=1, source_target_pairs={{0,1},{1,0},{2,3},{3,2},{4,5},{5,4},{6,7},{7,6},{8,9},{9,8},{10,11... | collective-permute-start | bytes 786440 | tf_op jit(solution)/shard_map/ppermute | solution.py:346
  84.2 22.6 %collective-permute-start.13 = (bf16[512,256]{1,0:T(8,128)(2,1)S(1)}, bf16[512,256]{1,0:T(8,128)(2,1)S(1)}, u32[]{:S(2)}, u32[]{:S(2)}) collective-permute-start(bf16[512,256]{1,0:T(8,128)(2,1)S(1)} %shard_map.62.refs_2_), channel_id=1, source_target_pairs={{0,4},{4,8},{8,12},{12,0},{1,5},{5,9},{9,13},{13,1},{2,6},{6,10},{... | collective-permute-start | bytes 786440 | tf_op jit(solution)/shard_map/ppermute | solution.py:353
  88.9 27.1 %collective-permute-start.14 = (bf16[512,256]{1,0:T(8,128)(2,1)S(1)}, bf16[512,256]{1,0:T(8,128)(2,1)S(1)}, u32[]{:S(2)}, u32[]{:S(2)}) collective-permute-start(bf16[512,256]{1,0:T(8,128)(2,1)S(1)} %shard_map.62.refs_2_), channel_id=1, source_target_pairs={{0,8},{4,12},{8,0},{12,4},{1,9},{5,13},{9,1},{13,5},{2,10},{6,14},... | collective-permute-start | bytes 786440 | tf_op jit(solution)/shard_map/ppermute | solution.py:353
  98.7 17.3 %collective-permute-start.15 = (bf16[512,256]{1,0:T(8,128)(2,1)S(1)}, bf16[512,256]{1,0:T(8,128)(2,1)S(1)}, u32[]{:S(2)}, u32[]{:S(2)}) collective-permute-start(bf16[512,256]{1,0:T(8,128)(2,1)S(1)} %shard_map.62.refs_2_), channel_id=1, source_target_pairs={{0,12},{4,0},{8,4},{12,8},{1,13},{5,1},{9,5},{13,9},{2,14},{6,2},{... | collective-permute-start | bytes 786440 | tf_op jit(solution)/shard_map/ppermute | solution.py:353
  117.8 11.4 %collective-permute-start.16 = (f32[512,256]{1,0:T(8,128)S(1)}, f32[512,256]{1,0:T(8,128)S(1)}, u32[]{:S(2)}, u32[]{:S(2)}) collective-permute-start(f32[512,256]{1,0:T(8,128)S(1)} %shard_map.74), channel_id=1, source_target_pairs={{0,1},{1,0},{2,3},{3,2},{4,5},{5,4},{6,7},{7,6},{8,9},{9,8},{10,11... | collective-permute-start | bytes 1572872 | tf_op jit(solution)/shard_map/ppermute | solution.py:346
  119.7 11.4 %collective-permute-start.17 = (f32[512,256]{1,0:T(8,128)S(1)}, f32[512,256]{1,0:T(8,128)S(1)}, u32[]{:S(2)}, u32[]{:S(2)}) collective-permute-start(f32[512,256]{1,0:T(8,128)S(1)} %shard_map.75), channel_id=1, source_target_pairs={{0,1},{1,0},{2,3},{3,2},{4,5},{5,4},{6,7},{7,6},{8,9},{9,8},{10,11... | collective-permute-start | bytes 1572872 | tf_op jit(solution)/shard_map/ppermute | solution.py:346
  120.3 8.3 %collective-permute-start.18 = (bf16[256,512]{1,0:T(8,128)(2,1)S(1)}, bf16[256,512]{1,0:T(8,128)(2,1)S(1)}, u32[]{:S(2)}, u32[]{:S(2)}) collective-permute-start(bf16[256,512]{1,0:T(8,128)(2,1)S(1)} %get-tuple-element.125.refs_2_), channel_id=1, source_target_pairs={{0,2},{1,3},{2,0},{3,1},{4,6},{5,7},{6,4},{7,5},{8,10},{9,11},{10,... | collective-permute-start | bytes 786440 | tf_op jit(solution)/shard_map/ppermute | solution.py:350
  128.6 18.6 %collective-permute-start.20 = (bf16[512,256]{1,0:T(8,128)(2,1)S(1)}, bf16[512,256]{1,0:T(8,128)(2,1)S(1)}, u32[]{:S(2)}, u32[]{:S(2)}) collective-permute-start(bf16[512,256]{1,0:T(8,128)(2,1)S(1)} %get-tuple-element.143), channel_id=1, source_target_pairs={{0,0},{1,4},{2,8},{3,12},{4,1},{5,5},{6,9},{7,13},{8,2},{9,6},{10,... | collective-permute-start | bytes 786440 | tf_op jit(solution)/shard_map/ppermute | solution.py:357
  134.6 15.4 %collective-permute-start.21 = (bf16[512,256]{1,0:T(8,128)(2,1)S(1)}, bf16[512,256]{1,0:T(8,128)(2,1)S(1)}, u32[]{:S(2)}, u32[]{:S(2)}) collective-permute-start(bf16[512,256]{1,0:T(8,128)(2,1)S(1)} %shard_map.76), channel_id=1, source_target_pairs={{0,2},{1,3},{2,0},{3,1},{4,6},{5,7},{6,4},{7,5},{8,10},{9,11},{10,... | collective-permute-start | bytes 786440 | tf_op jit(solution)/shard_map/ppermute | solution.py:350
  151.3 9.1 %collective-permute-start.23 = (bf16[256,512]{1,0:T(8,128)(2,1)S(1)}, bf16[256,512]{1,0:T(8,128)(2,1)S(1)}, u32[]{:S(2)}, u32[]{:S(2)}) collective-permute-start(bf16[256,512]{1,0:T(8,128)(2,1)S(1)} %get-tuple-element.153.refs_2_), channel_id=1, source_target_pairs={{0,2},{1,3},{2,0},{3,1},{4,6},{5,7},{6,4},{7,5},{8,10},{9,11},{10,... | collective-permute-start | bytes 786440 | tf_op jit(solution)/shard_map/ppermute | solution.py:350
  153.8 10.2 %collective-permute-start.22 = (bf16[256,512]{1,0:T(8,128)(2,1)S(1)}, bf16[256,512]{1,0:T(8,128)(2,1)S(1)}, u32[]{:S(2)}, u32[]{:S(2)}) collective-permute-start(bf16[256,512]{1,0:T(8,128)(2,1)S(1)} %get-tuple-element.153.refs_2_), channel_id=1, source_target_pairs={{0,1},{1,0},{2,3},{3,2},{4,5},{5,4},{6,7},{7,6},{8,9},{9,8},{10,11... | collective-permute-start | bytes 786440 | tf_op jit(solution)/shard_map/ppermute | solution.py:346
  153.8 21.1 %collective-permute-start.27 = (bf16[256,512]{1,0:T(8,128)(2,1)S(1)}, bf16[256,512]{1,0:T(8,128)(2,1)S(1)}, u32[]{:S(2)}, u32[]{:S(2)}) collective-permute-start(bf16[256,512]{1,0:T(8,128)(2,1)S(1)} %shard_map.80), channel_id=1, source_target_pairs={{0,12},{4,0},{8,4},{12,8},{1,13},{5,1},{9,5},{13,9},{2,14},{6,2},{... | collective-permute-start | bytes 786440 | tf_op jit(solution)/shard_map/ppermute | solution.py:353
  156.8 30.2 %collective-permute-start.26 = (bf16[256,512]{1,0:T(8,128)(2,1)S(1)}, bf16[256,512]{1,0:T(8,128)(2,1)S(1)}, u32[]{:S(2)}, u32[]{:S(2)}) collective-permute-start(bf16[256,512]{1,0:T(8,128)(2,1)S(1)} %shard_map.79), channel_id=1, source_target_pairs={{0,8},{4,12},{8,0},{12,4},{1,9},{5,13},{9,1},{13,5},{2,10},{6,14},... | collective-permute-start | bytes 786440 | tf_op jit(solution)/shard_map/ppermute | solution.py:353
  157.4 29.6 %collective-permute-start.25 = (bf16[256,512]{1,0:T(8,128)(2,1)S(1)}, bf16[256,512]{1,0:T(8,128)(2,1)S(1)}, u32[]{:S(2)}, u32[]{:S(2)}) collective-permute-start(bf16[256,512]{1,0:T(8,128)(2,1)S(1)} %shard_map.78), channel_id=1, source_target_pairs={{0,4},{4,8},{8,12},{12,0},{1,5},{5,9},{9,13},{13,1},{2,6},{6,10},{... | collective-permute-start | bytes 786440 | tf_op jit(solution)/shard_map/ppermute | solution.py:353
  160.4 8.1 %collective-permute-start.24 = (bf16[256,512]{1,0:T(8,128)(2,1)S(1)}, bf16[256,512]{1,0:T(8,128)(2,1)S(1)}, u32[]{:S(2)}, u32[]{:S(2)}) collective-permute-start(bf16[256,512]{1,0:T(8,128)(2,1)S(1)} %collective-permute-done.23.refs_4_), channel_id=1, source_target_pairs={{0,1},{1,0},{2,3},{3,2},{4,5},{5,4},{6,7},{7,6},{8,9},{9,8},{10,11... | collective-permute-start | bytes 786440 | tf_op jit(solution)/shard_map/ppermute | solution.py:346
  164.0 27.5 %collective-permute-start.28 = (bf16[512,256]{1,0:T(8,128)(2,1)S(1)}, bf16[512,256]{1,0:T(8,128)(2,1)S(1)}, u32[]{:S(2)}, u32[]{:S(2)}) collective-permute-start(bf16[512,256]{1,0:T(8,128)(2,1)S(1)} %get-tuple-element.168), channel_id=1, source_target_pairs={{0,0},{1,4},{2,8},{3,12},{4,1},{5,5},{6,9},{7,13},{8,2},{9,6},{10,... | collective-permute-start | bytes 786440 | tf_op jit(solution)/shard_map/ppermute | solution.py:357
  189.2 8.3 %collective-permute-start.36 = (bf16[256,512]{1,0:T(8,128)(2,1)S(1)}, bf16[256,512]{1,0:T(8,128)(2,1)S(1)}, u32[]{:S(2)}, u32[]{:S(2)}) collective-permute-start(bf16[256,512]{1,0:T(8,128)(2,1)S(1)} %shard_map.88), channel_id=1, source_target_pairs={{0,12},{4,0},{8,4},{12,8},{1,13},{5,1},{9,5},{13,9},{2,14},{6,2},{... | collective-permute-start | bytes 786440 | tf_op jit(solution)/shard_map/ppermute | solution.py:353
  189.3 25.4 %collective-permute-start.35 = (bf16[256,512]{1,0:T(8,128)(2,1)S(1)}, bf16[256,512]{1,0:T(8,128)(2,1)S(1)}, u32[]{:S(2)}, u32[]{:S(2)}) collective-permute-start(bf16[256,512]{1,0:T(8,128)(2,1)S(1)} %shard_map.87), channel_id=1, source_target_pairs={{0,8},{4,12},{8,0},{12,4},{1,9},{5,13},{9,1},{13,5},{2,10},{6,14},... | collective-permute-start | bytes 786440 | tf_op jit(solution)/shard_map/ppermute | solution.py:353
  189.4 25.3 %collective-permute-start.34 = (bf16[256,512]{1,0:T(8,128)(2,1)S(1)}, bf16[256,512]{1,0:T(8,128)(2,1)S(1)}, u32[]{:S(2)}, u32[]{:S(2)}) collective-permute-start(bf16[256,512]{1,0:T(8,128)(2,1)S(1)} %shard_map.86), channel_id=1, source_target_pairs={{0,4},{4,8},{8,12},{12,0},{1,5},{5,9},{9,13},{13,1},{2,6},{6,10},{... | collective-permute-start | bytes 786440 | tf_op jit(solution)/shard_map/ppermute | solution.py:353
  191.5 25.6 %collective-permute-start.29 = (f32[4,2,16,1024]{3,2,0,1:T(8,128)S(1)}, f32[4,2,16,1024]{3,2,0,1:T(8,128)S(1)}, u32[]{:S(2)}, u32[]{:S(2)}) collective-permute-start(f32[4,2,16,1024]{3,2,0,1:T(8,128)S(1)} %bitcast.102), channel_id=1, source_target_pairs={{0,1},{1,0},{2,3},{3,2},{4,5},{5,4},{6,7},{7,6},{8,9},{9,8},{10,11... | collective-permute-start | bytes 1572872 | tf_op jit(solution)/shard_map/ppermute | solution.py:346
  217.2 10.3 %collective-permute-start.30 = (bf16[4,16,1024]{2,1,0:T(8,128)(2,1)S(1)}, bf16[4,16,1024]{2,1,0:T(8,128)(2,1)S(1)}, u32[]{:S(2)}, u32[]{:S(2)}) collective-permute-start(bf16[4,16,1024]{2,1,0:T(8,128)(2,1)S(1)} %fusion.7), channel_id=1, source_target_pairs={{0,2},{1,3},{2,0},{3,1},{4,6},{5,7},{6,4},{7,5},{8,10},{9,11},{10,... | collective-permute-start | bytes 393224 | tf_op jit(solution)/shard_map/ppermute | solution.py:350
  223.3 8.3 %collective-permute-start.38 = (bf16[4,16,1024]{2,1,0:T(8,128)(2,1)S(1)}, bf16[4,16,1024]{2,1,0:T(8,128)(2,1)S(1)}, u32[]{:S(2)}, u32[]{:S(2)}) collective-permute-start(bf16[4,16,1024]{2,1,0:T(8,128)(2,1)S(1)} %fusion.10), channel_id=1, source_target_pairs={{0,2},{1,3},{2,0},{3,1},{4,6},{5,7},{6,4},{7,5},{8,10},{9,11},{10,... | collective-permute-start | bytes 393224 | tf_op jit(solution)/shard_map/ppermute | solution.py:350
  227.8 10.8 %collective-permute-start.32 = (bf16[16,1024]{1,0:T(8,128)(2,1)S(1)}, bf16[16,1024]{1,0:T(8,128)(2,1)S(1)}, u32[]{:S(2)}, u32[]{:S(2)}) collective-permute-start(bf16[16,1024]{1,0:T(8,128)(2,1)S(1)} %get-tuple-element.195), channel_id=1, source_target_pairs={{0,8},{4,12},{8,0},{12,4},{1,9},{5,13},{9,1},{13,5},{2,10},{6,14},... | collective-permute-start | bytes 98312 | tf_op jit(solution)/shard_map/ppermute | solution.py:353
  227.8 10.8 %collective-permute-start.33 = (bf16[16,1024]{1,0:T(8,128)(2,1)S(1)}, bf16[16,1024]{1,0:T(8,128)(2,1)S(1)}, u32[]{:S(2)}, u32[]{:S(2)}) collective-permute-start(bf16[16,1024]{1,0:T(8,128)(2,1)S(1)} %get-tuple-element.194), channel_id=1, source_target_pairs={{0,12},{4,0},{8,4},{12,8},{1,13},{5,1},{9,5},{13,9},{2,14},{6,2},{... | collective-permute-start | bytes 98312 | tf_op jit(solution)/shard_map/ppermute | solution.py:353
  (15 other events, 84.2 us)

commit v2 on v1

--- a/solution.py
+++ b/solution.py
@@ -134,7 +134,7 @@
 
 def product_one(queue, cov, blocks, acc, row_of, count, add=None, coded=False):
     hi, lo = cov
-    n, width = blocks[0][0].shape
+    n, width = blocks[0][0][0].shape
     whole = count * n == hi.shape[0]
     terms = len(blocks)
     tall = n
@@ -143,8 +143,8 @@
 
     def body(m, *refs):
         refs = list(refs)
-        his, los, codes = refs[:terms], refs[terms : 2 * terms], refs[2 * terms : 3 * terms]
-        refs = refs[3 * terms :]
+        his, los, refs = refs[:terms], refs[terms : 2 * terms], refs[2 * terms :]
+        codes = [[refs.pop(0) for _ in got] for got, _ in blocks]
         acc_ref = refs.pop(0) if acc is not None else None
         add_ref = refs.pop(0) if add is not None else None
         out, p_hi, p_lo = refs
@@ -152,7 +152,8 @@
         @pl.when(pl.program_id(0) == 0)
         def _():
             for t in range(terms):
-                p_hi[t], p_lo[t] = halves(decode(codes[t][...], SCALE_P))
+                code = sum(ref[...].astype(F32) for ref in codes[t])
+                p_hi[t], p_lo[t] = halves(decode(code, SCALE_P))
 
         got = None
         for t in range(terms):
@@ -168,8 +169,9 @@
     specs = [
         pl.BlockSpec((tall, n), lambda i, m, at=at: (row_of(i, m), m[at])) for _, at in blocks
     ]
-    ins = specs + specs + [pl.BlockSpec((n, width), lambda i, m: (0, 0))] * terms
-    args = [hi] * terms + [lo] * terms + [code for code, _ in blocks]
+    codes = [code for got, _ in blocks for code in got]
+    ins = specs + specs + [pl.BlockSpec((n, width), lambda i, m: (0, 0))] * len(codes)
+    args = [hi] * terms + [lo] * terms + codes
     alias = None
     if acc is not None:
         if whole:
@@ -192,32 +194,34 @@
     )
 
 
-def finish_grad(queue, part, codes, mirrored_a, k, step):
+def finish_grad(queue, part, codes, mirrored_a, step):
     n, width = part.shape
     tile = min(n, 128)
-    count = len(codes)
-
-    def body(m, part, a, *rest):
+    count, pieces = len(codes), len(mirrored_a)
+
+    def body(m, part, *rest):
         grad = part[...]
         for ref in rest[:count]:
             grad = grad + decode(ref[...], SCALE_G)
-        grad_code, a_code = rest[count:]
+        grad_code, a_code = rest[count + pieces :]
         grad_code[...] = encode(grad, SCALE_G)
-        a_new = a[...].astype(F32) + step * grad
+        a_new = step * grad
+        for ref in rest[count : count + pieces]:
+            a_new = a_new + ref[...].astype(F32)
         a_code[...] = encode(a_new.T, SCALE_A)
 
     spec = pl.BlockSpec((tile, width), lambda i, m: (i, 0))
     return queue.call(
         body,
         (n // tile,),
-        [spec, pl.BlockSpec((tile, width), lambda i, m: (i, k))] + [spec] * count,
+        [spec] * (1 + count + pieces),
         [spec, pl.BlockSpec((width, tile), lambda i, m: (0, i))],
         [shape((n, width), BF16), shape((width, n), BF16)],
-        [part, mirrored_a, *codes],
-    )
-
-
-def product_two(queue, cov, blocks, acc, col_of, count, coded=False):
+        [part, *codes, *mirrored_a],
+    )
+
+
+def product_two(queue, cov, blocks, acc, col_of, count, coded=False, add=None):
     hi, lo = cov
     width, n = blocks[0][0].shape
     whole = count * n == hi.shape[1]
@@ -228,6 +232,7 @@
         his, los, codes = refs[:terms], refs[terms : 2 * terms], refs[2 * terms : 3 * terms]
         refs = refs[3 * terms :]
         acc_ref = refs.pop(0) if acc is not None else None
+        add_ref = refs.pop(0) if add is not None else None
         out, parts = refs
 
         @pl.when(pl.program_id(0) == 0)
@@ -243,6 +248,8 @@
             got = part if got is None else got + part
         if acc is not None:
             got = got + acc_ref[...]
+        if add is not None:
+            got = got + decode(add_ref[...], SCALE_F)
         out[...] = encode(got, SCALE_F) if coded else got
 
     specs = [
@@ -256,6 +263,9 @@
             alias = {1 + len(args): 0}
         ins.append(pl.BlockSpec((width, n), lambda i, m: (0, col_of(i, m))))
         args.append(acc)
+    if add is not None:
+        ins.append(pl.BlockSpec((width, n), lambda i, m: (0, i)))
+        args.append(add)
     return queue.call(
         body,
         (count,),
@@ -269,13 +279,18 @@
     )
 
 
-def second_diff(queue, grad_code, w, a, b, k, step):
-    n, rank = grad_code.shape
+def second_diff(queue, grad_codes, w, a, b, k, step):
+    n, rank = grad_codes[0].shape
     features = b.shape[2]
     tile = min(n, 256)
-
-    def body(m, grad_code, w, a, b, new_a, diff):
-        a_new = a[...].astype(F32) + step * decode(grad_code[...], SCALE_G)
+    pieces = len(grad_codes)
+
+    def body(m, w, a, b, *rest):
+        new_a, diff = rest[pieces:]
+        code = rest[0][...].astype(F32)
+        for ref in rest[1:pieces]:
+            code = code + ref[...].astype(F32)
+        a_new = a[...].astype(F32) + step * decode(code, SCALE_G)
         new_a[...] = a_new
         high, low = halves(a_new)
         value = mm(high, b[0]) + mm(low, b[0])
@@ -286,14 +301,14 @@
         body,
         (n // tile,),
         [
-            narrow,
             pl.BlockSpec((tile, features), lambda i, m: (i, k)),
             pl.BlockSpec((tile, rank), lambda i, m: (i, k)),
             pl.BlockSpec((1, rank, features), lambda i, m: (k, 0, 0)),
-        ],
+        ]
+        + [narrow] * pieces,
         [narrow, pl.BlockSpec((tile, features), lambda i, m: (i, 0))],
         [shape((n, rank), F32), shape((n, features), BF16)],
-        [grad_code, w, a, b],
+        [w, a, b, *grad_codes],
         flops=4 * n * rank * features,
     )
 
@@ -350,24 +365,24 @@
         return lax.ppermute(x, "col", pairs)
 
     def shift_row(x, s):
-        return lax.ppermute(x, "row", [(i, (i + s) % side) for i in range(side)])
+        return lax.ppermute(x, "row", [(i, i ^ s) for i in range(side)])
 
     def mirror(x):
         pairs = [(i * side + j, j * side + i) for i in range(side) for j in range(side)]
-        return lax.ppermute(x, ("row", "col"), pairs)
+        return [lax.ppermute(x, ("row", "col"), pairs)]
 
     def pick(x, i, axis=0):
         return lax.dynamic_index_in_dim(x, i, axis, keepdims=False)
 
     hops, lanes = jnp.arange(side), jnp.arange(ys)
     meta = jnp.concatenate(
-        [(row - hops) % side, (row + hops) % side, (y - lanes) % ys, (y + lanes) % ys, core[None]]
+        [row ^ hops, row ^ hops, (y - lanes) % ys, (y + lanes) % ys, core[None]]
     ).astype(jnp.int32)
     from_row, to_row = 0, side
     from_y, to_y = 2 * side, 2 * side + ys
     core_at = 2 * side + 2 * ys
     here = [core, 1 - core, y, row]
-    here += [(y + t) % ys for t in range(1, ys)] + [(row + t) % side for t in range(1, side)]
+    here += [(y + t) % ys for t in range(1, ys)] + [row ^ t for t in range(1, side)]
     here = [i.astype(jnp.uint32) for i in here]
     a = factor_a.reshape(n, width)
     w = weight.reshape(n, projections * features)
@@ -377,10 +392,8 @@
     queue = Queue(meta)
 
     z = jnp.stack([factor_b] + [shift_row(factor_b, s) for s in range(1, side)])
-    mirrored_a = mirror(factor_a)
     zy = jnp.stack([z] + [shift_y(z, s) for s in range(1, ys)])
-    cov = split_cov(queue, covariance)
-    cov = [pltpu.with_memory_space_constraint(x, pltpu.VMEM) for x in cov]
+    mirrored_a = [mirror(a[:, k * rank : (k + 1) * rank]) for k in range(projections)]
     zyc = swap_core(zy)
     if share % 16 == 0:
         b = place_b(queue, zy, zyc, from_row, from_y, core_at)
@@ -391,11 +404,21 @@
         b = both.transpose(3, 2, 1, 0, 4, 5).reshape(projections, rank, features)
 
     ks = range(projections)
+    relay = side == 4
+    ends_in, ends_out, middle = [(0, 1), (3, 2)], [(1, 0), (2, 3)], [(1, 2), (2, 1)]
+
+    def spread(code):
+        got = [[code]] + [[shift_row(code, s)] for s in range(1, side)]
+        if relay:
+            got[3] = [lax.ppermute(code, "row", middle), lax.ppermute(got[2][0], "row", ends_out)]
+        return got
+
     panels = []
     for k in ks:
         code = project(queue, w, a, b, k)
-        panels.append([code] + [shift_row(code, s) for s in range(1, side)])
-    mirrored_a = mirrored_a.reshape(n, width)
+        panels.append(spread(code))
+    cov = split_cov(queue, covariance)
+    cov = [pltpu.with_memory_space_constraint(x, pltpu.VMEM) for x in cov]
     late = 2
 
     def early_one(k, acc, s):
@@ -419,66 +442,108 @@
         return near, far
 
     def start_two(k, near, far):
-        grad_code, a_code = finish_grad(queue, near, far, mirrored_a, k, step_a)
+        grad_code, a_code = finish_grad(queue, near, far, mirrored_a[k], step_a)
         codes = [a_code] + [shift_y(a_code, s) for s in range(1, ys)]
         others = [swap_core(x) for x in codes]
-        back = mirror(grad_code)
         blocks = []
         for s in range(ys):
             blocks.append((codes[s], lambda m, s=s: m[from_y + s] * CORES + m[core_at]))
             blocks.append((others[s], lambda m, s=s: m[from_y + s] * CORES + 1 - m[core_at]))
+        return blocks, mirror(grad_code)
+
+    def early_two(blocks):
         acc = None
         for block in blocks[:-late]:
             acc = product_two(queue, cov, [block], acc, lambda i, m: i, side)
-        return acc, blocks[-late:], back
-
-    def pieces_two(acc, blocks):
-        landed = []
-        for hop in range(1, side):
+        return acc, blocks[-late:]
+
+    def away_two(acc, blocks, between):
+        landed, passed = [], None
+        for hop in away_order(side):
             piece = product_two(
-                queue, cov, blocks, acc, lambda i, m, hop=hop: m[to_row + hop], 1, coded=True
+                queue,
+                cov,
+                blocks,
+                acc,
+                lambda i, m, hop=hop: m[to_row + hop],
+                1,
+                coded=True,
+                add=passed if relay and hop == 2 else None,
             )
-            landed.append(shift_row(piece, hop))
-        kept = product_two(queue, cov, blocks, acc, lambda i, m: m[to_row], 1)
-        return kept, landed
-
-    def finish_b(k, value):
+            if relay and hop == 3:
+                passed = lax.ppermute(piece, "row", ends_in)
+                landed.append(lax.ppermute(piece, "row", middle))
+            else:
+                landed.append(shift_row(piece, hop))
+            if between is not None:
+                between()
+                between = None
+        return landed
+
+    def kept_two(acc, blocks):
+        return product_two(queue, cov, blocks, acc, lambda i, m: m[to_row], 1)
+
+    def finish_b(value):
         value = value.reshape(side, ys, CORES, share, features)
         value = pick(value, own_core, 2) + swap_core(pick(value, other_core, 2))
         mine = pick(value, own_y, 1)
         for s in range(1, ys):
             away = encode(pick(value, next_y[s], 1), SCALE_V)
             mine = mine + decode(shift_y(away, s), SCALE_V)
-        total = pick(mine, own_row, 0)
+        return mine
+
+    def sum_rows(mine):
+        total = pick(mine, own_row, 1)
         for s in range(1, side):
-            away = encode(pick(mine, next_row[s], 0), SCALE_V)
+            away = encode(pick(mine, next_row[s], 1), SCALE_V)
             total = total + decode(shift_row(away, s), SCALE_V)
-        return factor_b[k].astype(F32) + step_b * total
-
-    accs = [None] * projections
+        return factor_b.astype(F32) + step_b * total
+
+    accs = [early_one(k, None, 0) for k in ks]
+    sums, seconds, fields, values = [], [], [], []
+
+    new_a, diffs = [], []
+
+    def finish_one(k):
+        blocks, back = start_two(k, *sums[k])
+        seconds.append([blocks, back])
+
+    def diff_two(k):
+        a_new, diff = second_diff(queue, seconds[k][1], w, a, b, k, step_a)
+        new_a.append(a_new)
+        diffs.append(diff)
+
+    def grad_two(k):
+        values.append(finish_b(second_grad(queue, kept[k], fields[k], diffs[k])))
+
+    last = projections - 1
     for k in ks:
-        accs[k] = early_one(k, None, 0)
-    sums, seconds, fields, diffs, new_a, new_b = ({} for _ in range(6))
-    for k in range(projections + 1):
-        if k < projections:
-            for s in range(1, side - late):
-                accs[k] = early_one(k, accs[k], s)
-            sums[k] = pieces_one(k, accs[k])
+        for s in range(1, side - late):
+            accs[k] = early_one(k, accs[k], s)
         if k > 0:
-            fields[k - 1] = pieces_two(*seconds[k - 1][:2])
-        if k > 1:
-            value = second_grad(queue, fields[k - 2][0], fields[k - 2][1], diffs[k - 2])
-            new_b[k - 2] = finish_b(k - 2, value)
+            finish_one(k - 1)
+            seconds[k - 1][0] = early_two(seconds[k - 1][0])
+        sums.append(pieces_one(k, accs[k]))
         if k > 0:
-            new_a[k - 1], diffs[k - 1] = second_diff(
-                queue, seconds[k - 1][2], w, a, b, k - 1, step_a
-            )
-        if k < projections:
-            seconds[k] = start_two(k, *sums[k])
-    last = projections - 1
-    value = second_grad(queue, fields[last][0], fields[last][1], diffs[last])
-    new_b[last] = finish_b(last, value)
-    return jnp.stack([new_a[k] for k in ks], 1), jnp.stack([new_b[k] for k in ks], 0)
+            after = (lambda: finish_one(last)) if k == last else None
+            fields.append(away_two(*seconds[k - 1][0], after))
+    if last == 0:
+        finish_one(last)
+    seconds[last][0] = early_two(seconds[last][0])
+    fields.append(away_two(*seconds[last][0], None))
+    kept = [kept_two(*seconds[k][0]) for k in reversed(ks)][::-1]
+    for k in range(last):
+        diff_two(k)
+        grad_two(k)
+    diff_two(last)
+    new_a = jnp.stack(new_a, 1)
+    queue.meta, new_a = lax.optimization_barrier((queue.meta, new_a))
+    grad_two(last)
+    return new_a, sum_rows(jnp.stack(values, 0))
+
+
+def away_order(side):
+    return (3, 1, 2) if side == 4 else tuple(range(1, side))
 
 
 def solution(mesh):

time: 240 us -> 232 us (0.967)
  starting transfers between devices: 73.7 us -> 66.3 us
    ppermute x7, starting transfers between devices: 21.8 us -> 13.7 us  [shift_y(): return lax.ppermute(x, 'col', pairs)]
    ppermute x24 -> x26, starting transfers between devices: 43.3 us -> 51.1 us  [the longest x14 37.8 us: shift_row(): return lax.ppermute(x, 'row', [(i, i ^ s) for i in range(side)])]
    ppermute x11, starting transfers between devices: 8.61 us -> 1.55 us  [swap_core(): return lax.ppermute(x, 'col', [(i, i ^ 1) for i in range(ys * CORES)])]
    ppermute x24 -> x26, waiting for transfers between devices: 49.1 us -> 44.7 us  [the longest x14 40.5 us: shift_row(): return lax.ppermute(x, 'row', [(i, i ^ s) for i in range(side)])]
  transfers between devices with their start and end apart: 42 -> 44, of which waited for: 14 -> 17; matrix products, arithmetic and copies ran while one was open for 2% -> 2% of each run, Pallas kernels for 29% -> 31%
where the time goes in v2:
time: 232 us
  Pallas kernels  80.6 us (35%)
  waiting for transfers between devices  76.6 us (33%)
  starting transfers between devices  66.3 us (29%)
  local copies, waits for them, and re-layouts  4.55 us (2%)
  other arithmetic  2.33 us (1%)
    pallas_call x34, Pallas kernels, call(): pl.pallas_call(body, out_shape=shapes, grid_spec=spec, input_output_alias...  80.6 us
    ppermute x14, waiting for transfers between devices, shift_row(): return lax.ppermute(x, 'row', [(i, i ^ s) for i in range(side)])  40.5 us
    ppermute x14, starting transfers between devices, shift_row(): return lax.ppermute(x, 'row', [(i, i ^ s) for i in range(side)])  37.8 us
    ppermute x7, waiting for transfers between devices, shift_y(): return lax.ppermute(x, 'col', pairs)  30.1 us
    ppermute x7, starting transfers between devices, shift_y(): return lax.ppermute(x, 'col', pairs)  13.7 us
    ppermute x2, starting transfers between devices, away_two(): passed = lax.ppermute(piece, 'row', ends_in)  4.81 us
  transfers between devices with their start and end apart: 44, of which 17 were waited for; matrix products, arithmetic and copies ran while one was open for 2% of the time, Pallas kernels for 31%

profile of v2, /device:TPU:0, one launch (start us, length us, event | category | flops | bytes accessed | tf_op | source)
XLA Modules:
  0.0 231.7 jit_solution(10146413636218508070)
XLA Ops:
  0.6 3.1 %collective-permute-start = (bf16[2,16,1024]{2,1,0:T(8,128)(2,1)}, bf16[2,16,1024]{2,1,0:T(8,128)(2,1)S(1)}, u32[]{:S(2)}, u32[]{:S(2)}) collective-permute-start(bf16[2,16,1024]{2,1,0:T(8,128)(2,1)} %param.7), channel_id=1, source_target_pairs={{0,4},{4,0},{8,12},{12,8},{1,5},{5,1},{9,13},{13,9},{2,6},{6,2},{1... | collective-permute-start | bytes 196616 | tf_op jit(solution)/shard_map/ppermute | solution.py:368
  3.7 2.6 %collective-permute-start.1 = (bf16[2,16,1024]{2,1,0:T(8,128)(2,1)}, bf16[2,16,1024]{2,1,0:T(8,128)(2,1)S(1)}, u32[]{:S(2)}, u32[]{:S(2)}) collective-permute-start(bf16[2,16,1024]{2,1,0:T(8,128)(2,1)} %param.7), channel_id=1, source_target_pairs={{0,8},{4,12},{8,0},{12,4},{1,9},{5,13},{9,1},{13,5},{2,10},{6,14},... | collective-permute-start | bytes 196616 | tf_op jit(solution)/shard_map/ppermute | solution.py:368
  6.3 4.9 %collective-permute-done.1 = bf16[2,16,1024]{2,1,0:T(8,128)(2,1)S(1)} collective-permute-done((bf16[2,16,1024]{2,1,0:T(8,128)(2,1)}, bf16[2,16,1024]{2,1,0:T(8,128)(2,1)S(1)}, u32[]{:S(2)}, u32[]{:S(2)}) %collective-permute-start.1) | collective-permute-done | bytes 65568 | tf_op jit(solution)/shard_map/ppermute | solution.py:368
  15.1 4.9 %collective-permute-done.3 = bf16[4,2,16,1024]{3,2,1,0:T(8,128)(2,1)S(1)} collective-permute-done((bf16[4,2,16,1024]{3,2,1,0:T(8,128)(2,1)S(1)}, bf16[4,2,16,1024]{3,2,1,0:T(8,128)(2,1)S(1)}, u32[]{:S(2)}, u32[]{:S(2)}) %collective-permute-start.3) | collective-permute-done | bytes 262176 | tf_op jit(solution)/shard_map/ppermute | solution.py:365
  20.2 2.2 copy.17
  22.6 2.5 %shard_map.59.b = bf16[2,256,1024]{2,1,0:T(8,128)(2,1)S(1)} custom-call(s32[13]{0:T(128)S(1)} %concatenate.3.m, bf16[2,4,2,16,1024]{4,3,2,1,0:T(8,128)(2,1)S(1)} %pad_maximum_fusion.1.own, bf16[2,4,2,16,1024]{4,3,2,1,0:T(8,128)(2,1)} %collective-permute-done.4.other), custom_call_target="tpu_custom_call" | custom-call | bytes 2097152 | tf_op jit(solution)/shard_map/pallas_call | solution.py:54
  31.9 9.2 %shard_map.62 = (bf16[2048,2048]{1,0:T(8,128)(2,1)S(1)}, bf16[2048,2048]{1,0:T(8,128)(2,1)S(1)}) custom-call(s32[13]{0:T(128)S(1)} %concatenate.3.m, f32[2048,2048]{1,0:T(8,128)} %c.1), custom_call_target="tpu_custom_call" | custom-call | bytes 33554432 | tf_op jit(solution)/shard_map/pallas_call | solution.py:54
  41.1 3.1 %shard_map.63.refs_3_ = f32[2048,256]{1,0:T(8,128)S(1)} custom-call(s32[13]{0:T(128)S(1)} %concatenate.3.m, bf16[2048,2048]{1,0:T(8,128)(2,1)S(1)} %get-tuple-element.107.refs_0_.refs_1_, bf16[2048,2048]{1,0:T(8,128)(2,1)S(1)} %get-tuple-element.108.refs_1_.refs_2_.refs_3_, bf16[512,256]{1,0:T(8,128)(2,1)S(1)} %shard_map.60.refs_2_), custom_call_target="tpu_custom_call" | custom-call | flops 1610612736 | bytes 19136512 | tf_op jit(solution)/shard_map/pallas_call | solution.py:54
  45.5 3.1 %shard_map.64.refs_3_ = f32[2048,256]{1,0:T(8,128)S(1)} custom-call(s32[13]{0:T(128)S(1)} %concatenate.3.m, bf16[2048,2048]{1,0:T(8,128)(2,1)S(1)} %get-tuple-element.107.refs_0_.refs_1_, bf16[2048,2048]{1,0:T(8,128)(2,1)S(1)} %get-tuple-element.108.refs_1_.refs_2_.refs_3_, bf16[512,256]{1,0:T(8,128)(2,1)S(1)} %shard_map.61.refs_2_), custom_call_target="tpu_custom_call" | custom-call | flops 1610612736 | bytes 19136512 | tf_op jit(solution)/shard_map/pallas_call | solution.py:54
  48.6 3.3 %shard_map.65.refs_7_ = f32[2048,256]{1,0:T(8,128)S(1)} custom-call(s32[13]{0:T(128)S(1)} %concatenate.3.m, bf16[2048,2048]{1,0:T(8,128)(2,1)S(1)} %get-tuple-element.107.refs_0_.refs_1_, bf16[2048,2048]{1,0:T(8,128)(2,1)S(1)} %get-tuple-element.108.refs_1_.refs_2_.refs_3_, ...), custom_call_target="tpu_custom_call", output_to_operand_aliasing={{}: (4, {})} | custom-call | flops 1610612736 | bytes 21233664 | tf_op jit(solution)/shard_map/pallas_call | solution.py:54
  51.9 3.0 %collective-permute-done.8.refs_6_ = bf16[512,256]{1,0:T(8,128)(2,1)S(1)} collective-permute-done((bf16[512,256]{1,0:T(8,128)(2,1)S(1)}, bf16[512,256]{1,0:T(8,128)(2,1)S(1)}, u32[]{:S(2)}, u32[]{:S(2)}) %collective-permute-start.8) | collective-permute-done | bytes 262176 | tf_op jit(solution)/shard_map/ppermute | solution.py:413
  62.2 5.7 %collective-permute-start.12 = (bf16[512,256]{1,0:T(8,128)(2,1)S(1)}, bf16[512,256]{1,0:T(8,128)(2,1)S(1)}, u32[]{:S(2)}, u32[]{:S(2)}) collective-permute-start(bf16[512,256]{1,0:T(8,128)(2,1)S(1)} %shard_map.68), channel_id=1, source_target_pairs={{0,2},{1,3},{2,0},{3,1},{4,6},{5,7},{6,4},{7,5},{8,10},{9,11},{10,... | collective-permute-start | bytes 786440 | tf_op jit(solution)/shard_map/ppermute | solution.py:365
  69.7 3.3 %shard_map.70.refs_7_ = f32[2048,256]{1,0:T(8,128)S(1)} custom-call(s32[13]{0:T(128)S(1)} %concatenate.3.m, bf16[2048,2048]{1,0:T(8,128)(2,1)S(1)} %get-tuple-element.107.refs_0_.refs_1_, bf16[2048,2048]{1,0:T(8,128)(2,1)S(1)} %get-tuple-element.108.refs_1_.refs_2_.refs_3_, ...), custom_call_target="tpu_custom_call", output_to_operand_aliasing={{}: (4, {})} | custom-call | flops 1610612736 | bytes 21233664 | tf_op jit(solution)/shard_map/pallas_call | solution.py:54
  73.0 3.5 %collective-permute-done.12.rest_0_ = bf16[512,256]{1,0:T(8,128)(2,1)S(1)} collective-permute-done((bf16[512,256]{1,0:T(8,128)(2,1)S(1)}, bf16[512,256]{1,0:T(8,128)(2,1)S(1)}, u32[]{:S(2)}, u32[]{:S(2)}) %collective-permute-start.12) | collective-permute-done | bytes 262176 | tf_op jit(solution)/shard_map/ppermute | solution.py:365
  78.5 10.5 %collective-permute-done.15.refs_4_ = bf16[512,256]{1,0:T(8,128)(2,1)S(1)} collective-permute-done((bf16[512,256]{1,0:T(8,128)(2,1)S(1)}, bf16[512,256]{1,0:T(8,128)(2,1)S(1)}, u32[]{:S(2)}, u32[]{:S(2)}) %collective-permute-start.15) | collective-permute-done | bytes 262176 | tf_op jit(solution)/shard_map/ppermute | solution.py:368
  90.3 3.6 %shard_map.72.refs_3_ = f32[256,2048]{1,0:T(8,128)S(1)} custom-call(s32[13]{0:T(128)S(1)} %concatenate.3.m, bf16[2048,2048]{1,0:T(8,128)(2,1)S(1)} %get-tuple-element.107.refs_0_.refs_1_, bf16[2048,2048]{1,0:T(8,128)(2,1)S(1)} %get-tuple-element.108.refs_1_.refs_2_.refs_3_, bf16[256,512]{1,0:T(8,128)(2,1)S(1)} %get-tuple-element.129.refs_2_), custom_call_target="tpu_custom_call" | custom-call | flops 1610612736 | bytes 19136512 | tf_op jit(solution)/shard_map/pallas_call | solution.py:54
  93.9 3.8 %shard_map.73.refs_6_ = f32[256,2048]{1,0:T(8,128)S(1)} custom-call(s32[13]{0:T(128)S(1)} %concatenate.3.m, bf16[2048,2048]{1,0:T(8,128)(2,1)S(1)} %get-tuple-element.107.refs_0_.refs_1_, bf16[2048,2048]{1,0:T(8,128)(2,1)S(1)} %get-tuple-element.108.refs_1_.refs_2_.refs_3_, ...), custom_call_target="tpu_custom_call", output_to_operand_aliasing={{}: (4, {})} | custom-call | flops 1610612736 | bytes 21233664 | tf_op jit(solution)/shard_map/pallas_call | solution.py:54
  103.2 8.3 %collective-permute-done.20.refs_4_ = bf16[256,512]{1,0:T(8,128)(2,1)S(1)} collective-permute-done((bf16[256,512]{1,0:T(8,128)(2,1)S(1)}, bf16[256,512]{1,0:T(8,128)(2,1)S(1)}, u32[]{:S(2)}, u32[]{:S(2)}) %collective-permute-start.20) | collective-permute-done | bytes 262176 | tf_op jit(solution)/shard_map/ppermute | solution.py:365
  114.0 3.3 %collective-permute-start.22 = (bf16[512,256]{1,0:T(8,128)(2,1)S(1)}, bf16[512,256]{1,0:T(8,128)(2,1)S(1)}, u32[]{:S(2)}, u32[]{:S(2)}) collective-permute-start(bf16[512,256]{1,0:T(8,128)(2,1)S(1)} %shard_map.76), channel_id=1, source_target_pairs={{0,2},{1,3},{2,0},{3,1},{4,6},{5,7},{6,4},{7,5},{8,10},{9,11},{10,... | collective-permute-start | bytes 786440 | tf_op jit(solution)/shard_map/ppermute | solution.py:365
  120.8 2.8 %collective-permute-start.24 = (bf16[256,512]{1,0:T(8,128)(2,1)S(1)}, bf16[256,512]{1,0:T(8,128)(2,1)S(1)}, u32[]{:S(2)}, u32[]{:S(2)}) collective-permute-start(bf16[256,512]{1,0:T(8,128)(2,1)S(1)} %shard_map.78), channel_id=1, source_target_pairs={{0,4},{12,8},{1,5},{13,9},{2,6},{14,10},{3,7},{15,11},{16,20},{28,... | collective-permute-start | bytes 786440 | tf_op jit(solution)/shard_map/ppermute | solution.py:474
  123.7 4.6 %collective-permute-done.22.rest_0_ = bf16[512,256]{1,0:T(8,128)(2,1)S(1)} collective-permute-done((bf16[512,256]{1,0:T(8,128)(2,1)S(1)}, bf16[512,256]{1,0:T(8,128)(2,1)S(1)}, u32[]{:S(2)}, u32[]{:S(2)}) %collective-permute-start.22) | collective-permute-done | bytes 262176 | tf_op jit(solution)/shard_map/ppermute | solution.py:365
  129.5 2.5 %collective-permute-start.26 = (bf16[256,512]{1,0:T(8,128)(2,1)S(1)}, bf16[256,512]{1,0:T(8,128)(2,1)S(1)}, u32[]{:S(2)}, u32[]{:S(2)}) collective-permute-start(bf16[256,512]{1,0:T(8,128)(2,1)S(1)} %get-tuple-element.150.refs_2_), channel_id=1, source_target_pairs={{0,2},{1,3},{2,0},{3,1},{4,6},{5,7},{6,4},{7,5},{8,10},{9,11},{10,... | collective-permute-start | bytes 786440 | tf_op jit(solution)/shard_map/ppermute | solution.py:365
  135.4 2.5 %collective-permute-done.26.refs_4_ = bf16[256,512]{1,0:T(8,128)(2,1)S(1)} collective-permute-done((bf16[256,512]{1,0:T(8,128)(2,1)S(1)}, bf16[256,512]{1,0:T(8,128)(2,1)S(1)}, u32[]{:S(2)}, u32[]{:S(2)}) %collective-permute-start.26) | collective-permute-done | bytes 262176 | tf_op jit(solution)/shard_map/ppermute | solution.py:365
  137.9 3.6 %shard_map.82.refs_3_ = f32[256,2048]{1,0:T(8,128)S(1)} custom-call(s32[13]{0:T(128)S(1)} %concatenate.3.m, bf16[2048,2048]{1,0:T(8,128)(2,1)S(1)} %get-tuple-element.107.refs_0_.refs_1_, bf16[2048,2048]{1,0:T(8,128)(2,1)S(1)} %get-tuple-element.108.refs_1_.refs_2_.refs_3_, bf16[256,512]{1,0:T(8,128)(2,1)S(1)} %get-tuple-element.150.refs_2_), custom_call_target="tpu_custom_call" | custom-call | flops 1610612736 | bytes 19136512 | tf_op jit(solution)/shard_map/pallas_call | solution.py:54
  141.5 3.8 %shard_map.83.refs_6_ = f32[256,2048]{1,0:T(8,128)S(1)} custom-call(s32[13]{0:T(128)S(1)} %concatenate.3.m, bf16[2048,2048]{1,0:T(8,128)(2,1)S(1)} %get-tuple-element.107.refs_0_.refs_1_, bf16[2048,2048]{1,0:T(8,128)(2,1)S(1)} %get-tuple-element.108.refs_1_.refs_2_.refs_3_, ...), custom_call_target="tpu_custom_call", output_to_operand_aliasing={{}: (4, {})} | custom-call | flops 1610612736 | bytes 21233664 | tf_op jit(solution)/shard_map/pallas_call | solution.py:54
  150.3 6.6 %collective-permute-start.32 = (bf16[256,512]{1,0:T(8,128)(2,1)S(1)}, bf16[256,512]{1,0:T(8,128)(2,1)S(1)}, u32[]{:S(2)}, u32[]{:S(2)}) collective-permute-start(bf16[256,512]{1,0:T(8,128)(2,1)S(1)} %shard_map.81), channel_id=1, source_target_pairs={{0,8},{4,12},{8,0},{12,4},{1,9},{5,13},{9,1},{13,5},{2,10},{6,14},... | collective-permute-start | bytes 786440 | tf_op jit(solution)/shard_map/ppermute | solution.py:368
  167.4 17.7 %collective-permute-start.37 = (bf16[256,512]{1,0:T(8,128)(2,1)S(1)}, bf16[256,512]{1,0:T(8,128)(2,1)S(1)}, u32[]{:S(2)}, u32[]{:S(2)}) collective-permute-start(bf16[256,512]{1,0:T(8,128)(2,1)S(1)} %shard_map.85), channel_id=1, source_target_pairs={{0,4},{4,0},{8,12},{12,8},{1,5},{5,1},{9,13},{13,9},{2,6},{6,2},{1... | collective-permute-start | bytes 786440 | tf_op jit(solution)/shard_map/ppermute | solution.py:368
  185.1 10.7 %collective-permute-done.32.rest_2_ = bf16[256,512]{1,0:T(8,128)(2,1)S(1)} collective-permute-done((bf16[256,512]{1,0:T(8,128)(2,1)S(1)}, bf16[256,512]{1,0:T(8,128)(2,1)S(1)}, u32[]{:S(2)}, u32[]{:S(2)}) %collective-permute-start.32) | collective-permute-done | bytes 262176 | tf_op jit(solution)/shard_map/ppermute | solution.py:368
  200.1 10.2 %collective-permute-done.38.rest_2_ = bf16[256,512]{1,0:T(8,128)(2,1)S(1)} collective-permute-done((bf16[256,512]{1,0:T(8,128)(2,1)S(1)}, bf16[256,512]{1,0:T(8,128)(2,1)S(1)}, u32[]{:S(2)}, u32[]{:S(2)}) %collective-permute-start.38) | collective-permute-done | bytes 262176 | tf_op jit(solution)/shard_map/ppermute | solution.py:368
  215.2 4.1 %collective-permute-done.35 = bf16[4,16,1024]{2,1,0:T(8,128)(2,1)S(1)} collective-permute-done((bf16[4,16,1024]{2,1,0:T(8,128)(2,1)S(1)}, bf16[4,16,1024]{2,1,0:T(8,128)(2,1)S(1)}, u32[]{:S(2)}, u32[]{:S(2)}) %collective-permute-start.35) | collective-permute-done | bytes 131104 | tf_op jit(solution)/shard_map/ppermute | solution.py:365
  219.4 2.2 collective-permute-done.40
  221.9 2.9 %collective-permute-start.42 = (bf16[2,16,1024]{2,1,0:T(8,128)(2,1)S(1)}, bf16[2,16,1024]{2,1,0:T(8,128)(2,1)S(1)}, u32[]{:S(2)}, u32[]{:S(2)}) collective-permute-start(bf16[2,16,1024]{2,1,0:T(8,128)(2,1)S(1)} %get-tuple-element.200), channel_id=1, source_target_pairs={{0,8},{4,12},{8,0},{12,4},{1,9},{5,13},{9,1},{13,5},{2,10},{6,14},... | collective-permute-start | bytes 196616 | tf_op jit(solution)/shard_map/ppermute | solution.py:368
  (120 shorter events, 72.1 us)
Async XLA Ops:
  27.0 17.2 %collective-permute-start.6 = (bf16[512,256]{1,0:T(8,128)(2,1)S(1)}, bf16[512,256]{1,0:T(8,128)(2,1)S(1)}, u32[]{:S(2)}, u32[]{:S(2)}) collective-permute-start(bf16[512,256]{1,0:T(8,128)(2,1)S(1)} %shard_map.60.refs_2_), channel_id=1, source_target_pairs={{0,8},{4,12},{8,0},{12,4},{1,9},{5,13},{9,1},{13,5},{2,10},{6,14},... | collective-permute-start | bytes 786440 | tf_op jit(solution)/shard_map/ppermute | solution.py:368
  29.2 19.5 %collective-permute-start.5 = (bf16[512,256]{1,0:T(8,128)(2,1)S(1)}, bf16[512,256]{1,0:T(8,128)(2,1)S(1)}, u32[]{:S(2)}, u32[]{:S(2)}) collective-permute-start(bf16[512,256]{1,0:T(8,128)(2,1)S(1)} %shard_map.60.refs_2_), channel_id=1, source_target_pairs={{0,4},{4,0},{8,12},{12,8},{1,5},{5,1},{9,13},{13,9},{2,6},{6,2},{1... | collective-permute-start | bytes 786440 | tf_op jit(solution)/shard_map/ppermute | solution.py:368
  29.4 22.5 %collective-permute-start.7 = (bf16[512,256]{1,0:T(8,128)(2,1)S(1)}, bf16[512,256]{1,0:T(8,128)(2,1)S(1)}, u32[]{:S(2)}, u32[]{:S(2)}) collective-permute-start(bf16[512,256]{1,0:T(8,128)(2,1)S(1)} %shard_map.60.refs_2_), channel_id=1, source_target_pairs={{4,8},{8,4},{5,9},{9,5},{6,10},{10,6},{7,11},{11,7},{20,24},{24,20... | collective-permute-start | bytes 786440 | tf_op jit(solution)/shard_map/ppermute | solution.py:413
  44.2 10.7 %collective-permute-start.8 = (bf16[512,256]{1,0:T(8,128)(2,1)S(1)}, bf16[512,256]{1,0:T(8,128)(2,1)S(1)}, u32[]{:S(2)}, u32[]{:S(2)}) collective-permute-start(bf16[512,256]{1,0:T(8,128)(2,1)S(1)} %collective-permute-done.6.refs_4_), channel_id=1, source_target_pairs={{4,0},{8,12},{5,1},{9,13},{6,2},{10,14},{7,3},{11,15},{20,16},{24,... | collective-permute-start | bytes 786440 | tf_op jit(solution)/shard_map/ppermute | solution.py:413
  58.6 9.3 %collective-permute-start.10 = (f32[512,256]{1,0:T(8,128)S(1)}, f32[512,256]{1,0:T(8,128)S(1)}, u32[]{:S(2)}, u32[]{:S(2)}) collective-permute-start(f32[512,256]{1,0:T(8,128)S(1)} %shard_map.67), channel_id=1, source_target_pairs={{0,1},{1,0},{2,3},{3,2},{4,5},{5,4},{6,7},{7,6},{8,9},{9,8},{10,11... | collective-permute-start | bytes 1572872 | tf_op jit(solution)/shard_map/ppermute | solution.py:361
  59.2 10.5 %collective-permute-start.11 = (bf16[512,256]{1,0:T(8,128)(2,1)S(1)}, bf16[512,256]{1,0:T(8,128)(2,1)S(1)}, u32[]{:S(2)}, u32[]{:S(2)}) collective-permute-start(bf16[512,256]{1,0:T(8,128)(2,1)S(1)} %shard_map.61.refs_2_), channel_id=1, source_target_pairs={{0,4},{4,0},{8,12},{12,8},{1,5},{5,1},{9,13},{13,9},{2,6},{6,2},{1... | collective-permute-start | bytes 786440 | tf_op jit(solution)/shard_map/ppermute | solution.py:368
  59.5 13.5 %collective-permute-start.13 = (bf16[512,256]{1,0:T(8,128)(2,1)S(1)}, bf16[512,256]{1,0:T(8,128)(2,1)S(1)}, u32[]{:S(2)}, u32[]{:S(2)}) collective-permute-start(bf16[512,256]{1,0:T(8,128)(2,1)S(1)} %get-tuple-element.202), channel_id=1, source_target_pairs={{0,0},{1,4},{2,8},{3,12},{4,1},{5,5},{6,9},{7,13},{8,2},{9,6},{10,... | collective-permute-start | bytes 786440 | tf_op jit(solution)/shard_map/ppermute | solution.py:372
  62.2 14.3 %collective-permute-start.12 = (bf16[512,256]{1,0:T(8,128)(2,1)S(1)}, bf16[512,256]{1,0:T(8,128)(2,1)S(1)}, u32[]{:S(2)}, u32[]{:S(2)}) collective-permute-start(bf16[512,256]{1,0:T(8,128)(2,1)S(1)} %shard_map.68), channel_id=1, source_target_pairs={{0,2},{1,3},{2,0},{3,1},{4,6},{5,7},{6,4},{7,5},{8,10},{9,11},{10,... | collective-permute-start | bytes 786440 | tf_op jit(solution)/shard_map/ppermute | solution.py:365
  67.9 21.1 %collective-permute-start.15 = (bf16[512,256]{1,0:T(8,128)(2,1)S(1)}, bf16[512,256]{1,0:T(8,128)(2,1)S(1)}, u32[]{:S(2)}, u32[]{:S(2)}) collective-permute-start(bf16[512,256]{1,0:T(8,128)(2,1)S(1)} %shard_map.61.refs_2_), channel_id=1, source_target_pairs={{0,8},{4,12},{8,0},{12,4},{1,9},{5,13},{9,1},{13,5},{2,10},{6,14},... | collective-permute-start | bytes 786440 | tf_op jit(solution)/shard_map/ppermute | solution.py:368
  77.8 16.2 %collective-permute-start.14 = (bf16[256,512]{1,0:T(8,128)(2,1)S(1)}, bf16[256,512]{1,0:T(8,128)(2,1)S(1)}, u32[]{:S(2)}, u32[]{:S(2)}) collective-permute-start(bf16[256,512]{1,0:T(8,128)(2,1)S(1)} %get-tuple-element.129.refs_2_), channel_id=1, source_target_pairs={{0,1},{1,0},{2,3},{3,2},{4,5},{5,4},{6,7},{7,6},{8,9},{9,8},{10,11... | collective-permute-start | bytes 786440 | tf_op jit(solution)/shard_map/ppermute | solution.py:361
  77.9 19.9 %collective-permute-start.16 = (bf16[512,256]{1,0:T(8,128)(2,1)S(1)}, bf16[512,256]{1,0:T(8,128)(2,1)S(1)}, u32[]{:S(2)}, u32[]{:S(2)}) collective-permute-start(bf16[512,256]{1,0:T(8,128)(2,1)S(1)} %shard_map.61.refs_2_), channel_id=1, source_target_pairs={{4,8},{8,4},{5,9},{9,5},{6,10},{10,6},{7,11},{11,7},{20,24},{24,20... | collective-permute-start | bytes 786440 | tf_op jit(solution)/shard_map/ppermute | solution.py:413
  89.0 9.9 %collective-permute-start.17 = (bf16[512,256]{1,0:T(8,128)(2,1)S(1)}, bf16[512,256]{1,0:T(8,128)(2,1)S(1)}, u32[]{:S(2)}, u32[]{:S(2)}) collective-permute-start(bf16[512,256]{1,0:T(8,128)(2,1)S(1)} %collective-permute-done.15.refs_4_), channel_id=1, source_target_pairs={{4,0},{8,12},{5,1},{9,13},{6,2},{10,14},{7,3},{11,15},{20,16},{24,... | collective-permute-start | bytes 786440 | tf_op jit(solution)/shard_map/ppermute | solution.py:413
  100.8 11.4 %collective-permute-start.18 = (f32[512,256]{1,0:T(8,128)S(1)}, f32[512,256]{1,0:T(8,128)S(1)}, u32[]{:S(2)}, u32[]{:S(2)}) collective-permute-start(f32[512,256]{1,0:T(8,128)S(1)} %shard_map.74), channel_id=1, source_target_pairs={{0,1},{1,0},{2,3},{3,2},{4,5},{5,4},{6,7},{7,6},{8,9},{9,8},{10,11... | collective-permute-start | bytes 1572872 | tf_op jit(solution)/shard_map/ppermute | solution.py:361
  102.7 14.7 %collective-permute-start.19 = (f32[512,256]{1,0:T(8,128)S(1)}, f32[512,256]{1,0:T(8,128)S(1)}, u32[]{:S(2)}, u32[]{:S(2)}) collective-permute-start(f32[512,256]{1,0:T(8,128)S(1)} %shard_map.75), channel_id=1, source_target_pairs={{0,1},{1,0},{2,3},{3,2},{4,5},{5,4},{6,7},{7,6},{8,9},{9,8},{10,11... | collective-permute-start | bytes 1572872 | tf_op jit(solution)/shard_map/ppermute | solution.py:361
  103.2 8.3 %collective-permute-start.20 = (bf16[256,512]{1,0:T(8,128)(2,1)S(1)}, bf16[256,512]{1,0:T(8,128)(2,1)S(1)}, u32[]{:S(2)}, u32[]{:S(2)}) collective-permute-start(bf16[256,512]{1,0:T(8,128)(2,1)S(1)} %get-tuple-element.129.refs_2_), channel_id=1, source_target_pairs={{0,2},{1,3},{2,0},{3,1},{4,6},{5,7},{6,4},{7,5},{8,10},{9,11},{10,... | collective-permute-start | bytes 786440 | tf_op jit(solution)/shard_map/ppermute | solution.py:365
  111.5 7.7 %collective-permute-start.21 = (bf16[256,512]{1,0:T(8,128)(2,1)S(1)}, bf16[256,512]{1,0:T(8,128)(2,1)S(1)}, u32[]{:S(2)}, u32[]{:S(2)}) collective-permute-start(bf16[256,512]{1,0:T(8,128)(2,1)S(1)} %collective-permute-done.20.refs_4_), channel_id=1, source_target_pairs={{0,1},{1,0},{2,3},{3,2},{4,5},{5,4},{6,7},{7,6},{8,9},{9,8},{10,11... | collective-permute-start | bytes 786440 | tf_op jit(solution)/shard_map/ppermute | solution.py:361
  111.5 12.2 %collective-permute-start.23 = (bf16[512,256]{1,0:T(8,128)(2,1)S(1)}, bf16[512,256]{1,0:T(8,128)(2,1)S(1)}, u32[]{:S(2)}, u32[]{:S(2)}) collective-permute-start(bf16[512,256]{1,0:T(8,128)(2,1)S(1)} %get-tuple-element.201), channel_id=1, source_target_pairs={{0,0},{1,4},{2,8},{3,12},{4,1},{5,5},{6,9},{7,13},{8,2},{9,6},{10,... | collective-permute-start | bytes 786440 | tf_op jit(solution)/shard_map/ppermute | solution.py:372
  114.0 14.2 %collective-permute-start.22 = (bf16[512,256]{1,0:T(8,128)(2,1)S(1)}, bf16[512,256]{1,0:T(8,128)(2,1)S(1)}, u32[]{:S(2)}, u32[]{:S(2)}) collective-permute-start(bf16[512,256]{1,0:T(8,128)(2,1)S(1)} %shard_map.76), channel_id=1, source_target_pairs={{0,2},{1,3},{2,0},{3,1},{4,6},{5,7},{6,4},{7,5},{8,10},{9,11},{10,... | collective-permute-start | bytes 786440 | tf_op jit(solution)/shard_map/ppermute | solution.py:365
  120.8 12.9 %collective-permute-start.24 = (bf16[256,512]{1,0:T(8,128)(2,1)S(1)}, bf16[256,512]{1,0:T(8,128)(2,1)S(1)}, u32[]{:S(2)}, u32[]{:S(2)}) collective-permute-start(bf16[256,512]{1,0:T(8,128)(2,1)S(1)} %shard_map.78), channel_id=1, source_target_pairs={{0,4},{12,8},{1,5},{13,9},{2,6},{14,10},{3,7},{15,11},{16,20},{28,... | collective-permute-start | bytes 786440 | tf_op jit(solution)/shard_map/ppermute | solution.py:474
  129.5 8.4 %collective-permute-start.26 = (bf16[256,512]{1,0:T(8,128)(2,1)S(1)}, bf16[256,512]{1,0:T(8,128)(2,1)S(1)}, u32[]{:S(2)}, u32[]{:S(2)}) collective-permute-start(bf16[256,512]{1,0:T(8,128)(2,1)S(1)} %get-tuple-element.150.refs_2_), channel_id=1, source_target_pairs={{0,2},{1,3},{2,0},{3,1},{4,6},{5,7},{6,4},{7,5},{8,10},{9,11},{10,... | collective-permute-start | bytes 786440 | tf_op jit(solution)/shard_map/ppermute | solution.py:365
  132.1 9.5 %collective-permute-start.25 = (bf16[256,512]{1,0:T(8,128)(2,1)S(1)}, bf16[256,512]{1,0:T(8,128)(2,1)S(1)}, u32[]{:S(2)}, u32[]{:S(2)}) collective-permute-start(bf16[256,512]{1,0:T(8,128)(2,1)S(1)} %get-tuple-element.150.refs_2_), channel_id=1, source_target_pairs={{0,1},{1,0},{2,3},{3,2},{4,5},{5,4},{6,7},{7,6},{8,9},{9,8},{10,11... | collective-permute-start | bytes 786440 | tf_op jit(solution)/shard_map/ppermute | solution.py:361
  146.9 12.3 %collective-permute-start.28 = (bf16[256,512]{1,0:T(8,128)(2,1)S(1)}, bf16[256,512]{1,0:T(8,128)(2,1)S(1)}, u32[]{:S(2)}, u32[]{:S(2)}) collective-permute-start(bf16[256,512]{1,0:T(8,128)(2,1)S(1)} %shard_map.84), channel_id=1, source_target_pairs={{0,4},{12,8},{1,5},{13,9},{2,6},{14,10},{3,7},{15,11},{16,20},{28,... | collective-permute-start | bytes 786440 | tf_op jit(solution)/shard_map/ppermute | solution.py:474
  148.9 15.8 %collective-permute-start.29 = (bf16[512,256]{1,0:T(8,128)(2,1)S(1)}, bf16[512,256]{1,0:T(8,128)(2,1)S(1)}, u32[]{:S(2)}, u32[]{:S(2)}) collective-permute-start(bf16[512,256]{1,0:T(8,128)(2,1)S(1)} %get-tuple-element.161), channel_id=1, source_target_pairs={{0,0},{1,4},{2,8},{3,12},{4,1},{5,5},{6,9},{7,13},{8,2},{9,6},{10,... | collective-permute-start | bytes 786440 | tf_op jit(solution)/shard_map/ppermute | solution.py:372
  149.6 17.8 %collective-permute-start.30 = (bf16[256,512]{1,0:T(8,128)(2,1)S(1)}, bf16[256,512]{1,0:T(8,128)(2,1)S(1)}, u32[]{:S(2)}, u32[]{:S(2)}) collective-permute-start(bf16[256,512]{1,0:T(8,128)(2,1)S(1)} %shard_map.78), channel_id=1, source_target_pairs={{4,8},{8,4},{5,9},{9,5},{6,10},{10,6},{7,11},{11,7},{20,24},{24,20... | collective-permute-start | bytes 786440 | tf_op jit(solution)/shard_map/ppermute | solution.py:475
  150.3 45.5 %collective-permute-start.32 = (bf16[256,512]{1,0:T(8,128)(2,1)S(1)}, bf16[256,512]{1,0:T(8,128)(2,1)S(1)}, u32[]{:S(2)}, u32[]{:S(2)}) collective-permute-start(bf16[256,512]{1,0:T(8,128)(2,1)S(1)} %shard_map.81), channel_id=1, source_target_pairs={{0,8},{4,12},{8,0},{12,4},{1,9},{5,13},{9,1},{13,5},{2,10},{6,14},... | collective-permute-start | bytes 786440 | tf_op jit(solution)/shard_map/ppermute | solution.py:368
  157.0 38.8 %collective-permute-start.31 = (bf16[256,512]{1,0:T(8,128)(2,1)S(1)}, bf16[256,512]{1,0:T(8,128)(2,1)S(1)}, u32[]{:S(2)}, u32[]{:S(2)}) collective-permute-start(bf16[256,512]{1,0:T(8,128)(2,1)S(1)} %shard_map.80), channel_id=1, source_target_pairs={{0,4},{4,0},{8,12},{12,8},{1,5},{5,1},{9,13},{13,9},{2,6},{6,2},{1... | collective-permute-start | bytes 786440 | tf_op jit(solution)/shard_map/ppermute | solution.py:368
  159.2 39.1 %collective-permute-start.33 = (bf16[512,256]{1,0:T(8,128)(2,1)S(1)}, bf16[512,256]{1,0:T(8,128)(2,1)S(1)}, u32[]{:S(2)}, u32[]{:S(2)}) collective-permute-start(bf16[512,256]{1,0:T(8,128)(2,1)S(1)} %get-tuple-element.170), channel_id=1, source_target_pairs={{0,0},{1,4},{2,8},{3,12},{4,1},{5,5},{6,9},{7,13},{8,2},{9,6},{10,... | collective-permute-start | bytes 786440 | tf_op jit(solution)/shard_map/ppermute | solution.py:372
  164.7 35.4 %collective-permute-start.36 = (bf16[256,512]{1,0:T(8,128)(2,1)S(1)}, bf16[256,512]{1,0:T(8,128)(2,1)S(1)}, u32[]{:S(2)}, u32[]{:S(2)}) collective-permute-start(bf16[256,512]{1,0:T(8,128)(2,1)S(1)} %shard_map.84), channel_id=1, source_target_pairs={{4,8},{8,4},{5,9},{9,5},{6,10},{10,6},{7,11},{11,7},{20,24},{24,20... | collective-permute-start | bytes 786440 | tf_op jit(solution)/shard_map/ppermute | solution.py:475
  167.4 32.7 %collective-permute-start.37 = (bf16[256,512]{1,0:T(8,128)(2,1)S(1)}, bf16[256,512]{1,0:T(8,128)(2,1)S(1)}, u32[]{:S(2)}, u32[]{:S(2)}) collective-permute-start(bf16[256,512]{1,0:T(8,128)(2,1)S(1)} %shard_map.85), channel_id=1, source_target_pairs={{0,4},{4,0},{8,12},{12,8},{1,5},{5,1},{9,13},{13,9},{2,6},{6,2},{1... | collective-permute-start | bytes 786440 | tf_op jit(solution)/shard_map/ppermute | solution.py:368
  198.0 12.3 %collective-permute-start.38 = (bf16[256,512]{1,0:T(8,128)(2,1)S(1)}, bf16[256,512]{1,0:T(8,128)(2,1)S(1)}, u32[]{:S(2)}, u32[]{:S(2)}) collective-permute-start(bf16[256,512]{1,0:T(8,128)(2,1)S(1)} %shard_map.86), channel_id=1, source_target_pairs={{0,8},{4,12},{8,0},{12,4},{1,9},{5,13},{9,1},{13,5},{2,10},{6,14},... | collective-permute-start | bytes 786440 | tf_op jit(solution)/shard_map/ppermute | solution.py:368
  198.2 14.5 %collective-permute-start.34 = (f32[4,2,16,1024]{3,2,0,1:T(8,128)S(1)}, f32[4,2,16,1024]{3,2,0,1:T(8,128)S(1)}, u32[]{:S(2)}, u32[]{:S(2)}) collective-permute-start(f32[4,2,16,1024]{3,2,0,1:T(8,128)S(1)} %bitcast.77), channel_id=1, source_target_pairs={{0,1},{1,0},{2,3},{3,2},{4,5},{5,4},{6,7},{7,6},{8,9},{9,8},{10,11... | collective-permute-start | bytes 1572872 | tf_op jit(solution)/shard_map/ppermute | solution.py:361
  221.9 7.6 %collective-permute-start.42 = (bf16[2,16,1024]{2,1,0:T(8,128)(2,1)S(1)}, bf16[2,16,1024]{2,1,0:T(8,128)(2,1)S(1)}, u32[]{:S(2)}, u32[]{:S(2)}) collective-permute-start(bf16[2,16,1024]{2,1,0:T(8,128)(2,1)S(1)} %get-tuple-element.200), channel_id=1, source_target_pairs={{0,8},{4,12},{8,0},{12,4},{1,9},{5,13},{9,1},{13,5},{2,10},{6,14},... | collective-permute-start | bytes 196616 | tf_op jit(solution)/shard_map/ppermute | solution.py:368
  (16 other events, 93.1 us)

commit v3 on v2

--- a/solution.py
+++ b/solution.py
@@ -79,7 +79,6 @@
     spec = pl.BlockSpec((tile, cols), lambda i, m: (i, 0))
     return queue.call(
         body, (rows // tile,), [spec], [spec, spec], [shape(cov.shape, BF16)] * 2, [cov],
-        limit=3 * VMEM_LIMIT,
     )
 
 
@@ -132,9 +131,10 @@
     )
 
 
-def product_one(queue, cov, blocks, acc, row_of, count, add=None, coded=False):
+def product_one(queue, cov, blocks, acc, row_of, count, add=None, coded=False, ready=None, emit=False):
     hi, lo = cov
     n, width = blocks[0][0][0].shape
+    fresh = ready is None
     whole = count * n == hi.shape[0]
     terms = len(blocks)
     tall = n
@@ -144,12 +144,17 @@
     def body(m, *refs):
         refs = list(refs)
         his, los, refs = refs[:terms], refs[terms : 2 * terms], refs[2 * terms :]
-        codes = [[refs.pop(0) for _ in got] for got, _ in blocks]
+        if fresh:
+            codes = [[refs.pop(0) for _ in got] for got, _ in blocks]
+        else:
+            p_hi, p_lo = refs.pop(0), refs.pop(0)
         acc_ref = refs.pop(0) if acc is not None else None
         add_ref = refs.pop(0) if add is not None else None
-        out, p_hi, p_lo = refs
-
-        @pl.when(pl.program_id(0) == 0)
+        out = refs.pop(0)
+        if fresh:
+            p_hi, p_lo = refs
+
+        @pl.when(fresh and pl.program_id(0) == 0)
         def _():
             for t in range(terms):
                 code = sum(ref[...].astype(F32) for ref in codes[t])
@@ -169,8 +174,10 @@
     specs = [
         pl.BlockSpec((tall, n), lambda i, m, at=at: (row_of(i, m), m[at])) for _, at in blocks
     ]
-    codes = [code for got, _ in blocks for code in got]
-    ins = specs + specs + [pl.BlockSpec((n, width), lambda i, m: (0, 0))] * len(codes)
+    codes = [code for got, _ in blocks for code in got] if fresh else list(ready)
+    parts = pl.BlockSpec((terms, n, width), lambda i, m: (0, 0, 0))
+    held = pl.BlockSpec((n, width), lambda i, m: (0, 0)) if fresh else parts
+    ins = specs + specs + [held] * len(codes)
     args = [hi] * terms + [lo] * terms + codes
     alias = None
     if acc is not None:
@@ -185,10 +192,11 @@
         body,
         (count,),
         ins,
-        [pl.BlockSpec((tall, width), lambda i, m: (i, 0))],
-        [shape((count * tall, width), BF16 if coded else F32)],
+        [pl.BlockSpec((tall, width), lambda i, m: (i, 0))] + [parts] * (2 * emit),
+        [shape((count * tall, width), BF16 if coded else F32)]
+        + [shape((terms, n, width), BF16)] * (2 * emit),
         args,
-        scratch=[pltpu.VMEM((terms, n, width), BF16)] * 2,
+        scratch=[pltpu.VMEM((terms, n, width), BF16)] * (2 * (fresh and not emit)),
         alias=alias,
         flops=6 * terms * count * tall * n * width,
     )
@@ -221,21 +229,25 @@
     )
 
 
-def product_two(queue, cov, blocks, acc, col_of, count, coded=False, add=None):
+def product_two(queue, cov, blocks, acc, col_of, count, coded=False, add=None, ready=None, emit=False):
     hi, lo = cov
     width, n = blocks[0][0].shape
+    fresh = ready is None
     whole = count * n == hi.shape[1]
     terms = len(blocks)
 
     def body(m, *refs):
         refs = list(refs)
-        his, los, codes = refs[:terms], refs[terms : 2 * terms], refs[2 * terms : 3 * terms]
-        refs = refs[3 * terms :]
+        his, los, refs = refs[:terms], refs[terms : 2 * terms], refs[2 * terms :]
+        codes = [refs.pop(0) for _ in blocks] if fresh else []
+        parts = None if fresh else refs.pop(0)
         acc_ref = refs.pop(0) if acc is not None else None
         add_ref = refs.pop(0) if add is not None else None
-        out, parts = refs
-
-        @pl.when(pl.program_id(0) == 0)
+        out = refs.pop(0)
+        if fresh:
+            (parts,) = refs
+
+        @pl.when(fresh and pl.program_id(0) == 0)
         def _():
             for t in range(terms):
                 parts[t, :width], parts[t, width:] = halves(decode(codes[t][...], SCALE_A))
@@ -255,8 +267,11 @@
     specs = [
         pl.BlockSpec((n, n), lambda i, m, row=row: (row(m), col_of(i, m))) for _, row in blocks
     ]
-    ins = specs + specs + [pl.BlockSpec((width, n), lambda i, m: (0, 0))] * terms
-    args = [hi] * terms + [lo] * terms + [code for code, _ in blocks]
+    whole_parts = pl.BlockSpec((terms, 2 * width, n), lambda i, m: (0, 0, 0))
+    codes = [code for code, _ in blocks] if fresh else [ready]
+    held = pl.BlockSpec((width, n), lambda i, m: (0, 0)) if fresh else whole_parts
+    ins = specs + specs + [held] * len(codes)
+    args = [hi] * terms + [lo] * terms + codes
     alias = None
     if acc is not None:
         if whole:
@@ -270,10 +285,11 @@
         body,
         (count,),
         ins,
-        [pl.BlockSpec((width, n), lambda i, m: (0, i))],
-        [shape((width, count * n), BF16 if coded else F32)],
+        [pl.BlockSpec((width, n), lambda i, m: (0, i))] + [whole_parts] * emit,
+        [shape((width, count * n), BF16 if coded else F32)]
+        + [shape((terms, 2 * width, n), BF16)] * emit,
         args,
-        scratch=[pltpu.VMEM((terms, 2 * width, n), BF16)],
+        scratch=[pltpu.VMEM((terms, 2 * width, n), BF16)] * (fresh and not emit),
         alias=alias,
         flops=6 * terms * count * n * n * width,
     )
@@ -427,10 +443,13 @@
     def pieces_one(k, acc):
         blocks = [(panels[k][s], from_row + s) for s in range(side - late, side)]
 
+        ready = None
+
         def piece(row_of, count, add=None, coded=False):
-            return product_one(queue, cov, blocks, acc, row_of, count, add, coded)
-
-        far_other = piece(lambda i, m: m[to_y + 1 + i] * CORES + 1 - m[core_at], ys - 1)
+            first = ready is None
+            return product_one(queue, cov, blocks, acc, row_of, count, add, coded, ready, first)
+
+        far_other, *ready = piece(lambda i, m: m[to_y + 1 + i] * CORES + 1 - m[core_at], ys - 1)
         far_add = swap_core(far_other)
         near_other = piece(lambda i, m: m[to_y] * CORES + 1 - m[core_at], 1)
         near_add = swap_core(near_other)
@@ -457,8 +476,8 @@
             acc = product_two(queue, cov, [block], acc, lambda i, m: i, side)
         return acc, blocks[-late:]
 
-    def away_two(acc, blocks, between):
-        landed, passed = [], None
+    def away_two(k, acc, blocks, between):
+        landed, passed, ready = [], None, None
         for hop in away_order(side):
             piece = product_two(
                 queue,
@@ -469,7 +488,12 @@
                 1,
                 coded=True,
                 add=passed if relay and hop == 2 else None,
+                ready=ready,
+                emit=ready is None,
             )
+            if ready is None:
+                piece, ready = piece
+            parts_two[k] = ready
             if relay and hop == 3:
                 passed = lax.ppermute(piece, "row", ends_in)
                 landed.append(lax.ppermute(piece, "row", middle))
@@ -480,8 +504,11 @@
                 between = None
         return landed
 
-    def kept_two(acc, blocks):
-        return product_two(queue, cov, blocks, acc, lambda i, m: m[to_row], 1)
+    def kept_two(k, acc, blocks):
+        return product_two(
+            queue, cov, blocks, acc, lambda i, m: m[to_row], 1,
+            ready=parts_two[k],
+        )
 
     def finish_b(value):
         value = value.reshape(side, ys, CORES, share, features)
@@ -502,7 +529,7 @@
     accs = [early_one(k, None, 0) for k in ks]
     sums, seconds, fields, values = [], [], [], []
 
-    new_a, diffs = [], []
+    new_a, diffs, parts_two = [], [], {}
 
     def finish_one(k):
         blocks, back = start_two(k, *sums[k])
@@ -526,12 +553,12 @@
         sums.append(pieces_one(k, accs[k]))
         if k > 0:
             after = (lambda: finish_one(last)) if k == last else None
-            fields.append(away_two(*seconds[k - 1][0], after))
+            fields.append(away_two(k - 1, *seconds[k - 1][0], after))
     if last == 0:
         finish_one(last)
     seconds[last][0] = early_two(seconds[last][0])
-    fields.append(away_two(*seconds[last][0], None))
-    kept = [kept_two(*seconds[k][0]) for k in reversed(ks)][::-1]
+    fields.append(away_two(last, *seconds[last][0], None))
+    kept = [kept_two(k, *seconds[k][0]) for k in reversed(ks)][::-1]
     for k in range(last):
         diff_two(k)
         grad_two(k)

time: 232 us -> 232 us (level)
  Pallas kernels: 80.6 us -> 72.8 us
  local copies, waits for them, and re-layouts: 4.55 us -> 10.3 us
    pallas_call x34, Pallas kernels: 80.6 us -> 72.8 us  [call(): pl.pallas_call(body, out_shape=shapes, grid_spec=spec, input_output_alias...]
    unnamed x11 -> x13, local copies, waits for them, and re-layouts: 4.13 us -> 9.89 us
  transfers between devices with their start and end apart: 44 -> 44, of which waited for: 17 -> 17; matrix products, arithmetic and copies ran while one was open for 2% -> 2% of each run, Pallas kernels for 31% -> 27%
where the time goes in v3:
time: 232 us; the launch traced here: 231 us
  waiting for transfers between devices  77.2 us (33%)
  Pallas kernels  72.8 us (31%)
  starting transfers between devices  67 us (29%)
  local copies, waits for them, and re-layouts  10.3 us (4%)
  other arithmetic  2.33 us (1%)
    pallas_call x34, Pallas kernels, call(): pl.pallas_call(body, out_shape=shapes, grid_spec=spec, input_output_alias...  72.8 us
    ppermute x14, waiting for transfers between devices, shift_row(): return lax.ppermute(x, 'row', [(i, i ^ s) for i in range(side)])  40.9 us
    ppermute x14, starting transfers between devices, shift_row(): return lax.ppermute(x, 'row', [(i, i ^ s) for i in range(side)])  38 us
    ppermute x7, waiting for transfers between devices, shift_y(): return lax.ppermute(x, 'col', pairs)  30.6 us
    ppermute x7, starting transfers between devices, shift_y(): return lax.ppermute(x, 'col', pairs)  13.8 us
    unnamed x13, local copies, waits for them, and re-layouts  9.89 us
    ppermute x2, starting transfers between devices, away_two(): passed = lax.ppermute(piece, 'row', ends_in)  5.34 us
  transfers between devices with their start and end apart: 44, of which 17 were waited for; matrix products, arithmetic and copies ran while one was open for 2% of the time, Pallas kernels for 27%

profile of v3, /device:TPU:0, one launch (start us, length us, event | category | flops | bytes accessed | tf_op | source)
XLA Modules:
  0.0 231.1 jit_solution(16899395973836791259)
XLA Ops:
  0.6 3.1 %collective-permute-start = (bf16[2,16,1024]{2,1,0:T(8,128)(2,1)}, bf16[2,16,1024]{2,1,0:T(8,128)(2,1)S(1)}, u32[]{:S(2)}, u32[]{:S(2)}) collective-permute-start(bf16[2,16,1024]{2,1,0:T(8,128)(2,1)} %param.7), channel_id=1, source_target_pairs={{0,4},{4,0},{8,12},{12,8},{1,5},{5,1},{9,13},{13,9},{2,6},{6,2},{1... | collective-permute-start | bytes 196616 | tf_op jit(solution)/shard_map/ppermute | solution.py:384
  3.7 2.6 %collective-permute-start.1 = (bf16[2,16,1024]{2,1,0:T(8,128)(2,1)}, bf16[2,16,1024]{2,1,0:T(8,128)(2,1)S(1)}, u32[]{:S(2)}, u32[]{:S(2)}) collective-permute-start(bf16[2,16,1024]{2,1,0:T(8,128)(2,1)} %param.7), channel_id=1, source_target_pairs={{0,8},{4,12},{8,0},{12,4},{1,9},{5,13},{9,1},{13,5},{2,10},{6,14},... | collective-permute-start | bytes 196616 | tf_op jit(solution)/shard_map/ppermute | solution.py:384
  6.3 4.9 %collective-permute-done.1 = bf16[2,16,1024]{2,1,0:T(8,128)(2,1)S(1)} collective-permute-done((bf16[2,16,1024]{2,1,0:T(8,128)(2,1)}, bf16[2,16,1024]{2,1,0:T(8,128)(2,1)S(1)}, u32[]{:S(2)}, u32[]{:S(2)}) %collective-permute-start.1) | collective-permute-done | bytes 65568 | tf_op jit(solution)/shard_map/ppermute | solution.py:384
  15.1 4.9 %collective-permute-done.3 = bf16[4,2,16,1024]{3,2,1,0:T(8,128)(2,1)S(1)} collective-permute-done((bf16[4,2,16,1024]{3,2,1,0:T(8,128)(2,1)S(1)}, bf16[4,2,16,1024]{3,2,1,0:T(8,128)(2,1)S(1)}, u32[]{:S(2)}, u32[]{:S(2)}) %collective-permute-start.3) | collective-permute-done | bytes 262176 | tf_op jit(solution)/shard_map/ppermute | solution.py:381
  20.2 2.2 copy.17
  22.6 2.5 %shard_map.59.b = bf16[2,256,1024]{2,1,0:T(8,128)(2,1)S(1)} custom-call(s32[13]{0:T(128)S(1)} %concatenate.3.m, bf16[2,4,2,16,1024]{4,3,2,1,0:T(8,128)(2,1)S(1)} %pad_maximum_fusion.1.own, bf16[2,4,2,16,1024]{4,3,2,1,0:T(8,128)(2,1)} %collective-permute-done.4.other), custom_call_target="tpu_custom_call" | custom-call | bytes 2097152 | tf_op jit(solution)/shard_map/pallas_call | solution.py:54
  31.9 5.8 %copy-done.2 = f32[2048,2048]{1,0:T(8,128)S(1)} copy-done((f32[2048,2048]{1,0:T(8,128)S(1)}, f32[2048,2048]{1,0:T(8,128)}, u32[]{:S(2)}) %copy-start.2) | copy-done | bytes 16777240
  37.6 3.3 %shard_map.62 = (bf16[2048,2048]{1,0:T(8,128)(2,1)S(1)}, bf16[2048,2048]{1,0:T(8,128)(2,1)S(1)}) custom-call(s32[13]{0:T(128)S(1)} %concatenate.3.m, f32[2048,2048]{1,0:T(8,128)S(1)} %copy-done.2), custom_call_target="tpu_custom_call" | custom-call | bytes 33554432 | tf_op jit(solution)/shard_map/pallas_call | solution.py:54
  40.9 3.1 %shard_map.63.refs_3_ = f32[2048,256]{1,0:T(8,128)S(1)} custom-call(s32[13]{0:T(128)S(1)} %concatenate.3.m, bf16[2048,2048]{1,0:T(8,128)(2,1)S(1)} %get-tuple-element.123.refs_0_.refs_1_, bf16[2048,2048]{1,0:T(8,128)(2,1)S(1)} %get-tuple-element.124.refs_1_.refs_2_.refs_3_, bf16[512,256]{1,0:T(8,128)(2,1)S(1)} %shard_map.60.refs_2_), custom_call_target="tpu_custom_call" | custom-call | flops 1610612736 | bytes 19136512 | tf_op jit(solution)/shard_map/pallas_call | solution.py:54
  45.4 3.1 %shard_map.64.refs_3_ = f32[2048,256]{1,0:T(8,128)S(1)} custom-call(s32[13]{0:T(128)S(1)} %concatenate.3.m, bf16[2048,2048]{1,0:T(8,128)(2,1)S(1)} %get-tuple-element.123.refs_0_.refs_1_, bf16[2048,2048]{1,0:T(8,128)(2,1)S(1)} %get-tuple-element.124.refs_1_.refs_2_.refs_3_, bf16[512,256]{1,0:T(8,128)(2,1)S(1)} %shard_map.61.refs_2_), custom_call_target="tpu_custom_call" | custom-call | flops 1610612736 | bytes 19136512 | tf_op jit(solution)/shard_map/pallas_call | solution.py:54
  48.5 3.3 %shard_map.65.refs_7_.refs_6_ = f32[2048,256]{1,0:T(8,128)S(1)} custom-call(s32[13]{0:T(128)S(1)} %concatenate.3.m, bf16[2048,2048]{1,0:T(8,128)(2,1)S(1)} %get-tuple-element.123.refs_0_.refs_1_, bf16[2048,2048]{1,0:T(8,128)(2,1)S(1)} %get-tuple-element.124.refs_1_.refs_2_.refs_3_, ...), custom_call_target="tpu_custom_call", output_to_operand_aliasing={{}: (4, {})} | custom-call | flops 1610612736 | bytes 21233664 | tf_op jit(solution)/shard_map/pallas_call | solution.py:54
  51.8 3.0 %collective-permute-done.8.refs_6_ = bf16[512,256]{1,0:T(8,128)(2,1)S(1)} collective-permute-done((bf16[512,256]{1,0:T(8,128)(2,1)S(1)}, bf16[512,256]{1,0:T(8,128)(2,1)S(1)}, u32[]{:S(2)}, u32[]{:S(2)}) %collective-permute-start.8) | collective-permute-done | bytes 262176 | tf_op jit(solution)/shard_map/ppermute | solution.py:429
  61.3 5.7 %collective-permute-start.12 = (bf16[512,256]{1,0:T(8,128)(2,1)S(1)}, bf16[512,256]{1,0:T(8,128)(2,1)S(1)}, u32[]{:S(2)}, u32[]{:S(2)}) collective-permute-start(bf16[512,256]{1,0:T(8,128)(2,1)S(1)} %shard_map.68), channel_id=1, source_target_pairs={{0,2},{1,3},{2,0},{3,1},{4,6},{5,7},{6,4},{7,5},{8,10},{9,11},{10,... | collective-permute-start | bytes 786440 | tf_op jit(solution)/shard_map/ppermute | solution.py:381
  68.5 3.3 %shard_map.70.refs_7_.refs_6_ = f32[2048,256]{1,0:T(8,128)S(1)} custom-call(s32[13]{0:T(128)S(1)} %concatenate.3.m, bf16[2048,2048]{1,0:T(8,128)(2,1)S(1)} %get-tuple-element.123.refs_0_.refs_1_, bf16[2048,2048]{1,0:T(8,128)(2,1)S(1)} %get-tuple-element.124.refs_1_.refs_2_.refs_3_, ...), custom_call_target="tpu_custom_call", output_to_operand_aliasing={{}: (4, {})} | custom-call | flops 1610612736 | bytes 21233664 | tf_op jit(solution)/shard_map/pallas_call | solution.py:54
  71.8 3.9 %collective-permute-done.12.rest_0_ = bf16[512,256]{1,0:T(8,128)(2,1)S(1)} collective-permute-done((bf16[512,256]{1,0:T(8,128)(2,1)S(1)}, bf16[512,256]{1,0:T(8,128)(2,1)S(1)}, u32[]{:S(2)}, u32[]{:S(2)}) %collective-permute-start.12) | collective-permute-done | bytes 262176 | tf_op jit(solution)/shard_map/ppermute | solution.py:381
  77.8 10.9 %collective-permute-done.15.refs_4_ = bf16[512,256]{1,0:T(8,128)(2,1)S(1)} collective-permute-done((bf16[512,256]{1,0:T(8,128)(2,1)S(1)}, bf16[512,256]{1,0:T(8,128)(2,1)S(1)}, u32[]{:S(2)}, u32[]{:S(2)}) %collective-permute-start.15) | collective-permute-done | bytes 262176 | tf_op jit(solution)/shard_map/ppermute | solution.py:384
  90.1 3.6 %shard_map.72.refs_3_ = f32[256,2048]{1,0:T(8,128)S(1)} custom-call(s32[13]{0:T(128)S(1)} %concatenate.3.m, bf16[2048,2048]{1,0:T(8,128)(2,1)S(1)} %get-tuple-element.123.refs_0_.refs_1_, bf16[2048,2048]{1,0:T(8,128)(2,1)S(1)} %get-tuple-element.124.refs_1_.refs_2_.refs_3_, bf16[256,512]{1,0:T(8,128)(2,1)S(1)} %get-tuple-element.150.refs_2_), custom_call_target="tpu_custom_call" | custom-call | flops 1610612736 | bytes 19136512 | tf_op jit(solution)/shard_map/pallas_call | solution.py:54
  93.7 3.8 %shard_map.73.refs_6_.refs_5_ = f32[256,2048]{1,0:T(8,128)S(1)} custom-call(s32[13]{0:T(128)S(1)} %concatenate.3.m, bf16[2048,2048]{1,0:T(8,128)(2,1)S(1)} %get-tuple-element.123.refs_0_.refs_1_, bf16[2048,2048]{1,0:T(8,128)(2,1)S(1)} %get-tuple-element.124.refs_1_.refs_2_.refs_3_, ...), custom_call_target="tpu_custom_call", output_to_operand_aliasing={{}: (4, {})} | custom-call | flops 1610612736 | bytes 21233664 | tf_op jit(solution)/shard_map/pallas_call | solution.py:54
  102.6 8.3 %collective-permute-done.20.refs_4_ = bf16[256,512]{1,0:T(8,128)(2,1)S(1)} collective-permute-done((bf16[256,512]{1,0:T(8,128)(2,1)S(1)}, bf16[256,512]{1,0:T(8,128)(2,1)S(1)}, u32[]{:S(2)}, u32[]{:S(2)}) %collective-permute-start.20) | collective-permute-done | bytes 262176 | tf_op jit(solution)/shard_map/ppermute | solution.py:381
  113.1 3.5 %collective-permute-start.22 = (bf16[512,256]{1,0:T(8,128)(2,1)S(1)}, bf16[512,256]{1,0:T(8,128)(2,1)S(1)}, u32[]{:S(2)}, u32[]{:S(2)}) collective-permute-start(bf16[512,256]{1,0:T(8,128)(2,1)S(1)} %shard_map.76), channel_id=1, source_target_pairs={{0,2},{1,3},{2,0},{3,1},{4,6},{5,7},{6,4},{7,5},{8,10},{9,11},{10,... | collective-permute-start | bytes 786440 | tf_op jit(solution)/shard_map/ppermute | solution.py:381
  119.8 2.6 %collective-permute-start.24 = (bf16[256,512]{1,0:T(8,128)(2,1)S(1)}, bf16[256,512]{1,0:T(8,128)(2,1)S(1)}, u32[]{:S(2)}, u32[]{:S(2)}) collective-permute-start(bf16[256,512]{1,0:T(8,128)(2,1)S(1)} %get-tuple-element.177), channel_id=1, source_target_pairs={{0,4},{12,8},{1,5},{13,9},{2,6},{14,10},{3,7},{15,11},{16,20},{28,... | collective-permute-start | bytes 786440 | tf_op jit(solution)/shard_map/ppermute | solution.py:498
  122.4 5.1 %collective-permute-done.22.rest_0_ = bf16[512,256]{1,0:T(8,128)(2,1)S(1)} collective-permute-done((bf16[512,256]{1,0:T(8,128)(2,1)S(1)}, bf16[512,256]{1,0:T(8,128)(2,1)S(1)}, u32[]{:S(2)}, u32[]{:S(2)}) %collective-permute-start.22) | collective-permute-done | bytes 262176 | tf_op jit(solution)/shard_map/ppermute | solution.py:381
  128.7 2.5 %collective-permute-start.26 = (bf16[256,512]{1,0:T(8,128)(2,1)S(1)}, bf16[256,512]{1,0:T(8,128)(2,1)S(1)}, u32[]{:S(2)}, u32[]{:S(2)}) collective-permute-start(bf16[256,512]{1,0:T(8,128)(2,1)S(1)} %get-tuple-element.179.refs_2_), channel_id=1, source_target_pairs={{0,2},{1,3},{2,0},{3,1},{4,6},{5,7},{6,4},{7,5},{8,10},{9,11},{10,... | collective-permute-start | bytes 786440 | tf_op jit(solution)/shard_map/ppermute | solution.py:381
  136.6 3.6 %shard_map.82.refs_3_ = f32[256,2048]{1,0:T(8,128)S(1)} custom-call(s32[13]{0:T(128)S(1)} %concatenate.3.m, bf16[2048,2048]{1,0:T(8,128)(2,1)S(1)} %get-tuple-element.123.refs_0_.refs_1_, bf16[2048,2048]{1,0:T(8,128)(2,1)S(1)} %get-tuple-element.124.refs_1_.refs_2_.refs_3_, bf16[256,512]{1,0:T(8,128)(2,1)S(1)} %get-tuple-element.179.refs_2_), custom_call_target="tpu_custom_call" | custom-call | flops 1610612736 | bytes 19136512 | tf_op jit(solution)/shard_map/pallas_call | solution.py:54
  140.2 3.8 %shard_map.83.refs_6_.refs_5_ = f32[256,2048]{1,0:T(8,128)S(1)} custom-call(s32[13]{0:T(128)S(1)} %concatenate.3.m, bf16[2048,2048]{1,0:T(8,128)(2,1)S(1)} %get-tuple-element.123.refs_0_.refs_1_, bf16[2048,2048]{1,0:T(8,128)(2,1)S(1)} %get-tuple-element.124.refs_1_.refs_2_.refs_3_, ...), custom_call_target="tpu_custom_call", output_to_operand_aliasing={{}: (4, {})} | custom-call | flops 1610612736 | bytes 21233664 | tf_op jit(solution)/shard_map/pallas_call | solution.py:54
  145.6 2.7 %collective-permute-start.28 = (bf16[256,512]{1,0:T(8,128)(2,1)S(1)}, bf16[256,512]{1,0:T(8,128)(2,1)S(1)}, u32[]{:S(2)}, u32[]{:S(2)}) collective-permute-start(bf16[256,512]{1,0:T(8,128)(2,1)S(1)} %get-tuple-element.189), channel_id=1, source_target_pairs={{0,4},{12,8},{1,5},{13,9},{2,6},{14,10},{3,7},{15,11},{16,20},{28,... | collective-permute-start | bytes 786440 | tf_op jit(solution)/shard_map/ppermute | solution.py:498
  149.7 6.6 %collective-permute-start.32 = (bf16[256,512]{1,0:T(8,128)(2,1)S(1)}, bf16[256,512]{1,0:T(8,128)(2,1)S(1)}, u32[]{:S(2)}, u32[]{:S(2)}) collective-permute-start(bf16[256,512]{1,0:T(8,128)(2,1)S(1)} %shard_map.81), channel_id=1, source_target_pairs={{0,8},{4,12},{8,0},{12,4},{1,9},{5,13},{9,1},{13,5},{2,10},{6,14},... | collective-permute-start | bytes 786440 | tf_op jit(solution)/shard_map/ppermute | solution.py:384
  166.7 17.9 %collective-permute-start.37 = (bf16[256,512]{1,0:T(8,128)(2,1)S(1)}, bf16[256,512]{1,0:T(8,128)(2,1)S(1)}, u32[]{:S(2)}, u32[]{:S(2)}) collective-permute-start(bf16[256,512]{1,0:T(8,128)(2,1)S(1)} %shard_map.85), channel_id=1, source_target_pairs={{0,4},{4,0},{8,12},{12,8},{1,5},{5,1},{9,13},{13,9},{2,6},{6,2},{1... | collective-permute-start | bytes 786440 | tf_op jit(solution)/shard_map/ppermute | solution.py:384
  184.5 10.7 %collective-permute-done.32.rest_2_ = bf16[256,512]{1,0:T(8,128)(2,1)S(1)} collective-permute-done((bf16[256,512]{1,0:T(8,128)(2,1)S(1)}, bf16[256,512]{1,0:T(8,128)(2,1)S(1)}, u32[]{:S(2)}, u32[]{:S(2)}) %collective-permute-start.32) | collective-permute-done | bytes 262176 | tf_op jit(solution)/shard_map/ppermute | solution.py:384
  199.5 10.2 %collective-permute-done.38.rest_2_ = bf16[256,512]{1,0:T(8,128)(2,1)S(1)} collective-permute-done((bf16[256,512]{1,0:T(8,128)(2,1)S(1)}, bf16[256,512]{1,0:T(8,128)(2,1)S(1)}, u32[]{:S(2)}, u32[]{:S(2)}) %collective-permute-start.38) | collective-permute-done | bytes 262176 | tf_op jit(solution)/shard_map/ppermute | solution.py:384
  214.5 4.1 %collective-permute-done.35 = bf16[4,16,1024]{2,1,0:T(8,128)(2,1)S(1)} collective-permute-done((bf16[4,16,1024]{2,1,0:T(8,128)(2,1)S(1)}, bf16[4,16,1024]{2,1,0:T(8,128)(2,1)S(1)}, u32[]{:S(2)}, u32[]{:S(2)}) %collective-permute-start.35) | collective-permute-done | bytes 131104 | tf_op jit(solution)/shard_map/ppermute | solution.py:381
  221.3 2.9 %collective-permute-start.42 = (bf16[2,16,1024]{2,1,0:T(8,128)(2,1)S(1)}, bf16[2,16,1024]{2,1,0:T(8,128)(2,1)S(1)}, u32[]{:S(2)}, u32[]{:S(2)}) collective-permute-start(bf16[2,16,1024]{2,1,0:T(8,128)(2,1)S(1)} %get-tuple-element.232), channel_id=1, source_target_pairs={{0,8},{4,12},{8,0},{12,4},{1,9},{5,13},{9,1},{13,5},{2,10},{6,14},... | collective-permute-start | bytes 196616 | tf_op jit(solution)/shard_map/ppermute | solution.py:384
  (122 shorter events, 72.3 us)
Async XLA Ops:
  3.7 7.5 %collective-permute-start.1 = (bf16[2,16,1024]{2,1,0:T(8,128)(2,1)}, bf16[2,16,1024]{2,1,0:T(8,128)(2,1)S(1)}, u32[]{:S(2)}, u32[]{:S(2)}) collective-permute-start(bf16[2,16,1024]{2,1,0:T(8,128)(2,1)} %param.7), channel_id=1, source_target_pairs={{0,8},{4,12},{8,0},{12,4},{1,9},{5,13},{9,1},{13,5},{2,10},{6,14},... | collective-permute-start | bytes 196616 | tf_op jit(solution)/shard_map/ppermute | solution.py:384
  27.0 17.0 %collective-permute-start.6 = (bf16[512,256]{1,0:T(8,128)(2,1)S(1)}, bf16[512,256]{1,0:T(8,128)(2,1)S(1)}, u32[]{:S(2)}, u32[]{:S(2)}) collective-permute-start(bf16[512,256]{1,0:T(8,128)(2,1)S(1)} %shard_map.60.refs_2_), channel_id=1, source_target_pairs={{0,8},{4,12},{8,0},{12,4},{1,9},{5,13},{9,1},{13,5},{2,10},{6,14},... | collective-permute-start | bytes 786440 | tf_op jit(solution)/shard_map/ppermute | solution.py:384
  29.2 19.3 %collective-permute-start.5 = (bf16[512,256]{1,0:T(8,128)(2,1)S(1)}, bf16[512,256]{1,0:T(8,128)(2,1)S(1)}, u32[]{:S(2)}, u32[]{:S(2)}) collective-permute-start(bf16[512,256]{1,0:T(8,128)(2,1)S(1)} %shard_map.60.refs_2_), channel_id=1, source_target_pairs={{0,4},{4,0},{8,12},{12,8},{1,5},{5,1},{9,13},{13,9},{2,6},{6,2},{1... | collective-permute-start | bytes 786440 | tf_op jit(solution)/shard_map/ppermute | solution.py:384
  29.4 22.4 %collective-permute-start.7 = (bf16[512,256]{1,0:T(8,128)(2,1)S(1)}, bf16[512,256]{1,0:T(8,128)(2,1)S(1)}, u32[]{:S(2)}, u32[]{:S(2)}) collective-permute-start(bf16[512,256]{1,0:T(8,128)(2,1)S(1)} %shard_map.60.refs_2_), channel_id=1, source_target_pairs={{4,8},{8,4},{5,9},{9,5},{6,10},{10,6},{7,11},{11,7},{20,24},{24,20... | collective-permute-start | bytes 786440 | tf_op jit(solution)/shard_map/ppermute | solution.py:429
  44.1 10.7 %collective-permute-start.8 = (bf16[512,256]{1,0:T(8,128)(2,1)S(1)}, bf16[512,256]{1,0:T(8,128)(2,1)S(1)}, u32[]{:S(2)}, u32[]{:S(2)}) collective-permute-start(bf16[512,256]{1,0:T(8,128)(2,1)S(1)} %collective-permute-done.6.refs_4_), channel_id=1, source_target_pairs={{4,0},{8,12},{5,1},{9,13},{6,2},{10,14},{7,3},{11,15},{20,16},{24,... | collective-permute-start | bytes 786440 | tf_op jit(solution)/shard_map/ppermute | solution.py:429
  58.2 8.8 %collective-permute-start.10 = (f32[512,256]{1,0:T(8,128)S(1)}, f32[512,256]{1,0:T(8,128)S(1)}, u32[]{:S(2)}, u32[]{:S(2)}) collective-permute-start(f32[512,256]{1,0:T(8,128)S(1)} %shard_map.67), channel_id=1, source_target_pairs={{0,1},{1,0},{2,3},{3,2},{4,5},{5,4},{6,7},{7,6},{8,9},{9,8},{10,11... | collective-permute-start | bytes 1572872 | tf_op jit(solution)/shard_map/ppermute | solution.py:377
  58.8 9.8 %collective-permute-start.11 = (bf16[512,256]{1,0:T(8,128)(2,1)S(1)}, bf16[512,256]{1,0:T(8,128)(2,1)S(1)}, u32[]{:S(2)}, u32[]{:S(2)}) collective-permute-start(bf16[512,256]{1,0:T(8,128)(2,1)S(1)} %shard_map.61.refs_2_), channel_id=1, source_target_pairs={{0,4},{4,0},{8,12},{12,8},{1,5},{5,1},{9,13},{13,9},{2,6},{6,2},{1... | collective-permute-start | bytes 786440 | tf_op jit(solution)/shard_map/ppermute | solution.py:384
  59.0 12.8 %collective-permute-start.13 = (bf16[512,256]{1,0:T(8,128)(2,1)S(1)}, bf16[512,256]{1,0:T(8,128)(2,1)S(1)}, u32[]{:S(2)}, u32[]{:S(2)}) collective-permute-start(bf16[512,256]{1,0:T(8,128)(2,1)S(1)} %get-tuple-element.234), channel_id=1, source_target_pairs={{0,0},{1,4},{2,8},{3,12},{4,1},{5,5},{6,9},{7,13},{8,2},{9,6},{10,... | collective-permute-start | bytes 786440 | tf_op jit(solution)/shard_map/ppermute | solution.py:388
  61.3 14.5 %collective-permute-start.12 = (bf16[512,256]{1,0:T(8,128)(2,1)S(1)}, bf16[512,256]{1,0:T(8,128)(2,1)S(1)}, u32[]{:S(2)}, u32[]{:S(2)}) collective-permute-start(bf16[512,256]{1,0:T(8,128)(2,1)S(1)} %shard_map.68), channel_id=1, source_target_pairs={{0,2},{1,3},{2,0},{3,1},{4,6},{5,7},{6,4},{7,5},{8,10},{9,11},{10,... | collective-permute-start | bytes 786440 | tf_op jit(solution)/shard_map/ppermute | solution.py:381
  67.0 21.6 %collective-permute-start.15 = (bf16[512,256]{1,0:T(8,128)(2,1)S(1)}, bf16[512,256]{1,0:T(8,128)(2,1)S(1)}, u32[]{:S(2)}, u32[]{:S(2)}) collective-permute-start(bf16[512,256]{1,0:T(8,128)(2,1)S(1)} %shard_map.61.refs_2_), channel_id=1, source_target_pairs={{0,8},{4,12},{8,0},{12,4},{1,9},{5,13},{9,1},{13,5},{2,10},{6,14},... | collective-permute-start | bytes 786440 | tf_op jit(solution)/shard_map/ppermute | solution.py:384
  77.0 16.7 %collective-permute-start.14 = (bf16[256,512]{1,0:T(8,128)(2,1)S(1)}, bf16[256,512]{1,0:T(8,128)(2,1)S(1)}, u32[]{:S(2)}, u32[]{:S(2)}) collective-permute-start(bf16[256,512]{1,0:T(8,128)(2,1)S(1)} %get-tuple-element.150.refs_2_), channel_id=1, source_target_pairs={{0,1},{1,0},{2,3},{3,2},{4,5},{5,4},{6,7},{7,6},{8,9},{9,8},{10,11... | collective-permute-start | bytes 786440 | tf_op jit(solution)/shard_map/ppermute | solution.py:377
  77.1 20.4 %collective-permute-start.16 = (bf16[512,256]{1,0:T(8,128)(2,1)S(1)}, bf16[512,256]{1,0:T(8,128)(2,1)S(1)}, u32[]{:S(2)}, u32[]{:S(2)}) collective-permute-start(bf16[512,256]{1,0:T(8,128)(2,1)S(1)} %shard_map.61.refs_2_), channel_id=1, source_target_pairs={{4,8},{8,4},{5,9},{9,5},{6,10},{10,6},{7,11},{11,7},{20,24},{24,20... | collective-permute-start | bytes 786440 | tf_op jit(solution)/shard_map/ppermute | solution.py:429
  88.6 9.9 %collective-permute-start.17 = (bf16[512,256]{1,0:T(8,128)(2,1)S(1)}, bf16[512,256]{1,0:T(8,128)(2,1)S(1)}, u32[]{:S(2)}, u32[]{:S(2)}) collective-permute-start(bf16[512,256]{1,0:T(8,128)(2,1)S(1)} %collective-permute-done.15.refs_4_), channel_id=1, source_target_pairs={{4,0},{8,12},{5,1},{9,13},{6,2},{10,14},{7,3},{11,15},{20,16},{24,... | collective-permute-start | bytes 786440 | tf_op jit(solution)/shard_map/ppermute | solution.py:429
  100.4 11.1 %collective-permute-start.18 = (f32[512,256]{1,0:T(8,128)S(1)}, f32[512,256]{1,0:T(8,128)S(1)}, u32[]{:S(2)}, u32[]{:S(2)}) collective-permute-start(f32[512,256]{1,0:T(8,128)S(1)} %get-tuple-element.162), channel_id=1, source_target_pairs={{0,1},{1,0},{2,3},{3,2},{4,5},{5,4},{6,7},{7,6},{8,9},{9,8},{10,11... | collective-permute-start | bytes 1572872 | tf_op jit(solution)/shard_map/ppermute | solution.py:377
  102.0 14.6 %collective-permute-start.19 = (f32[512,256]{1,0:T(8,128)S(1)}, f32[512,256]{1,0:T(8,128)S(1)}, u32[]{:S(2)}, u32[]{:S(2)}) collective-permute-start(f32[512,256]{1,0:T(8,128)S(1)} %shard_map.75), channel_id=1, source_target_pairs={{0,1},{1,0},{2,3},{3,2},{4,5},{5,4},{6,7},{7,6},{8,9},{9,8},{10,11... | collective-permute-start | bytes 1572872 | tf_op jit(solution)/shard_map/ppermute | solution.py:377
  102.5 8.3 %collective-permute-start.20 = (bf16[256,512]{1,0:T(8,128)(2,1)S(1)}, bf16[256,512]{1,0:T(8,128)(2,1)S(1)}, u32[]{:S(2)}, u32[]{:S(2)}) collective-permute-start(bf16[256,512]{1,0:T(8,128)(2,1)S(1)} %get-tuple-element.150.refs_2_), channel_id=1, source_target_pairs={{0,2},{1,3},{2,0},{3,1},{4,6},{5,7},{6,4},{7,5},{8,10},{9,11},{10,... | collective-permute-start | bytes 786440 | tf_op jit(solution)/shard_map/ppermute | solution.py:381
  110.8 11.5 %collective-permute-start.23 = (bf16[512,256]{1,0:T(8,128)(2,1)S(1)}, bf16[512,256]{1,0:T(8,128)(2,1)S(1)}, u32[]{:S(2)}, u32[]{:S(2)}) collective-permute-start(bf16[512,256]{1,0:T(8,128)(2,1)S(1)} %get-tuple-element.233), channel_id=1, source_target_pairs={{0,0},{1,4},{2,8},{3,12},{4,1},{5,5},{6,9},{7,13},{8,2},{9,6},{10,... | collective-permute-start | bytes 786440 | tf_op jit(solution)/shard_map/ppermute | solution.py:388
  113.1 14.4 %collective-permute-start.22 = (bf16[512,256]{1,0:T(8,128)(2,1)S(1)}, bf16[512,256]{1,0:T(8,128)(2,1)S(1)}, u32[]{:S(2)}, u32[]{:S(2)}) collective-permute-start(bf16[512,256]{1,0:T(8,128)(2,1)S(1)} %shard_map.76), channel_id=1, source_target_pairs={{0,2},{1,3},{2,0},{3,1},{4,6},{5,7},{6,4},{7,5},{8,10},{9,11},{10,... | collective-permute-start | bytes 786440 | tf_op jit(solution)/shard_map/ppermute | solution.py:381
  119.8 13.1 %collective-permute-start.24 = (bf16[256,512]{1,0:T(8,128)(2,1)S(1)}, bf16[256,512]{1,0:T(8,128)(2,1)S(1)}, u32[]{:S(2)}, u32[]{:S(2)}) collective-permute-start(bf16[256,512]{1,0:T(8,128)(2,1)S(1)} %get-tuple-element.177), channel_id=1, source_target_pairs={{0,4},{12,8},{1,5},{13,9},{2,6},{14,10},{3,7},{15,11},{16,20},{28,... | collective-permute-start | bytes 786440 | tf_op jit(solution)/shard_map/ppermute | solution.py:498
  128.7 7.9 %collective-permute-start.26 = (bf16[256,512]{1,0:T(8,128)(2,1)S(1)}, bf16[256,512]{1,0:T(8,128)(2,1)S(1)}, u32[]{:S(2)}, u32[]{:S(2)}) collective-permute-start(bf16[256,512]{1,0:T(8,128)(2,1)S(1)} %get-tuple-element.179.refs_2_), channel_id=1, source_target_pairs={{0,2},{1,3},{2,0},{3,1},{4,6},{5,7},{6,4},{7,5},{8,10},{9,11},{10,... | collective-permute-start | bytes 786440 | tf_op jit(solution)/shard_map/ppermute | solution.py:381
  131.2 9.0 %collective-permute-start.25 = (bf16[256,512]{1,0:T(8,128)(2,1)S(1)}, bf16[256,512]{1,0:T(8,128)(2,1)S(1)}, u32[]{:S(2)}, u32[]{:S(2)}) collective-permute-start(bf16[256,512]{1,0:T(8,128)(2,1)S(1)} %get-tuple-element.179.refs_2_), channel_id=1, source_target_pairs={{0,1},{1,0},{2,3},{3,2},{4,5},{5,4},{6,7},{7,6},{8,9},{9,8},{10,11... | collective-permute-start | bytes 786440 | tf_op jit(solution)/shard_map/ppermute | solution.py:377
  145.6 13.0 %collective-permute-start.28 = (bf16[256,512]{1,0:T(8,128)(2,1)S(1)}, bf16[256,512]{1,0:T(8,128)(2,1)S(1)}, u32[]{:S(2)}, u32[]{:S(2)}) collective-permute-start(bf16[256,512]{1,0:T(8,128)(2,1)S(1)} %get-tuple-element.189), channel_id=1, source_target_pairs={{0,4},{12,8},{1,5},{13,9},{2,6},{14,10},{3,7},{15,11},{16,20},{28,... | collective-permute-start | bytes 786440 | tf_op jit(solution)/shard_map/ppermute | solution.py:498
  148.4 15.9 %collective-permute-start.29 = (bf16[512,256]{1,0:T(8,128)(2,1)S(1)}, bf16[512,256]{1,0:T(8,128)(2,1)S(1)}, u32[]{:S(2)}, u32[]{:S(2)}) collective-permute-start(bf16[512,256]{1,0:T(8,128)(2,1)S(1)} %get-tuple-element.193), channel_id=1, source_target_pairs={{0,0},{1,4},{2,8},{3,12},{4,1},{5,5},{6,9},{7,13},{8,2},{9,6},{10,... | collective-permute-start | bytes 786440 | tf_op jit(solution)/shard_map/ppermute | solution.py:388
  149.0 17.6 %collective-permute-start.30 = (bf16[256,512]{1,0:T(8,128)(2,1)S(1)}, bf16[256,512]{1,0:T(8,128)(2,1)S(1)}, u32[]{:S(2)}, u32[]{:S(2)}) collective-permute-start(bf16[256,512]{1,0:T(8,128)(2,1)S(1)} %get-tuple-element.177), channel_id=1, source_target_pairs={{4,8},{8,4},{5,9},{9,5},{6,10},{10,6},{7,11},{11,7},{20,24},{24,20... | collective-permute-start | bytes 786440 | tf_op jit(solution)/shard_map/ppermute | solution.py:499
  149.7 45.5 %collective-permute-start.32 = (bf16[256,512]{1,0:T(8,128)(2,1)S(1)}, bf16[256,512]{1,0:T(8,128)(2,1)S(1)}, u32[]{:S(2)}, u32[]{:S(2)}) collective-permute-start(bf16[256,512]{1,0:T(8,128)(2,1)S(1)} %shard_map.81), channel_id=1, source_target_pairs={{0,8},{4,12},{8,0},{12,4},{1,9},{5,13},{9,1},{13,5},{2,10},{6,14},... | collective-permute-start | bytes 786440 | tf_op jit(solution)/shard_map/ppermute | solution.py:384
  156.4 38.8 %collective-permute-start.31 = (bf16[256,512]{1,0:T(8,128)(2,1)S(1)}, bf16[256,512]{1,0:T(8,128)(2,1)S(1)}, u32[]{:S(2)}, u32[]{:S(2)}) collective-permute-start(bf16[256,512]{1,0:T(8,128)(2,1)S(1)} %shard_map.80), channel_id=1, source_target_pairs={{0,4},{4,0},{8,12},{12,8},{1,5},{5,1},{9,13},{13,9},{2,6},{6,2},{1... | collective-permute-start | bytes 786440 | tf_op jit(solution)/shard_map/ppermute | solution.py:384
  158.6 39.1 %collective-permute-start.33 = (bf16[512,256]{1,0:T(8,128)(2,1)S(1)}, bf16[512,256]{1,0:T(8,128)(2,1)S(1)}, u32[]{:S(2)}, u32[]{:S(2)}) collective-permute-start(bf16[512,256]{1,0:T(8,128)(2,1)S(1)} %get-tuple-element.202), channel_id=1, source_target_pairs={{0,0},{1,4},{2,8},{3,12},{4,1},{5,5},{6,9},{7,13},{8,2},{9,6},{10,... | collective-permute-start | bytes 786440 | tf_op jit(solution)/shard_map/ppermute | solution.py:388
  164.2 35.3 %collective-permute-start.36 = (bf16[256,512]{1,0:T(8,128)(2,1)S(1)}, bf16[256,512]{1,0:T(8,128)(2,1)S(1)}, u32[]{:S(2)}, u32[]{:S(2)}) collective-permute-start(bf16[256,512]{1,0:T(8,128)(2,1)S(1)} %get-tuple-element.189), channel_id=1, source_target_pairs={{4,8},{8,4},{5,9},{9,5},{6,10},{10,6},{7,11},{11,7},{20,24},{24,20... | collective-permute-start | bytes 786440 | tf_op jit(solution)/shard_map/ppermute | solution.py:499
  166.7 32.8 %collective-permute-start.37 = (bf16[256,512]{1,0:T(8,128)(2,1)S(1)}, bf16[256,512]{1,0:T(8,128)(2,1)S(1)}, u32[]{:S(2)}, u32[]{:S(2)}) collective-permute-start(bf16[256,512]{1,0:T(8,128)(2,1)S(1)} %shard_map.85), channel_id=1, source_target_pairs={{0,4},{4,0},{8,12},{12,8},{1,5},{5,1},{9,13},{13,9},{2,6},{6,2},{1... | collective-permute-start | bytes 786440 | tf_op jit(solution)/shard_map/ppermute | solution.py:384
  197.4 12.3 %collective-permute-start.38 = (bf16[256,512]{1,0:T(8,128)(2,1)S(1)}, bf16[256,512]{1,0:T(8,128)(2,1)S(1)}, u32[]{:S(2)}, u32[]{:S(2)}) collective-permute-start(bf16[256,512]{1,0:T(8,128)(2,1)S(1)} %shard_map.86), channel_id=1, source_target_pairs={{0,8},{4,12},{8,0},{12,4},{1,9},{5,13},{9,1},{13,5},{2,10},{6,14},... | collective-permute-start | bytes 786440 | tf_op jit(solution)/shard_map/ppermute | solution.py:384
  197.6 14.5 %collective-permute-start.34 = (f32[4,2,16,1024]{3,2,0,1:T(8,128)S(1)}, f32[4,2,16,1024]{3,2,0,1:T(8,128)S(1)}, u32[]{:S(2)}, u32[]{:S(2)}) collective-permute-start(f32[4,2,16,1024]{3,2,0,1:T(8,128)S(1)} %bitcast.77), channel_id=1, source_target_pairs={{0,1},{1,0},{2,3},{3,2},{4,5},{5,4},{6,7},{7,6},{8,9},{9,8},{10,11... | collective-permute-start | bytes 1572872 | tf_op jit(solution)/shard_map/ppermute | solution.py:377
  221.3 7.6 %collective-permute-start.42 = (bf16[2,16,1024]{2,1,0:T(8,128)(2,1)S(1)}, bf16[2,16,1024]{2,1,0:T(8,128)(2,1)S(1)}, u32[]{:S(2)}, u32[]{:S(2)}) collective-permute-start(bf16[2,16,1024]{2,1,0:T(8,128)(2,1)S(1)} %get-tuple-element.232), channel_id=1, source_target_pairs={{0,8},{4,12},{8,0},{12,4},{1,9},{5,13},{9,1},{13,5},{2,10},{6,14},... | collective-permute-start | bytes 196616 | tf_op jit(solution)/shard_map/ppermute | solution.py:384
  (17 other events, 97.9 us)

commit v4 on v3

--- a/solution.py
+++ b/solution.py
@@ -13,8 +13,8 @@
 SCALE_P = 2.0**-2
 SCALE_G = 2.0**-7
 SCALE_A = 2.0**-4
-SCALE_F = 2.0**-12
-SCALE_V = 2.0**-16
+SCALE_F = 2.0**-17
+SCALE_V = 2.0**-36
 
 
 def encode(x, scale):
@@ -25,6 +25,17 @@
 def decode(code, scale):
     v = code.astype(F32)
     root = lax.rsqrt(lax.rsqrt(jnp.abs(v))) * (1.0 / scale)
+    return jnp.where(v < 0, -root, root)
+
+
+def encode_wide(x):
+    u = x * SCALE_V
+    return (u * jnp.abs(u)).astype(BF16)
+
+
+def decode_wide(code):
+    v = code.astype(F32)
+    root = jnp.sqrt(jnp.abs(v)) * (1.0 / SCALE_V)
     return jnp.where(v < 0, -root, root)
 
 
@@ -515,15 +526,15 @@
         value = pick(value, own_core, 2) + swap_core(pick(value, other_core, 2))
         mine = pick(value, own_y, 1)
         for s in range(1, ys):
-            away = encode(pick(value, next_y[s], 1), SCALE_V)
-            mine = mine + decode(shift_y(away, s), SCALE_V)
+            away = encode_wide(pick(value, next_y[s], 1))
+            mine = mine + decode_wide(shift_y(away, s))
         return mine
 
     def sum_rows(mine):
         total = pick(mine, own_row, 1)
         for s in range(1, side):
-            away = encode(pick(mine, next_row[s], 1), SCALE_V)
-            total = total + decode(shift_row(away, s), SCALE_V)
+            away = encode_wide(pick(mine, next_row[s], 1))
+            total = total + decode_wide(shift_row(away, s))
         return factor_b.astype(F32) + step_b * total
 
     accs = [early_one(k, None, 0) for k in ks]

time: 232 us -> 232 us (level)
  no operation moved by 1% of the time
where the time goes in v4:
time: 232 us; the launch traced here: 231 us
  waiting for transfers between devices  77.2 us (33%)
  Pallas kernels  72.8 us (31%)
  starting transfers between devices  67 us (29%)
  local copies, waits for them, and re-layouts  10.3 us (4%)
  other arithmetic  2.38 us (1%)
    pallas_call x34, Pallas kernels, call(): pl.pallas_call(body, out_shape=shapes, grid_spec=spec, input_output_alias...  72.8 us
    ppermute x14, waiting for transfers between devices, shift_row(): return lax.ppermute(x, 'row', [(i, i ^ s) for i in range(side)])  40.9 us
    ppermute x14, starting transfers between devices, shift_row(): return lax.ppermute(x, 'row', [(i, i ^ s) for i in range(side)])  38 us
    ppermute x7, waiting for transfers between devices, shift_y(): return lax.ppermute(x, 'col', pairs)  30.6 us
    ppermute x7, starting transfers between devices, shift_y(): return lax.ppermute(x, 'col', pairs)  13.8 us
    unnamed x13, local copies, waits for them, and re-layouts  9.89 us
    ppermute x2, starting transfers between devices, away_two(): passed = lax.ppermute(piece, 'row', ends_in)  5.34 us
  transfers between devices with their start and end apart: 44, of which 17 were waited for; matrix products, arithmetic and copies ran while one was open for 2% of the time, Pallas kernels for 27%

profile of v4, /device:TPU:0, one launch (start us, length us, event | category | flops | bytes accessed | tf_op | source)
XLA Modules:
  0.0 231.1 jit_solution(5578507490022166452)
XLA Ops:
  0.6 3.1 %collective-permute-start = (bf16[2,16,1024]{2,1,0:T(8,128)(2,1)}, bf16[2,16,1024]{2,1,0:T(8,128)(2,1)S(1)}, u32[]{:S(2)}, u32[]{:S(2)}) collective-permute-start(bf16[2,16,1024]{2,1,0:T(8,128)(2,1)} %param.7), channel_id=1, source_target_pairs={{0,4},{4,0},{8,12},{12,8},{1,5},{5,1},{9,13},{13,9},{2,6},{6,2},{1... | collective-permute-start | bytes 196616 | tf_op jit(solution)/shard_map/ppermute | solution.py:395
  3.7 2.6 %collective-permute-start.1 = (bf16[2,16,1024]{2,1,0:T(8,128)(2,1)}, bf16[2,16,1024]{2,1,0:T(8,128)(2,1)S(1)}, u32[]{:S(2)}, u32[]{:S(2)}) collective-permute-start(bf16[2,16,1024]{2,1,0:T(8,128)(2,1)} %param.7), channel_id=1, source_target_pairs={{0,8},{4,12},{8,0},{12,4},{1,9},{5,13},{9,1},{13,5},{2,10},{6,14},... | collective-permute-start | bytes 196616 | tf_op jit(solution)/shard_map/ppermute | solution.py:395
  6.3 4.9 %collective-permute-done.1 = bf16[2,16,1024]{2,1,0:T(8,128)(2,1)S(1)} collective-permute-done((bf16[2,16,1024]{2,1,0:T(8,128)(2,1)}, bf16[2,16,1024]{2,1,0:T(8,128)(2,1)S(1)}, u32[]{:S(2)}, u32[]{:S(2)}) %collective-permute-start.1) | collective-permute-done | bytes 65568 | tf_op jit(solution)/shard_map/ppermute | solution.py:395
  15.1 4.9 %collective-permute-done.3 = bf16[4,2,16,1024]{3,2,1,0:T(8,128)(2,1)S(1)} collective-permute-done((bf16[4,2,16,1024]{3,2,1,0:T(8,128)(2,1)S(1)}, bf16[4,2,16,1024]{3,2,1,0:T(8,128)(2,1)S(1)}, u32[]{:S(2)}, u32[]{:S(2)}) %collective-permute-start.3) | collective-permute-done | bytes 262176 | tf_op jit(solution)/shard_map/ppermute | solution.py:392
  20.2 2.2 copy.17
  22.6 2.5 %shard_map.59.b = bf16[2,256,1024]{2,1,0:T(8,128)(2,1)S(1)} custom-call(s32[13]{0:T(128)S(1)} %concatenate.3.m, bf16[2,4,2,16,1024]{4,3,2,1,0:T(8,128)(2,1)S(1)} %pad_maximum_fusion.1.own, bf16[2,4,2,16,1024]{4,3,2,1,0:T(8,128)(2,1)} %collective-permute-done.4.other), custom_call_target="tpu_custom_call" | custom-call | bytes 2097152 | tf_op jit(solution)/shard_map/pallas_call | solution.py:65
  31.9 5.8 %copy-done.2 = f32[2048,2048]{1,0:T(8,128)S(1)} copy-done((f32[2048,2048]{1,0:T(8,128)S(1)}, f32[2048,2048]{1,0:T(8,128)}, u32[]{:S(2)}) %copy-start.2) | copy-done | bytes 16777240
  37.6 3.3 %shard_map.62 = (bf16[2048,2048]{1,0:T(8,128)(2,1)S(1)}, bf16[2048,2048]{1,0:T(8,128)(2,1)S(1)}) custom-call(s32[13]{0:T(128)S(1)} %concatenate.3.m, f32[2048,2048]{1,0:T(8,128)S(1)} %copy-done.2), custom_call_target="tpu_custom_call" | custom-call | bytes 33554432 | tf_op jit(solution)/shard_map/pallas_call | solution.py:65
  40.9 3.1 %shard_map.63.refs_3_ = f32[2048,256]{1,0:T(8,128)S(1)} custom-call(s32[13]{0:T(128)S(1)} %concatenate.3.m, bf16[2048,2048]{1,0:T(8,128)(2,1)S(1)} %get-tuple-element.123.refs_0_.refs_1_, bf16[2048,2048]{1,0:T(8,128)(2,1)S(1)} %get-tuple-element.124.refs_1_.refs_2_.refs_3_, bf16[512,256]{1,0:T(8,128)(2,1)S(1)} %shard_map.60.refs_2_), custom_call_target="tpu_custom_call" | custom-call | flops 1610612736 | bytes 19136512 | tf_op jit(solution)/shard_map/pallas_call | solution.py:65
  45.4 3.1 %shard_map.64.refs_3_ = f32[2048,256]{1,0:T(8,128)S(1)} custom-call(s32[13]{0:T(128)S(1)} %concatenate.3.m, bf16[2048,2048]{1,0:T(8,128)(2,1)S(1)} %get-tuple-element.123.refs_0_.refs_1_, bf16[2048,2048]{1,0:T(8,128)(2,1)S(1)} %get-tuple-element.124.refs_1_.refs_2_.refs_3_, bf16[512,256]{1,0:T(8,128)(2,1)S(1)} %shard_map.61.refs_2_), custom_call_target="tpu_custom_call" | custom-call | flops 1610612736 | bytes 19136512 | tf_op jit(solution)/shard_map/pallas_call | solution.py:65
  48.5 3.3 %shard_map.65.refs_7_.refs_6_ = f32[2048,256]{1,0:T(8,128)S(1)} custom-call(s32[13]{0:T(128)S(1)} %concatenate.3.m, bf16[2048,2048]{1,0:T(8,128)(2,1)S(1)} %get-tuple-element.123.refs_0_.refs_1_, bf16[2048,2048]{1,0:T(8,128)(2,1)S(1)} %get-tuple-element.124.refs_1_.refs_2_.refs_3_, ...), custom_call_target="tpu_custom_call", output_to_operand_aliasing={{}: (4, {})} | custom-call | flops 1610612736 | bytes 21233664 | tf_op jit(solution)/shard_map/pallas_call | solution.py:65
  51.8 3.0 %collective-permute-done.8.refs_6_ = bf16[512,256]{1,0:T(8,128)(2,1)S(1)} collective-permute-done((bf16[512,256]{1,0:T(8,128)(2,1)S(1)}, bf16[512,256]{1,0:T(8,128)(2,1)S(1)}, u32[]{:S(2)}, u32[]{:S(2)}) %collective-permute-start.8) | collective-permute-done | bytes 262176 | tf_op jit(solution)/shard_map/ppermute | solution.py:440
  61.3 5.7 %collective-permute-start.12 = (bf16[512,256]{1,0:T(8,128)(2,1)S(1)}, bf16[512,256]{1,0:T(8,128)(2,1)S(1)}, u32[]{:S(2)}, u32[]{:S(2)}) collective-permute-start(bf16[512,256]{1,0:T(8,128)(2,1)S(1)} %shard_map.68), channel_id=1, source_target_pairs={{0,2},{1,3},{2,0},{3,1},{4,6},{5,7},{6,4},{7,5},{8,10},{9,11},{10,... | collective-permute-start | bytes 786440 | tf_op jit(solution)/shard_map/ppermute | solution.py:392
  68.5 3.3 %shard_map.70.refs_7_.refs_6_ = f32[2048,256]{1,0:T(8,128)S(1)} custom-call(s32[13]{0:T(128)S(1)} %concatenate.3.m, bf16[2048,2048]{1,0:T(8,128)(2,1)S(1)} %get-tuple-element.123.refs_0_.refs_1_, bf16[2048,2048]{1,0:T(8,128)(2,1)S(1)} %get-tuple-element.124.refs_1_.refs_2_.refs_3_, ...), custom_call_target="tpu_custom_call", output_to_operand_aliasing={{}: (4, {})} | custom-call | flops 1610612736 | bytes 21233664 | tf_op jit(solution)/shard_map/pallas_call | solution.py:65
  71.8 3.9 %collective-permute-done.12.rest_0_ = bf16[512,256]{1,0:T(8,128)(2,1)S(1)} collective-permute-done((bf16[512,256]{1,0:T(8,128)(2,1)S(1)}, bf16[512,256]{1,0:T(8,128)(2,1)S(1)}, u32[]{:S(2)}, u32[]{:S(2)}) %collective-permute-start.12) | collective-permute-done | bytes 262176 | tf_op jit(solution)/shard_map/ppermute | solution.py:392
  77.8 10.9 %collective-permute-done.15.refs_4_ = bf16[512,256]{1,0:T(8,128)(2,1)S(1)} collective-permute-done((bf16[512,256]{1,0:T(8,128)(2,1)S(1)}, bf16[512,256]{1,0:T(8,128)(2,1)S(1)}, u32[]{:S(2)}, u32[]{:S(2)}) %collective-permute-start.15) | collective-permute-done | bytes 262176 | tf_op jit(solution)/shard_map/ppermute | solution.py:395
  90.1 3.6 %shard_map.72.refs_3_ = f32[256,2048]{1,0:T(8,128)S(1)} custom-call(s32[13]{0:T(128)S(1)} %concatenate.3.m, bf16[2048,2048]{1,0:T(8,128)(2,1)S(1)} %get-tuple-element.123.refs_0_.refs_1_, bf16[2048,2048]{1,0:T(8,128)(2,1)S(1)} %get-tuple-element.124.refs_1_.refs_2_.refs_3_, bf16[256,512]{1,0:T(8,128)(2,1)S(1)} %get-tuple-element.150.refs_2_), custom_call_target="tpu_custom_call" | custom-call | flops 1610612736 | bytes 19136512 | tf_op jit(solution)/shard_map/pallas_call | solution.py:65
  93.7 3.8 %shard_map.73.refs_6_.refs_5_ = f32[256,2048]{1,0:T(8,128)S(1)} custom-call(s32[13]{0:T(128)S(1)} %concatenate.3.m, bf16[2048,2048]{1,0:T(8,128)(2,1)S(1)} %get-tuple-element.123.refs_0_.refs_1_, bf16[2048,2048]{1,0:T(8,128)(2,1)S(1)} %get-tuple-element.124.refs_1_.refs_2_.refs_3_, ...), custom_call_target="tpu_custom_call", output_to_operand_aliasing={{}: (4, {})} | custom-call | flops 1610612736 | bytes 21233664 | tf_op jit(solution)/shard_map/pallas_call | solution.py:65
  102.6 8.3 %collective-permute-done.20.refs_4_ = bf16[256,512]{1,0:T(8,128)(2,1)S(1)} collective-permute-done((bf16[256,512]{1,0:T(8,128)(2,1)S(1)}, bf16[256,512]{1,0:T(8,128)(2,1)S(1)}, u32[]{:S(2)}, u32[]{:S(2)}) %collective-permute-start.20) | collective-permute-done | bytes 262176 | tf_op jit(solution)/shard_map/ppermute | solution.py:392
  113.1 3.5 %collective-permute-start.22 = (bf16[512,256]{1,0:T(8,128)(2,1)S(1)}, bf16[512,256]{1,0:T(8,128)(2,1)S(1)}, u32[]{:S(2)}, u32[]{:S(2)}) collective-permute-start(bf16[512,256]{1,0:T(8,128)(2,1)S(1)} %shard_map.76), channel_id=1, source_target_pairs={{0,2},{1,3},{2,0},{3,1},{4,6},{5,7},{6,4},{7,5},{8,10},{9,11},{10,... | collective-permute-start | bytes 786440 | tf_op jit(solution)/shard_map/ppermute | solution.py:392
  119.8 2.6 %collective-permute-start.24 = (bf16[256,512]{1,0:T(8,128)(2,1)S(1)}, bf16[256,512]{1,0:T(8,128)(2,1)S(1)}, u32[]{:S(2)}, u32[]{:S(2)}) collective-permute-start(bf16[256,512]{1,0:T(8,128)(2,1)S(1)} %get-tuple-element.177), channel_id=1, source_target_pairs={{0,4},{12,8},{1,5},{13,9},{2,6},{14,10},{3,7},{15,11},{16,20},{28,... | collective-permute-start | bytes 786440 | tf_op jit(solution)/shard_map/ppermute | solution.py:509
  122.4 5.1 %collective-permute-done.22.rest_0_ = bf16[512,256]{1,0:T(8,128)(2,1)S(1)} collective-permute-done((bf16[512,256]{1,0:T(8,128)(2,1)S(1)}, bf16[512,256]{1,0:T(8,128)(2,1)S(1)}, u32[]{:S(2)}, u32[]{:S(2)}) %collective-permute-start.22) | collective-permute-done | bytes 262176 | tf_op jit(solution)/shard_map/ppermute | solution.py:392
  128.7 2.5 %collective-permute-start.26 = (bf16[256,512]{1,0:T(8,128)(2,1)S(1)}, bf16[256,512]{1,0:T(8,128)(2,1)S(1)}, u32[]{:S(2)}, u32[]{:S(2)}) collective-permute-start(bf16[256,512]{1,0:T(8,128)(2,1)S(1)} %get-tuple-element.179.refs_2_), channel_id=1, source_target_pairs={{0,2},{1,3},{2,0},{3,1},{4,6},{5,7},{6,4},{7,5},{8,10},{9,11},{10,... | collective-permute-start | bytes 786440 | tf_op jit(solution)/shard_map/ppermute | solution.py:392
  136.6 3.6 %shard_map.82.refs_3_ = f32[256,2048]{1,0:T(8,128)S(1)} custom-call(s32[13]{0:T(128)S(1)} %concatenate.3.m, bf16[2048,2048]{1,0:T(8,128)(2,1)S(1)} %get-tuple-element.123.refs_0_.refs_1_, bf16[2048,2048]{1,0:T(8,128)(2,1)S(1)} %get-tuple-element.124.refs_1_.refs_2_.refs_3_, bf16[256,512]{1,0:T(8,128)(2,1)S(1)} %get-tuple-element.179.refs_2_), custom_call_target="tpu_custom_call" | custom-call | flops 1610612736 | bytes 19136512 | tf_op jit(solution)/shard_map/pallas_call | solution.py:65
  140.2 3.8 %shard_map.83.refs_6_.refs_5_ = f32[256,2048]{1,0:T(8,128)S(1)} custom-call(s32[13]{0:T(128)S(1)} %concatenate.3.m, bf16[2048,2048]{1,0:T(8,128)(2,1)S(1)} %get-tuple-element.123.refs_0_.refs_1_, bf16[2048,2048]{1,0:T(8,128)(2,1)S(1)} %get-tuple-element.124.refs_1_.refs_2_.refs_3_, ...), custom_call_target="tpu_custom_call", output_to_operand_aliasing={{}: (4, {})} | custom-call | flops 1610612736 | bytes 21233664 | tf_op jit(solution)/shard_map/pallas_call | solution.py:65
  145.6 2.7 %collective-permute-start.28 = (bf16[256,512]{1,0:T(8,128)(2,1)S(1)}, bf16[256,512]{1,0:T(8,128)(2,1)S(1)}, u32[]{:S(2)}, u32[]{:S(2)}) collective-permute-start(bf16[256,512]{1,0:T(8,128)(2,1)S(1)} %get-tuple-element.189), channel_id=1, source_target_pairs={{0,4},{12,8},{1,5},{13,9},{2,6},{14,10},{3,7},{15,11},{16,20},{28,... | collective-permute-start | bytes 786440 | tf_op jit(solution)/shard_map/ppermute | solution.py:509
  149.7 6.6 %collective-permute-start.32 = (bf16[256,512]{1,0:T(8,128)(2,1)S(1)}, bf16[256,512]{1,0:T(8,128)(2,1)S(1)}, u32[]{:S(2)}, u32[]{:S(2)}) collective-permute-start(bf16[256,512]{1,0:T(8,128)(2,1)S(1)} %shard_map.81), channel_id=1, source_target_pairs={{0,8},{4,12},{8,0},{12,4},{1,9},{5,13},{9,1},{13,5},{2,10},{6,14},... | collective-permute-start | bytes 786440 | tf_op jit(solution)/shard_map/ppermute | solution.py:395
  166.7 17.9 %collective-permute-start.37 = (bf16[256,512]{1,0:T(8,128)(2,1)S(1)}, bf16[256,512]{1,0:T(8,128)(2,1)S(1)}, u32[]{:S(2)}, u32[]{:S(2)}) collective-permute-start(bf16[256,512]{1,0:T(8,128)(2,1)S(1)} %shard_map.85), channel_id=1, source_target_pairs={{0,4},{4,0},{8,12},{12,8},{1,5},{5,1},{9,13},{13,9},{2,6},{6,2},{1... | collective-permute-start | bytes 786440 | tf_op jit(solution)/shard_map/ppermute | solution.py:395
  184.5 10.7 %collective-permute-done.32.rest_2_ = bf16[256,512]{1,0:T(8,128)(2,1)S(1)} collective-permute-done((bf16[256,512]{1,0:T(8,128)(2,1)S(1)}, bf16[256,512]{1,0:T(8,128)(2,1)S(1)}, u32[]{:S(2)}, u32[]{:S(2)}) %collective-permute-start.32) | collective-permute-done | bytes 262176 | tf_op jit(solution)/shard_map/ppermute | solution.py:395
  199.5 10.2 %collective-permute-done.38.rest_2_ = bf16[256,512]{1,0:T(8,128)(2,1)S(1)} collective-permute-done((bf16[256,512]{1,0:T(8,128)(2,1)S(1)}, bf16[256,512]{1,0:T(8,128)(2,1)S(1)}, u32[]{:S(2)}, u32[]{:S(2)}) %collective-permute-start.38) | collective-permute-done | bytes 262176 | tf_op jit(solution)/shard_map/ppermute | solution.py:395
  214.5 4.1 %collective-permute-done.35 = bf16[4,16,1024]{2,1,0:T(8,128)(2,1)S(1)} collective-permute-done((bf16[4,16,1024]{2,1,0:T(8,128)(2,1)S(1)}, bf16[4,16,1024]{2,1,0:T(8,128)(2,1)S(1)}, u32[]{:S(2)}, u32[]{:S(2)}) %collective-permute-start.35) | collective-permute-done | bytes 131104 | tf_op jit(solution)/shard_map/ppermute | solution.py:392
  221.2 2.9 %collective-permute-start.42 = (bf16[2,16,1024]{2,1,0:T(8,128)(2,1)S(1)}, bf16[2,16,1024]{2,1,0:T(8,128)(2,1)S(1)}, u32[]{:S(2)}, u32[]{:S(2)}) collective-permute-start(bf16[2,16,1024]{2,1,0:T(8,128)(2,1)S(1)} %get-tuple-element.232), channel_id=1, source_target_pairs={{0,8},{4,12},{8,0},{12,4},{1,9},{5,13},{9,1},{13,5},{2,10},{6,14},... | collective-permute-start | bytes 196616 | tf_op jit(solution)/shard_map/ppermute | solution.py:395
  (122 shorter events, 72.3 us)
Async XLA Ops:
  3.7 7.5 %collective-permute-start.1 = (bf16[2,16,1024]{2,1,0:T(8,128)(2,1)}, bf16[2,16,1024]{2,1,0:T(8,128)(2,1)S(1)}, u32[]{:S(2)}, u32[]{:S(2)}) collective-permute-start(bf16[2,16,1024]{2,1,0:T(8,128)(2,1)} %param.7), channel_id=1, source_target_pairs={{0,8},{4,12},{8,0},{12,4},{1,9},{5,13},{9,1},{13,5},{2,10},{6,14},... | collective-permute-start | bytes 196616 | tf_op jit(solution)/shard_map/ppermute | solution.py:395
  27.0 17.0 %collective-permute-start.6 = (bf16[512,256]{1,0:T(8,128)(2,1)S(1)}, bf16[512,256]{1,0:T(8,128)(2,1)S(1)}, u32[]{:S(2)}, u32[]{:S(2)}) collective-permute-start(bf16[512,256]{1,0:T(8,128)(2,1)S(1)} %shard_map.60.refs_2_), channel_id=1, source_target_pairs={{0,8},{4,12},{8,0},{12,4},{1,9},{5,13},{9,1},{13,5},{2,10},{6,14},... | collective-permute-start | bytes 786440 | tf_op jit(solution)/shard_map/ppermute | solution.py:395
  29.2 19.3 %collective-permute-start.5 = (bf16[512,256]{1,0:T(8,128)(2,1)S(1)}, bf16[512,256]{1,0:T(8,128)(2,1)S(1)}, u32[]{:S(2)}, u32[]{:S(2)}) collective-permute-start(bf16[512,256]{1,0:T(8,128)(2,1)S(1)} %shard_map.60.refs_2_), channel_id=1, source_target_pairs={{0,4},{4,0},{8,12},{12,8},{1,5},{5,1},{9,13},{13,9},{2,6},{6,2},{1... | collective-permute-start | bytes 786440 | tf_op jit(solution)/shard_map/ppermute | solution.py:395
  29.4 22.4 %collective-permute-start.7 = (bf16[512,256]{1,0:T(8,128)(2,1)S(1)}, bf16[512,256]{1,0:T(8,128)(2,1)S(1)}, u32[]{:S(2)}, u32[]{:S(2)}) collective-permute-start(bf16[512,256]{1,0:T(8,128)(2,1)S(1)} %shard_map.60.refs_2_), channel_id=1, source_target_pairs={{4,8},{8,4},{5,9},{9,5},{6,10},{10,6},{7,11},{11,7},{20,24},{24,20... | collective-permute-start | bytes 786440 | tf_op jit(solution)/shard_map/ppermute | solution.py:440
  44.1 10.7 %collective-permute-start.8 = (bf16[512,256]{1,0:T(8,128)(2,1)S(1)}, bf16[512,256]{1,0:T(8,128)(2,1)S(1)}, u32[]{:S(2)}, u32[]{:S(2)}) collective-permute-start(bf16[512,256]{1,0:T(8,128)(2,1)S(1)} %collective-permute-done.6.refs_4_), channel_id=1, source_target_pairs={{4,0},{8,12},{5,1},{9,13},{6,2},{10,14},{7,3},{11,15},{20,16},{24,... | collective-permute-start | bytes 786440 | tf_op jit(solution)/shard_map/ppermute | solution.py:440
  58.2 8.8 %collective-permute-start.10 = (f32[512,256]{1,0:T(8,128)S(1)}, f32[512,256]{1,0:T(8,128)S(1)}, u32[]{:S(2)}, u32[]{:S(2)}) collective-permute-start(f32[512,256]{1,0:T(8,128)S(1)} %shard_map.67), channel_id=1, source_target_pairs={{0,1},{1,0},{2,3},{3,2},{4,5},{5,4},{6,7},{7,6},{8,9},{9,8},{10,11... | collective-permute-start | bytes 1572872 | tf_op jit(solution)/shard_map/ppermute | solution.py:388
  58.8 9.8 %collective-permute-start.11 = (bf16[512,256]{1,0:T(8,128)(2,1)S(1)}, bf16[512,256]{1,0:T(8,128)(2,1)S(1)}, u32[]{:S(2)}, u32[]{:S(2)}) collective-permute-start(bf16[512,256]{1,0:T(8,128)(2,1)S(1)} %shard_map.61.refs_2_), channel_id=1, source_target_pairs={{0,4},{4,0},{8,12},{12,8},{1,5},{5,1},{9,13},{13,9},{2,6},{6,2},{1... | collective-permute-start | bytes 786440 | tf_op jit(solution)/shard_map/ppermute | solution.py:395
  59.0 12.8 %collective-permute-start.13 = (bf16[512,256]{1,0:T(8,128)(2,1)S(1)}, bf16[512,256]{1,0:T(8,128)(2,1)S(1)}, u32[]{:S(2)}, u32[]{:S(2)}) collective-permute-start(bf16[512,256]{1,0:T(8,128)(2,1)S(1)} %get-tuple-element.234), channel_id=1, source_target_pairs={{0,0},{1,4},{2,8},{3,12},{4,1},{5,5},{6,9},{7,13},{8,2},{9,6},{10,... | collective-permute-start | bytes 786440 | tf_op jit(solution)/shard_map/ppermute | solution.py:399
  61.3 14.5 %collective-permute-start.12 = (bf16[512,256]{1,0:T(8,128)(2,1)S(1)}, bf16[512,256]{1,0:T(8,128)(2,1)S(1)}, u32[]{:S(2)}, u32[]{:S(2)}) collective-permute-start(bf16[512,256]{1,0:T(8,128)(2,1)S(1)} %shard_map.68), channel_id=1, source_target_pairs={{0,2},{1,3},{2,0},{3,1},{4,6},{5,7},{6,4},{7,5},{8,10},{9,11},{10,... | collective-permute-start | bytes 786440 | tf_op jit(solution)/shard_map/ppermute | solution.py:392
  67.0 21.6 %collective-permute-start.15 = (bf16[512,256]{1,0:T(8,128)(2,1)S(1)}, bf16[512,256]{1,0:T(8,128)(2,1)S(1)}, u32[]{:S(2)}, u32[]{:S(2)}) collective-permute-start(bf16[512,256]{1,0:T(8,128)(2,1)S(1)} %shard_map.61.refs_2_), channel_id=1, source_target_pairs={{0,8},{4,12},{8,0},{12,4},{1,9},{5,13},{9,1},{13,5},{2,10},{6,14},... | collective-permute-start | bytes 786440 | tf_op jit(solution)/shard_map/ppermute | solution.py:395
  77.0 16.7 %collective-permute-start.14 = (bf16[256,512]{1,0:T(8,128)(2,1)S(1)}, bf16[256,512]{1,0:T(8,128)(2,1)S(1)}, u32[]{:S(2)}, u32[]{:S(2)}) collective-permute-start(bf16[256,512]{1,0:T(8,128)(2,1)S(1)} %get-tuple-element.150.refs_2_), channel_id=1, source_target_pairs={{0,1},{1,0},{2,3},{3,2},{4,5},{5,4},{6,7},{7,6},{8,9},{9,8},{10,11... | collective-permute-start | bytes 786440 | tf_op jit(solution)/shard_map/ppermute | solution.py:388
  77.1 20.4 %collective-permute-start.16 = (bf16[512,256]{1,0:T(8,128)(2,1)S(1)}, bf16[512,256]{1,0:T(8,128)(2,1)S(1)}, u32[]{:S(2)}, u32[]{:S(2)}) collective-permute-start(bf16[512,256]{1,0:T(8,128)(2,1)S(1)} %shard_map.61.refs_2_), channel_id=1, source_target_pairs={{4,8},{8,4},{5,9},{9,5},{6,10},{10,6},{7,11},{11,7},{20,24},{24,20... | collective-permute-start | bytes 786440 | tf_op jit(solution)/shard_map/ppermute | solution.py:440
  88.6 9.9 %collective-permute-start.17 = (bf16[512,256]{1,0:T(8,128)(2,1)S(1)}, bf16[512,256]{1,0:T(8,128)(2,1)S(1)}, u32[]{:S(2)}, u32[]{:S(2)}) collective-permute-start(bf16[512,256]{1,0:T(8,128)(2,1)S(1)} %collective-permute-done.15.refs_4_), channel_id=1, source_target_pairs={{4,0},{8,12},{5,1},{9,13},{6,2},{10,14},{7,3},{11,15},{20,16},{24,... | collective-permute-start | bytes 786440 | tf_op jit(solution)/shard_map/ppermute | solution.py:440
  100.4 11.1 %collective-permute-start.18 = (f32[512,256]{1,0:T(8,128)S(1)}, f32[512,256]{1,0:T(8,128)S(1)}, u32[]{:S(2)}, u32[]{:S(2)}) collective-permute-start(f32[512,256]{1,0:T(8,128)S(1)} %get-tuple-element.162), channel_id=1, source_target_pairs={{0,1},{1,0},{2,3},{3,2},{4,5},{5,4},{6,7},{7,6},{8,9},{9,8},{10,11... | collective-permute-start | bytes 1572872 | tf_op jit(solution)/shard_map/ppermute | solution.py:388
  102.0 14.6 %collective-permute-start.19 = (f32[512,256]{1,0:T(8,128)S(1)}, f32[512,256]{1,0:T(8,128)S(1)}, u32[]{:S(2)}, u32[]{:S(2)}) collective-permute-start(f32[512,256]{1,0:T(8,128)S(1)} %shard_map.75), channel_id=1, source_target_pairs={{0,1},{1,0},{2,3},{3,2},{4,5},{5,4},{6,7},{7,6},{8,9},{9,8},{10,11... | collective-permute-start | bytes 1572872 | tf_op jit(solution)/shard_map/ppermute | solution.py:388
  102.5 8.3 %collective-permute-start.20 = (bf16[256,512]{1,0:T(8,128)(2,1)S(1)}, bf16[256,512]{1,0:T(8,128)(2,1)S(1)}, u32[]{:S(2)}, u32[]{:S(2)}) collective-permute-start(bf16[256,512]{1,0:T(8,128)(2,1)S(1)} %get-tuple-element.150.refs_2_), channel_id=1, source_target_pairs={{0,2},{1,3},{2,0},{3,1},{4,6},{5,7},{6,4},{7,5},{8,10},{9,11},{10,... | collective-permute-start | bytes 786440 | tf_op jit(solution)/shard_map/ppermute | solution.py:392
  110.8 11.5 %collective-permute-start.23 = (bf16[512,256]{1,0:T(8,128)(2,1)S(1)}, bf16[512,256]{1,0:T(8,128)(2,1)S(1)}, u32[]{:S(2)}, u32[]{:S(2)}) collective-permute-start(bf16[512,256]{1,0:T(8,128)(2,1)S(1)} %get-tuple-element.233), channel_id=1, source_target_pairs={{0,0},{1,4},{2,8},{3,12},{4,1},{5,5},{6,9},{7,13},{8,2},{9,6},{10,... | collective-permute-start | bytes 786440 | tf_op jit(solution)/shard_map/ppermute | solution.py:399
  113.1 14.4 %collective-permute-start.22 = (bf16[512,256]{1,0:T(8,128)(2,1)S(1)}, bf16[512,256]{1,0:T(8,128)(2,1)S(1)}, u32[]{:S(2)}, u32[]{:S(2)}) collective-permute-start(bf16[512,256]{1,0:T(8,128)(2,1)S(1)} %shard_map.76), channel_id=1, source_target_pairs={{0,2},{1,3},{2,0},{3,1},{4,6},{5,7},{6,4},{7,5},{8,10},{9,11},{10,... | collective-permute-start | bytes 786440 | tf_op jit(solution)/shard_map/ppermute | solution.py:392
  119.8 13.1 %collective-permute-start.24 = (bf16[256,512]{1,0:T(8,128)(2,1)S(1)}, bf16[256,512]{1,0:T(8,128)(2,1)S(1)}, u32[]{:S(2)}, u32[]{:S(2)}) collective-permute-start(bf16[256,512]{1,0:T(8,128)(2,1)S(1)} %get-tuple-element.177), channel_id=1, source_target_pairs={{0,4},{12,8},{1,5},{13,9},{2,6},{14,10},{3,7},{15,11},{16,20},{28,... | collective-permute-start | bytes 786440 | tf_op jit(solution)/shard_map/ppermute | solution.py:509
  128.7 7.9 %collective-permute-start.26 = (bf16[256,512]{1,0:T(8,128)(2,1)S(1)}, bf16[256,512]{1,0:T(8,128)(2,1)S(1)}, u32[]{:S(2)}, u32[]{:S(2)}) collective-permute-start(bf16[256,512]{1,0:T(8,128)(2,1)S(1)} %get-tuple-element.179.refs_2_), channel_id=1, source_target_pairs={{0,2},{1,3},{2,0},{3,1},{4,6},{5,7},{6,4},{7,5},{8,10},{9,11},{10,... | collective-permute-start | bytes 786440 | tf_op jit(solution)/shard_map/ppermute | solution.py:392
  131.2 9.0 %collective-permute-start.25 = (bf16[256,512]{1,0:T(8,128)(2,1)S(1)}, bf16[256,512]{1,0:T(8,128)(2,1)S(1)}, u32[]{:S(2)}, u32[]{:S(2)}) collective-permute-start(bf16[256,512]{1,0:T(8,128)(2,1)S(1)} %get-tuple-element.179.refs_2_), channel_id=1, source_target_pairs={{0,1},{1,0},{2,3},{3,2},{4,5},{5,4},{6,7},{7,6},{8,9},{9,8},{10,11... | collective-permute-start | bytes 786440 | tf_op jit(solution)/shard_map/ppermute | solution.py:388
  145.6 13.0 %collective-permute-start.28 = (bf16[256,512]{1,0:T(8,128)(2,1)S(1)}, bf16[256,512]{1,0:T(8,128)(2,1)S(1)}, u32[]{:S(2)}, u32[]{:S(2)}) collective-permute-start(bf16[256,512]{1,0:T(8,128)(2,1)S(1)} %get-tuple-element.189), channel_id=1, source_target_pairs={{0,4},{12,8},{1,5},{13,9},{2,6},{14,10},{3,7},{15,11},{16,20},{28,... | collective-permute-start | bytes 786440 | tf_op jit(solution)/shard_map/ppermute | solution.py:509
  148.4 15.9 %collective-permute-start.29 = (bf16[512,256]{1,0:T(8,128)(2,1)S(1)}, bf16[512,256]{1,0:T(8,128)(2,1)S(1)}, u32[]{:S(2)}, u32[]{:S(2)}) collective-permute-start(bf16[512,256]{1,0:T(8,128)(2,1)S(1)} %get-tuple-element.193), channel_id=1, source_target_pairs={{0,0},{1,4},{2,8},{3,12},{4,1},{5,5},{6,9},{7,13},{8,2},{9,6},{10,... | collective-permute-start | bytes 786440 | tf_op jit(solution)/shard_map/ppermute | solution.py:399
  149.0 17.6 %collective-permute-start.30 = (bf16[256,512]{1,0:T(8,128)(2,1)S(1)}, bf16[256,512]{1,0:T(8,128)(2,1)S(1)}, u32[]{:S(2)}, u32[]{:S(2)}) collective-permute-start(bf16[256,512]{1,0:T(8,128)(2,1)S(1)} %get-tuple-element.177), channel_id=1, source_target_pairs={{4,8},{8,4},{5,9},{9,5},{6,10},{10,6},{7,11},{11,7},{20,24},{24,20... | collective-permute-start | bytes 786440 | tf_op jit(solution)/shard_map/ppermute | solution.py:510
  149.7 45.5 %collective-permute-start.32 = (bf16[256,512]{1,0:T(8,128)(2,1)S(1)}, bf16[256,512]{1,0:T(8,128)(2,1)S(1)}, u32[]{:S(2)}, u32[]{:S(2)}) collective-permute-start(bf16[256,512]{1,0:T(8,128)(2,1)S(1)} %shard_map.81), channel_id=1, source_target_pairs={{0,8},{4,12},{8,0},{12,4},{1,9},{5,13},{9,1},{13,5},{2,10},{6,14},... | collective-permute-start | bytes 786440 | tf_op jit(solution)/shard_map/ppermute | solution.py:395
  156.4 38.8 %collective-permute-start.31 = (bf16[256,512]{1,0:T(8,128)(2,1)S(1)}, bf16[256,512]{1,0:T(8,128)(2,1)S(1)}, u32[]{:S(2)}, u32[]{:S(2)}) collective-permute-start(bf16[256,512]{1,0:T(8,128)(2,1)S(1)} %shard_map.80), channel_id=1, source_target_pairs={{0,4},{4,0},{8,12},{12,8},{1,5},{5,1},{9,13},{13,9},{2,6},{6,2},{1... | collective-permute-start | bytes 786440 | tf_op jit(solution)/shard_map/ppermute | solution.py:395
  158.6 39.1 %collective-permute-start.33 = (bf16[512,256]{1,0:T(8,128)(2,1)S(1)}, bf16[512,256]{1,0:T(8,128)(2,1)S(1)}, u32[]{:S(2)}, u32[]{:S(2)}) collective-permute-start(bf16[512,256]{1,0:T(8,128)(2,1)S(1)} %get-tuple-element.202), channel_id=1, source_target_pairs={{0,0},{1,4},{2,8},{3,12},{4,1},{5,5},{6,9},{7,13},{8,2},{9,6},{10,... | collective-permute-start | bytes 786440 | tf_op jit(solution)/shard_map/ppermute | solution.py:399
  164.2 35.3 %collective-permute-start.36 = (bf16[256,512]{1,0:T(8,128)(2,1)S(1)}, bf16[256,512]{1,0:T(8,128)(2,1)S(1)}, u32[]{:S(2)}, u32[]{:S(2)}) collective-permute-start(bf16[256,512]{1,0:T(8,128)(2,1)S(1)} %get-tuple-element.189), channel_id=1, source_target_pairs={{4,8},{8,4},{5,9},{9,5},{6,10},{10,6},{7,11},{11,7},{20,24},{24,20... | collective-permute-start | bytes 786440 | tf_op jit(solution)/shard_map/ppermute | solution.py:510
  166.7 32.8 %collective-permute-start.37 = (bf16[256,512]{1,0:T(8,128)(2,1)S(1)}, bf16[256,512]{1,0:T(8,128)(2,1)S(1)}, u32[]{:S(2)}, u32[]{:S(2)}) collective-permute-start(bf16[256,512]{1,0:T(8,128)(2,1)S(1)} %shard_map.85), channel_id=1, source_target_pairs={{0,4},{4,0},{8,12},{12,8},{1,5},{5,1},{9,13},{13,9},{2,6},{6,2},{1... | collective-permute-start | bytes 786440 | tf_op jit(solution)/shard_map/ppermute | solution.py:395
  197.4 12.3 %collective-permute-start.38 = (bf16[256,512]{1,0:T(8,128)(2,1)S(1)}, bf16[256,512]{1,0:T(8,128)(2,1)S(1)}, u32[]{:S(2)}, u32[]{:S(2)}) collective-permute-start(bf16[256,512]{1,0:T(8,128)(2,1)S(1)} %shard_map.86), channel_id=1, source_target_pairs={{0,8},{4,12},{8,0},{12,4},{1,9},{5,13},{9,1},{13,5},{2,10},{6,14},... | collective-permute-start | bytes 786440 | tf_op jit(solution)/shard_map/ppermute | solution.py:395
  197.6 14.5 %collective-permute-start.34 = (f32[4,2,16,1024]{3,2,0,1:T(8,128)S(1)}, f32[4,2,16,1024]{3,2,0,1:T(8,128)S(1)}, u32[]{:S(2)}, u32[]{:S(2)}) collective-permute-start(f32[4,2,16,1024]{3,2,0,1:T(8,128)S(1)} %bitcast.71), channel_id=1, source_target_pairs={{0,1},{1,0},{2,3},{3,2},{4,5},{5,4},{6,7},{7,6},{8,9},{9,8},{10,11... | collective-permute-start | bytes 1572872 | tf_op jit(solution)/shard_map/ppermute | solution.py:388
  221.2 7.6 %collective-permute-start.42 = (bf16[2,16,1024]{2,1,0:T(8,128)(2,1)S(1)}, bf16[2,16,1024]{2,1,0:T(8,128)(2,1)S(1)}, u32[]{:S(2)}, u32[]{:S(2)}) collective-permute-start(bf16[2,16,1024]{2,1,0:T(8,128)(2,1)S(1)} %get-tuple-element.232), channel_id=1, source_target_pairs={{0,8},{4,12},{8,0},{12,4},{1,9},{5,13},{9,1},{13,5},{2,10},{6,14},... | collective-permute-start | bytes 196616 | tf_op jit(solution)/shard_map/ppermute | solution.py:395
  (17 other events, 97.9 us)
